TPU v7x, 128 devices: a whole 4x4x4 slice. The times are simulated.
128 devices in a mesh: leaf: 8 (over y, core), tile: 16 (over z, x).
Axes of the slice: x: 4, y: 4, z: 4, core: 2. Of those that a mesh axis runs over, the one named last changes fastest.
Arguments:
- right_sides: float32 [4, 4096, 128], P(None, ('leaf', 'tile')), may hold values from -6 to 6
- diag_inverse: bfloat16 [4096, 7680], P(('leaf', 'tile')), may hold values from -2.8 to 2.8, as said below
- coupling: bfloat16 [4096, 1088], P(('leaf', 'tile')), may hold values from -0.375 to 0.375
- pattern: int32 [128, 34], P(('leaf', 'tile')), may hold values 0 or 1
Outputs:
- solution: float32 [4, 4096, 128], P(None, ('leaf', 'tile'))
Inputs may be any that keep to these rules, and one draw needn't show every extreme that they name: Within each supernode the block of diag_inverse is the inverse of a lower triangular diagonal block of the factor: zero above its diagonal and between 0.6 and 1.4 on it.
All inputs are finite; a program needn't handle non-finite values. No bound on the sum of `pattern` on one device may be relied on, other than what follows from the above.
Results may differ from a plain program's by a relative error of at most 0.018.
Values may be sent and summed in bfloat16 or wider, within the bound.
No kernel may reach another device: no remote copies, remote signals or barrier semaphores. Data moves between devices by JAX's collectives and lax.ppermute only.
A program may use at most 64 MiB of HBM per device.

v0:
```python
import jax
import jax.numpy as jnp
from jax import lax
from jax.sharding import PartitionSpec as P


def pair_offsets(levels):
    offset_map = {}
    cursor = 0
    for top_level in range(1, levels):
        for low_level in range(top_level):
            offset_map[top_level, low_level] = cursor
            cursor += 2**top_level
    return offset_map


def section_rows(values, group_span, group_start):
    if group_span == 1:
        return values[None]
    everything = lax.all_gather(values[None], "leaf", axis=0, tiled=True)
    return lax.dynamic_slice_in_dim(everything, group_start, group_span, 0)


def group_sum(inverse_part, remainder, group_span, group_start, leaves):
    shares = lax.psum_scatter(
        jnp.einsum(
            "rkc,rn->ckn", inverse_part, remainder, preferred_element_type=jnp.float32
        ).astype(jnp.bfloat16),
        "tile",
        scatter_dimension=0,
        tiled=True,
    ).astype(jnp.float32)
    if group_span == 1:
        return shares[:, 0]
    padded = jnp.zeros((shares.shape[0], leaves, shares.shape[2]), jnp.float32)
    padded = lax.dynamic_update_slice_in_dim(padded, shares, group_start, 1)
    return lax.psum_scatter(
        padded.astype(jnp.bfloat16), "leaf", scatter_dimension=1, tiled=True
    ).astype(jnp.float32)[:, 0]


def local(right_sides, diag_inverse, coupling, pattern):
    levels = right_sides.shape[0]
    local_rows = right_sides.shape[1]
    columns = right_sides.shape[2]
    leaves = lax.axis_size("leaf")
    leaf_index = lax.axis_index("leaf")
    panel_width = lax.axis_size("tile") * local_rows
    block_count = pattern.shape[1]
    offset_map = pair_offsets(levels)
    masked = coupling.reshape(local_rows, block_count, local_rows) * pattern.reshape(
        1, block_count, 1
    ).astype(coupling.dtype)
    masked = masked.reshape(local_rows, block_count * local_rows)

    def coupling_part(height, low_level):
        group_span = 2**height
        first_col = offset_map[height, low_level] * local_rows
        return masked[:, first_col : first_col + group_span * local_rows].reshape(
            local_rows, group_span, local_rows
        )

    def inverse_columns(height):
        group_span = 2**height
        picked = diag_inverse[
            :, (group_span - 1) * panel_width : (2 * group_span - 1) * panel_width
        ]
        return picked.reshape(local_rows, group_span, panel_width)

    gathered = []
    solved = []
    for height in range(levels):
        group_span = 2**height
        group_start = leaf_index // group_span * group_span
        reduced = right_sides[height]
        for low_level in range(height):
            source = lax.dynamic_slice_in_dim(gathered[low_level], group_start, group_span, 0)
            reduced = reduced - jnp.einsum(
                "rkb,kbn->rn",
                coupling_part(height, low_level),
                source,
                preferred_element_type=jnp.float32,
            )
        group_rows = section_rows(reduced.astype(jnp.bfloat16), group_span, group_start)
        inverse_part = inverse_columns(height)

        def accumulate(running, shard_rows, first_row, inverse_part=inverse_part):
            return jnp.einsum(
                "rkc,kcn->rn", inverse_part, shard_rows, preferred_element_type=jnp.float32
            )

        solution = accumulate(
            jnp.zeros((local_rows, columns), jnp.float32),
            lax.all_gather(group_rows, "tile", axis=1, tiled=True),
            jnp.int32(0),
        )
        solved_half = solution.astype(jnp.bfloat16)
        solved.append(solved_half)
        if height + 1 < levels:
            collected = lax.all_gather(solved_half, "leaf", axis=0, tiled=True)
            gathered.append(collected.reshape(leaves, local_rows, columns))
    pending = [jnp.zeros((local_rows, columns), jnp.float32) for height in range(levels)]
    answers = [None] * levels
    for height in reversed(range(levels)):
        group_span = 2**height
        group_start = leaf_index // group_span * group_span
        remainder = (solved[height].astype(jnp.float32) - pending[height]).astype(jnp.bfloat16)
        answers[height] = group_sum(
            inverse_columns(height), remainder, group_span, group_start, leaves
        )
        if height > 0:
            answer_half = answers[height].astype(jnp.bfloat16)
            stacked = jnp.stack(
                [coupling_part(height, low_level) for low_level in range(height)], 0
            )
            updates = jnp.einsum(
                "lrkb,rn->klbn", stacked, answer_half, preferred_element_type=jnp.float32
            )
            padded = jnp.zeros((leaves,) + updates.shape[1:], jnp.float32)
            padded = lax.dynamic_update_slice_in_dim(padded, updates, group_start, 0)
            received = lax.psum_scatter(
                padded.astype(jnp.bfloat16), "leaf", scatter_dimension=0, tiled=True
            ).astype(jnp.float32)[0]
            for low_level in range(height):
                pending[low_level] = pending[low_level] + received[low_level]
    return jnp.stack(answers, 0)


def solution(mesh):
    placed = (
        P(None, ("leaf", "tile"), None),
        P(("leaf", "tile"), None),
        P(("leaf", "tile"), None),
        P(("leaf", "tile"), None),
    )
    return jax.shard_map(
        local,
        mesh=mesh,
        in_specs=placed,
        out_specs=P(None, ("leaf", "tile"), None),
        check_vma=False,
    )
```

profile of v0, /device:TPU:0, one launch (start us, length us, event | category | flops | bytes accessed | tf_op | source)
XLA Modules:
  0.0 743.7 jit_solution(17393212681733842846)
XLA Ops:
  6.5 0.7 convert_bitcast_fusion
  7.4 0.9 broadcast_multiply_fusion
  8.4 0.8 slice.80
  9.2 0.9 slice.85
  10.2 0.7 slice.146
  11.0 25.2 %all_gather.30 = bf16[1,512,128]{2,1,0:T(8,128)(2,1)S(1)} all-gather(bf16[1,32,128]{2,1,0:T(8,128)(2,1)S(1)} %slice.146), channel_id=1, replica_groups=mesh['leaf'=8,'tile'=16] {'tile'}, dimensions={1}, use_global_device_ids=true | all-gather | bytes 139264 | tf_op jit(solution)/shard_map/all_gather | solution.py:94
  36.1 0.9 convolution_convert_fusion.4
  37.0 13.3 %all_gather.31 = bf16[256,128]{1,0:T(8,128)(2,1)S(1)} all-gather(bf16[32,128]{1,0:T(8,128)(2,1)S(1)} %convolution_convert_fusion.4), channel_id=1, replica_groups=mesh['leaf'=8,'tile'=16] {'leaf'}, dimensions={0}, use_global_device_ids=true | all-gather | bytes 73728 | tf_op jit(solution)/shard_map/all_gather | solution.py:100
  50.6 12.8 %all-gather = bf16[256,128]{1,0:T(8,128)(2,1)S(1)} all-gather(bf16[32,128]{1,0:T(8,128)(2,1)S(1)} %fusion.12), channel_id=2, replica_groups=mesh['leaf'=8,'tile'=16] {'leaf'}, dimensions={0}, use_global_device_ids=true | all-gather | bytes 73728 | tf_op jit(solution)/shard_map/all_gather | solution.py:20
  63.3 23.1 %all_gather.33 = bf16[2,512,128]{2,1,0:T(8,128)(2,1)S(1)} all-gather(bf16[2,32,128]{2,1,0:T(8,128)(2,1)S(1)} %constant_dynamic-slice_fusion.1), channel_id=1, replica_groups=mesh['leaf'=8,'tile'=16] {'tile'}, dimensions={1}, use_global_device_ids=true | all-gather | bytes 278528 | tf_op jit(solution)/shard_map/all_gather | solution.py:94
  86.6 12.8 %all_gather.34 = bf16[256,128]{1,0:T(8,128)(2,1)S(1)} all-gather(bf16[32,128]{1,0:T(8,128)(2,1)S(1)} %fusion.19), channel_id=1, replica_groups=mesh['leaf'=8,'tile'=16] {'leaf'}, dimensions={0}, use_global_device_ids=true | all-gather | bytes 73728 | tf_op jit(solution)/shard_map/all_gather | solution.py:100
  99.9 12.8 %all-gather.1 = bf16[256,128]{1,0:T(8,128)(2,1)S(1)} all-gather(bf16[32,128]{1,0:T(8,128)(2,1)S(1)} %fusion.11), channel_id=3, replica_groups=mesh['leaf'=8,'tile'=16] {'leaf'}, dimensions={0}, use_global_device_ids=true | all-gather | bytes 73728 | tf_op jit(solution)/shard_map/all_gather | solution.py:20
  112.7 22.0 %all_gather.36 = bf16[4,512,128]{2,1,0:T(8,128)(2,1)S(1)} all-gather(bf16[4,32,128]{2,1,0:T(8,128)(2,1)S(1)} %constant_dynamic-slice_fusion), channel_id=1, replica_groups=mesh['leaf'=8,'tile'=16] {'tile'}, dimensions={1}, use_global_device_ids=true | all-gather | bytes 557056 | tf_op jit(solution)/shard_map/all_gather | solution.py:94
  134.9 12.8 %all_gather.37 = bf16[256,128]{1,0:T(8,128)(2,1)S(1)} all-gather(bf16[32,128]{1,0:T(8,128)(2,1)S(1)} %fusion.18), channel_id=1, replica_groups=mesh['leaf'=8,'tile'=16] {'leaf'}, dimensions={0}, use_global_device_ids=true | all-gather | bytes 73728 | tf_op jit(solution)/shard_map/all_gather | solution.py:100
  148.5 13.8 %all-gather.2 = bf16[256,128]{1,0:T(8,128)(2,1)} all-gather(bf16[32,128]{1,0:T(8,128)(2,1)S(1)} %fusion.13), channel_id=4, replica_groups=mesh['leaf'=8,'tile'=16] {'leaf'}, dimensions={0}, use_global_device_ids=true | all-gather | bytes 73728 | tf_op jit(solution)/shard_map/all_gather | solution.py:20
  162.5 41.9 %all-gather.5.cloned.1.call-done = bf16[8,512,128]{2,1,0:T(8,128)(2,1)} async-done(((bf16[8,32,128]{2,1,0:T(8,128)(2,1)}), bf16[8,512,128]{2,1,0:T(8,128)(2,1)}) %all-gather.5.cloned.1.call-update) | async-done | bytes 1048592 | tf_op jit(solution)/shard_map/all_gather | solution.py:94
  204.4 2.0 fusion
  206.4 1.5 copy.101
  207.9 73.6 %reduce-scatter.8.cloned.1.call-done = bf16[32,8,128]{2,1,0:T(8,128)(2,1)} async-done(((bf16[512,8,128]{2,1,0:T(8,128)(2,1)}), bf16[32,8,128]{2,1,0:T(8,128)(2,1)}) %reduce-scatter.8.cloned.1.call-update) | async-done | bytes 65552 | tf_op jit(solution)/shard_map/reduce_scatter | solution.py:25
  281.5 1.5 copy.102
  283.5 30.4 %reduce-scatter.10.cloned.1.call-done = bf16[32,1,128]{2,0,1:T(8,128)(2,1)} async-done(((bf16[32,8,128]{2,0,1:T(8,128)(2,1)}), bf16[32,1,128]{2,0,1:T(8,128)(2,1)}) %reduce-scatter.10.cloned.1.call-update) | async-done | bytes 8208 | tf_op jit(solution)/shard_map/reduce_scatter | solution.py:37
  313.8 0.9 fusion.64
  314.7 0.7 copy.161
  315.5 30.2 %reduce-scatter.12.cloned.1.call-done = bf16[1,3,32,128]{3,2,1,0:T(8,128)(2,1)} async-done(((bf16[8,3,32,128]{3,2,1,0:T(8,128)(2,1)}), bf16[1,3,32,128]{3,2,1,0:T(8,128)(2,1)}) %reduce-scatter.12.cloned.1.call-update) | async-done | bytes 24592 | tf_op jit(solution)/shard_map/reduce_scatter | solution.py:121
  345.6 0.7 convert_element_type.156
  346.7 1.1 copy.108
  347.9 0.6 dynamic-slice
  349.1 84.3 %all-reduce.7.cloned.1.call-done = bf16[512,4,128]{2,1,0:T(4,128)(2,1)} async-done(((bf16[512,4,128]{2,1,0:T(4,128)(2,1)}), bf16[512,4,128]{2,1,0:T(4,128)(2,1)}) %all-reduce.7.cloned.1.call-update) | async-done | bytes 524304
  433.4 0.8 constant_dynamic-slice_fusion.4
  434.2 0.6 copy-done.3
  435.1 30.5 %reduce-scatter.14.cloned.1.call-done = bf16[32,1,128]{2,0,1:T(8,128)(2,1)} async-done(((bf16[32,8,128]{2,0,1:T(8,128)(2,1)}), bf16[32,1,128]{2,0,1:T(8,128)(2,1)}) %reduce-scatter.14.cloned.1.call-update) | async-done | bytes 8208 | tf_op jit(solution)/shard_map/reduce_scatter | solution.py:37
  465.6 0.9 fusion.4
  466.5 0.6 copy-done.1
  467.3 30.3 %reduce-scatter.16.cloned.1.call-done = bf16[1,2,32,128]{3,2,1,0:T(8,128)(2,1)} async-done(((bf16[8,2,32,128]{3,2,1,0:T(8,128)(2,1)}), bf16[1,2,32,128]{3,2,1,0:T(8,128)(2,1)}) %reduce-scatter.16.cloned.1.call-update) | async-done | bytes 16400 | tf_op jit(solution)/shard_map/reduce_scatter | solution.py:121
  497.5 0.7 convert_element_type.165
  498.5 0.9 copy.113
  499.5 85.2 %all-reduce.9.cloned.1.call-done = bf16[512,2,128]{2,1,0:T(2,128)(2,1)} async-done(((bf16[512,2,128]{2,1,0:T(2,128)(2,1)}), bf16[512,2,128]{2,1,0:T(2,128)(2,1)}) %all-reduce.9.cloned.1.call-update) | async-done | bytes 262160
  584.7 0.7 constant_dynamic-slice_fusion.3
  585.5 0.6 copy-done.4
  586.2 30.9 %reduce-scatter.18.cloned.1.call-done = bf16[32,1,128]{2,0,1:T(8,128)(2,1)} async-done(((bf16[32,8,128]{2,0,1:T(8,128)(2,1)}), bf16[32,1,128]{2,0,1:T(8,128)(2,1)}) %reduce-scatter.18.cloned.1.call-update) | async-done | bytes 8208 | tf_op jit(solution)/shard_map/reduce_scatter | solution.py:37
  617.0 0.9 fusion.62
  618.0 0.6 copy-done.2
  618.7 30.1 %reduce-scatter.20.cloned.1.call-done = bf16[1,1,32,128]{3,2,1,0:T(8,128)(2,1)} async-done(((bf16[8,1,32,128]{3,2,1,0:T(8,128)(2,1)}), bf16[1,1,32,128]{3,2,1,0:T(8,128)(2,1)}) %reduce-scatter.20.cloned.1.call-update) | async-done | bytes 8208 | tf_op jit(solution)/shard_map/reduce_scatter | solution.py:121
  648.8 0.9 fusion.3
  649.7 0.9 copy.116
  650.6 85.2 %all-reduce.11.cloned.1.call-done = bf16[512,1,128]{2,1,0:T(2,128)(2,1)} async-done(((bf16[512,1,128]{2,1,0:T(2,128)(2,1)}), bf16[512,1,128]{2,1,0:T(2,128)(2,1)}) %all-reduce.11.cloned.1.call-update) | async-done | bytes 131088
  735.8 0.7 constant_dynamic-slice_fusion.2
  736.5 0.6 maximum_convert_fusion
  (77 shorter events, 4.3 us)
Async XLA Ops:
  6.5 43.8 %copy-start.5 = (f32[4,32,128]{2,1,0:T(8,128)S(1)}, f32[4,32,128]{2,1,0:T(8,128)}, u32[]{:S(2)}) copy-start(f32[4,32,128]{2,1,0:T(8,128)} %param.4) | copy-start | bytes 196612
  6.5 197.9 %all-gather.5.cloned.1.call-start = ((), (), s32[]{:S(2)}) async-start(), calls=%async_computation.7 | async-start | bytes 1114112 | tf_op jit(solution)/shard_map/all_gather | solution.py:94
  134.7 69.7 %slice-start = ((bf16[32,7680]{1,0:T(8,128)(2,1)}), bf16[32,4096]{1,0:T(8,128)(2,1)S(1)}, s32[]{:S(2)}) async-start(bf16[32,7680]{1,0:T(8,128)(2,1)} %param.5), calls=%async_computation.18 | async-start | bytes 524288 | tf_op jit(solution)/shard_map/slice | solution.py:65
  162.4 119.1 %reduce-scatter.8.cloned.1.call-start = ((), (), s32[]{:S(2)}) async-start(), calls=%async_computation.8 | async-start | bytes 1114112 | tf_op jit(solution)/shard_map/reduce_scatter | solution.py:25
  207.9 106.0 %reduce-scatter.10.cloned.1.call-start = ((), (), s32[]{:S(2)}) async-start(), calls=%async_computation.9 | async-start | bytes 73728 | tf_op jit(solution)/shard_map/reduce_scatter | solution.py:37
  283.0 62.7 %reduce-scatter.12.cloned.1.call-start = ((), (), s32[]{:S(2)}) async-start(), calls=%async_computation.10 | async-start | bytes 221184 | tf_op jit(solution)/shard_map/reduce_scatter | solution.py:121
  315.4 117.9 %all-reduce.7.cloned.1.call-start = ((), (), s32[]{:S(2)}) async-start(), calls=%async_computation.15 | async-start | bytes 1048576
  346.4 1.5 copy-start.9
  347.8 117.8 %reduce-scatter.14.cloned.1.call-start = ((), (), s32[]{:S(2)}) async-start(), calls=%async_computation.11 | async-start | bytes 73728 | tf_op jit(solution)/shard_map/reduce_scatter | solution.py:37
  434.2 0.6 copy-start.3
  434.8 62.7 %reduce-scatter.16.cloned.1.call-start = ((), (), s32[]{:S(2)}) async-start(), calls=%async_computation.12 | async-start | bytes 147456 | tf_op jit(solution)/shard_map/reduce_scatter | solution.py:121
  465.6 183.2 %copy-start = (bf16[32,7680]{1,0:T(8,128)(2,1)S(1)}, bf16[32,7680]{1,0:T(8,128)(2,1)}, u32[]{:S(2)}) copy-start(bf16[32,7680]{1,0:T(8,128)(2,1)} %param.5) | copy-start | bytes 1474564
  466.5 0.7 copy-start.1
  467.2 117.5 %all-reduce.9.cloned.1.call-start = ((), (), s32[]{:S(2)}) async-start(), calls=%async_computation.16 | async-start | bytes 524288
  498.5 238.0 %copy-start.6 = (bf16[32,1,128]{2,0,1:T(8,128)(2,1)S(1)}, bf16[32,1,128]{2,0,1:T(8,128)(2,1)}, u32[]{:S(2)}) copy-start(bf16[32,1,128]{2,0,1:T(8,128)(2,1)} %reduce-scatter.10.cloned.1.call-done) | copy-start | bytes 24580
  498.5 238.0 %copy-start.7 = (bf16[32,1,128]{2,0,1:T(8,128)(2,1)S(1)}, bf16[32,1,128]{2,0,1:T(8,128)(2,1)}, u32[]{:S(2)}) copy-start(bf16[32,1,128]{2,0,1:T(8,128)(2,1)} %reduce-scatter.14.cloned.1.call-done) | copy-start | bytes 24580
  499.4 117.6 %reduce-scatter.18.cloned.1.call-start = ((), (), s32[]{:S(2)}) async-start(), calls=%async_computation.13 | async-start | bytes 73728 | tf_op jit(solution)/shard_map/reduce_scatter | solution.py:37
  585.5 0.6 copy-start.4
  586.1 62.7 %reduce-scatter.20.cloned.1.call-start = ((), (), s32[]{:S(2)}) async-start(), calls=%async_computation.14 | async-start | bytes 73728 | tf_op jit(solution)/shard_map/reduce_scatter | solution.py:121
  617.0 119.5 %copy-start.8 = (bf16[32,1,128]{2,0,1:T(8,128)(2,1)S(1)}, bf16[32,1,128]{2,0,1:T(8,128)(2,1)}, u32[]{:S(2)}) copy-start(bf16[32,1,128]{2,0,1:T(8,128)(2,1)} %reduce-scatter.18.cloned.1.call-done) | copy-start | bytes 24580
  618.0 0.6 copy-start.2
  618.6 117.2 %all-reduce.11.cloned.1.call-start = ((), (), s32[]{:S(2)}) async-start(), calls=%async_computation.17 | async-start | bytes 524288
Sparse Core Ops, SparseCore 0:
  162.5 41.8 all-gather.4
  208.0 73.4 reduce-scatter.7
  283.8 29.9 reduce-scatter.9
  316.0 29.5 reduce-scatter.11
  348.7 84.6 all-reduce.6
  435.6 29.9 reduce-scatter.13
  467.9 29.5 reduce-scatter.15
  500.7 83.9 all-reduce.8
  587.0 29.9 reduce-scatter.17
  619.2 29.5 reduce-scatter.19
  652.0 83.7 all-reduce.10
where the time goes:
time: 745 us; the launch traced here: 744 us
  waiting for transfers between devices  553 us (74%)
  blocking collectives  148 us (20%)
  local copies, waits for them, and re-layouts  15.9 us (2%)
  between operations  14.2 us (2%)
  matrix products  8.43 us (1%)
    unnamed x14, waiting for transfers between devices  255 us
    reduce_scatter x3, waiting for transfers between devices, group_sum(): lax.psum_scatter(padded.astype(jnp.bfloat16), 'leaf', scatter_dimension=1...  91.7 us
    reduce_scatter x3, waiting for transfers between devices, local(): lax.psum_scatter(padded.astype(jnp.bfloat16), 'leaf', scatter_dimension=0...  90.6 us
    reduce_scatter x1, waiting for transfers between devices, group_sum(): lax.psum_scatter(jnp.einsum('rkc,rn->ckn', inverse_part, remainder, prefe...  73.6 us
    all_gather x3, blocking collectives, local(): lax.all_gather(group_rows, 'tile', axis=1, tiled=True)  70.3 us
    all_gather x1, waiting for transfers between devices, local(): lax.all_gather(group_rows, 'tile', axis=1, tiled=True)  41.9 us
    all_gather x3, blocking collectives, section_rows(): everything = lax.all_gather(values[None], 'leaf', axis=0, tiled=True)  39.3 us
    all_gather x3, blocking collectives, local(): collected = lax.all_gather(solved_half, 'leaf', axis=0, tiled=True)  38.8 us
  transfers between devices with their start and end apart: 11, of which 11 were waited for; matrix products, arithmetic and copies ran while one was open for 0% of the time, Pallas kernels for 0%

commit v1 on v0

v1 whole, which is shorter than its diff:
```python
import functools

import jax
import jax.numpy as jnp
from jax import lax
from jax.experimental import pallas as pl
from jax.experimental.pallas import tpu as pltpu
from jax.sharding import PartitionSpec as P

BF = jnp.bfloat16
F32 = jnp.float32
PAIRS = ((1, 0), (2, 0), (2, 1), (3, 0), (3, 1), (3, 2))
OFFSET = {(1, 0): 0, (2, 0): 2, (2, 1): 6, (3, 0): 10, (3, 1): 18, (3, 2): 26}
BLOCKS = 34
VMEM = pl.BlockSpec(memory_space=pltpu.VMEM)
SMEM = pl.BlockSpec(memory_space=pltpu.SMEM)
RHS_ROWS, C_TILES, D0_TILES, D1_TILES = 16, 9, 4, 8
C_AT = RHS_ROWS
D0_AT = C_AT + 32 * C_TILES
D1_AT = D0_AT + 32 * D0_TILES
MESSAGE = D1_AT + 32 * D1_TILES


def params(mib=48):
    return pltpu.CompilerParams(vmem_limit_bytes=mib * 2**20)


def lane_chunk(rows):
    return lax.broadcasted_iota(jnp.int32, (rows, 128), 1) // 32


def dot_nt(a, b):
    return lax.dot_general(a, b, (((1,), (1,)), ((), ())), preferred_element_type=F32)


def dot_nn(a, b):
    return jnp.dot(a, b, preferred_element_type=F32)


class Rolled:
    def __init__(self, tiles):
        self.tiles = tiles
        self.made = {}

    def take(self, tile, source, target):
        shift = (target - source) % 4 * 32
        if shift == 0:
            return self.tiles[tile]
        if (tile, shift) not in self.made:
            self.made[tile, shift] = pltpu.roll(self.tiles[tile], shift, 1)
        return self.made[tile, shift]


def merge(parts, chunk):
    result = parts[0]
    for c in range(1, len(parts)):
        result = jnp.where(chunk == c, parts[c], result)
    return result


def split_kernel(coupling_ref, pattern_ref, out_ref):
    chunk = lane_chunk(32)
    tiles = []
    for tile in range(C_TILES):
        if tile < 8:
            values = coupling_ref[:, 128 * tile : 128 * tile + 128].astype(F32)
        else:
            half = coupling_ref[:, 1024:1088].astype(F32)
            values = jnp.concatenate([half, jnp.zeros_like(half)], 1)
        keep = jnp.zeros((32, 128), F32)
        for c in range(4):
            if 4 * tile + c < BLOCKS:
                keep = jnp.where(chunk == c, pattern_ref[0, 4 * tile + c].astype(F32), keep)
        tiles.append(values * keep)
    rolled = Rolled(tiles)
    for leaf in range(8):
        parts = []
        for q, (w, u) in enumerate(PAIRS):
            block = OFFSET[w, u] + leaf % 2**w
            parts.append(rolled.take(block // 4, block % 4, q % 4))
        out_ref[leaf, :, 0:128] = merge(parts[:4], chunk).astype(BF)
        out_ref[leaf, :, 128:256] = merge(parts[4:], chunk).astype(BF)


def message_kernel(leaf_ref, columns_ref, rhs_ref, diag_ref, out_ref):
    leaf = leaf_ref[0]
    chunk = lane_chunk(32)
    common = []
    sources = []
    for w, u in PAIRS:
        q = PAIRS.index((w, u))
        for i in range(2**w):
            sources.append((leaf // 2**w * 2**w + i, q))
    for tile in range(C_TILES):
        parts = []
        for c in range(4):
            if 4 * tile + c < BLOCKS:
                source, q = sources[4 * tile + c]
                values = columns_ref[source, :, 128 * (q // 4) : 128 * (q // 4) + 128].astype(F32)
                shift = (c - q) % 4 * 32
                parts.append(values if shift == 0 else pltpu.roll(values, shift, 1))
        common.append(merge(parts, chunk).astype(BF))
    for tile in range(D0_TILES + D1_TILES):
        common.append(diag_ref[:, 128 * tile : 128 * tile + 128])
    rhs = jnp.transpose(rhs_ref[...].reshape(128, 128))
    high = rhs.astype(BF).astype(F32)
    low = rhs - high
    for tile in range(16):
        both = jnp.concatenate([high[8 * tile : 8 * tile + 8], low[8 * tile : 8 * tile + 8]], 0)
        out_ref[tile, 0:RHS_ROWS] = both.astype(BF)
        for n, values in enumerate(common):
            out_ref[tile, C_AT + 32 * n : C_AT + 32 * n + 32] = values


def couple(parts, bd_ref):
    out = []
    for j in range(4):
        total = None
        for vector, m in parts:
            term = dot_nt(vector[:, 128 * j : 128 * j + 128], bd_ref[m, j])
            total = term if total is None else total + term
        out.append(-total)
    return jnp.concatenate(out, 1)


def first_kernel(leaf_ref, msg_ref, b_ref, bd_ref, d0_ref, d1_ref, y0_ref, p1_ref):
    leaf = leaf_ref[0]
    chunk8 = lane_chunk(8)
    rhs = Rolled(
        [msg_ref[t, 0:8].astype(F32) + msg_ref[t, 8:16].astype(F32) for t in range(16)]
    )
    for v in range(4):
        for j in range(4):
            parts = [rhs.take(4 * j + c, v, c) for c in range(4)]
            b_ref[v, :, 128 * j : 128 * j + 128] = merge(parts, chunk8)
    row_chunk = lax.broadcasted_iota(jnp.int32, (128, 128), 0) // 32
    same = row_chunk == lane_chunk(128)
    rows = lax.broadcasted_iota(jnp.int32, (128, 128), 0)
    lanes = lax.broadcasted_iota(jnp.int32, (128, 128), 1)
    pick = [
        jnp.where(rows == lanes % 32 + 32 * c, 1.0, 0.0).astype(BF) for c in range(4)
    ]
    for m in range(BLOCKS):
        at = C_AT + 32 * (m // 4)
        for j in range(4):
            block = msg_ref[4 * j : 4 * j + 4, at : at + 32, :].reshape(128, 128)
            spread = dot_nn(block, pick[m % 4])
            bd_ref[m, j] = jnp.where(same, spread, 0.0).astype(BF)
    for tile in range(D0_TILES):
        at = D0_AT + 32 * tile
        d0_ref[:, 128 * tile : 128 * tile + 128] = msg_ref[:, at : at + 32, :].reshape(512, 128)
    for tile in range(D1_TILES):
        at = D1_AT + 32 * tile
        d1_ref[:, 128 * tile : 128 * tile + 128] = msg_ref[:, at : at + 32, :].reshape(512, 128)
    y0 = dot_nt(b_ref[0].astype(BF), d0_ref[...]).astype(BF)
    y0_ref[...] = y0
    for i in range(2):
        mine = jnp.where(leaf % 2 == i, b_ref[1], 0.0)
        p1_ref[:, 512 * i : 512 * i + 512] = (couple([(y0, i)], bd_ref) + mine).astype(BF)


def times_rows(z, d_ref, width):
    total = jnp.zeros((8, 512), F32)
    for at in range(0, width, 1024):
        total = total + dot_nt(z[:, at : at + 1024], d_ref[:, at : at + 1024])
    return total


def forward_kernel(level, leaf_ref, own_ref, other_ref, d_ref, b_ref, bd_ref, *rest):
    ys, (y_ref, p_ref) = rest[:-2], rest[-2:]
    leaf = leaf_ref[0]
    z = (own_ref[...].astype(F32) + other_ref[...].astype(F32)).astype(BF)
    y = times_rows(z, d_ref, z.shape[1]).astype(BF)
    y_ref[...] = y
    vectors = [r[...] for r in ys] + [y]
    span = 2 ** (level + 1)
    for i in range(span):
        mine = jnp.where(leaf % span == i, b_ref[level + 1], 0.0)
        parts = [(vec, OFFSET[level + 1, u] + i) for u, vec in enumerate(vectors)]
        p_ref[:, 512 * i : 512 * i + 512] = (couple(parts, bd_ref) + mine).astype(BF)


def top_kernel(own_ref, other_ref, d_ref, x_ref):
    z = (own_ref[...].astype(F32) + other_ref[...].astype(F32)).astype(BF)
    y = times_rows(z, d_ref, 4096).astype(BF)
    for at in range(0, 4096, 1024):
        x_ref[:, at : at + 1024] = dot_nn(y, d_ref[:, at : at + 1024]).astype(BF)


def back_kernel(level, leaf_ref, own_ref, other_ref, d_ref, y_ref, bd_ref, *rest):
    first = level == 2
    pending = () if first else rest[: level + 1]
    outs = rest[len(pending) :]
    x_ref, xp_ref, next_refs = outs[0], outs[1], outs[2:]
    leaf = leaf_ref[0]
    span = 2 ** (level + 1)
    total = own_ref[...].astype(F32) + other_ref[...].astype(F32)
    x = total.astype(BF)
    mine = total[:, 0:512]
    for i in range(1, span):
        mine = jnp.where(leaf % span == i, total[:, 512 * i : 512 * i + 512], mine)
    x_ref[...] = mine
    for u in range(level + 1):
        columns = []
        for j in range(4):
            term = None
            for i in range(span):
                at = 512 * i + 128 * j
                part = dot_nn(x[:, at : at + 128], bd_ref[OFFSET[level + 1, u] + i, j])
                term = part if term is None else term + part
            columns.append(term)
        p = jnp.concatenate(columns, 1)
        if not first:
            p = p + pending[u][...]
        if u < level:
            next_refs[u][...] = p
        else:
            q = (y_ref[...].astype(F32) - p).astype(BF)
    if level > 0:
        width = 512 * 2**level
        for at in range(0, width, 1024):
            xp_ref[:, at : at + 1024] = dot_nn(q, d_ref[:, at : at + 1024]).astype(BF)
    else:
        xp_ref[...] = dot_nn(q, d_ref[...])


def pack_kernel(x0_ref, x1_ref, x2_ref, x3_ref, out_ref):
    chunk = lane_chunk(8)
    tiles = [r[:, 128 * j : 128 * j + 128] for r in (x0_ref, x1_ref, x2_ref, x3_ref) for j in range(4)]
    rolled = Rolled(tiles)
    for t in range(16):
        parts = [rolled.take(4 * v + t // 4, t % 4, v) for v in range(4)]
        out_ref[t] = merge(parts, chunk)


def shape(dims, kind=BF):
    return jax.ShapeDtypeStruct(dims, kind)


def reduce_over(part, level):
    hops = [
        [(i, i ^ 1) for i in range(8)],
        [(i, i ^ 2) for i in range(8)],
        [(i, (3 - i // 2) * 2 + i % 2) for i in range(8)],
    ]
    for n in range(level):
        other = lax.ppermute(part, "leaf", hops[n])
        if n == level - 1:
            return part, other
        part = (part.astype(F32) + other.astype(F32)).astype(BF)


def local(right_sides, diag_inverse, coupling, pattern):
    leaf = lax.axis_index("leaf").astype(jnp.int32).reshape(1)
    d23 = lax.all_gather(diag_inverse[:, 1536:], "tile", axis=0, tiled=True)
    split = pl.pallas_call(
        split_kernel,
        out_shape=shape((8, 32, 256)),
        in_specs=[VMEM, SMEM],
        out_specs=VMEM,
        compiler_params=params(),
        name="split_couplings",
    )(coupling, pattern)
    columns = lax.all_to_all(split, "leaf", 0, 0, tiled=True)
    message = pl.pallas_call(
        message_kernel,
        out_shape=shape((16, MESSAGE, 128)),
        grid=(1,),
        in_specs=[
            SMEM,
            pl.BlockSpec((8, 32, 256), lambda i: (0, 0, 0)),
            pl.BlockSpec((4, 32, 128), lambda i: (0, 0, 0)),
            pl.BlockSpec((32, 1536), lambda i: (0, 0)),
        ],
        out_specs=pl.BlockSpec((16, MESSAGE, 128), lambda i: (0, 0, 0)),
        compiler_params=params(),
        name="message",
    )(leaf, columns, right_sides, diag_inverse)
    message = lax.all_to_all(message, "tile", 0, 0, tiled=True)
    b, bd, d0, d1, y0, p1 = pl.pallas_call(
        first_kernel,
        out_shape=(
            shape((4, 8, 512), F32),
            shape((BLOCKS, 4, 128, 128)),
            shape((512, 512)),
            shape((512, 1024)),
            shape((8, 512)),
            shape((8, 1024)),
        ),
        in_specs=[SMEM, VMEM],
        out_specs=(VMEM,) * 6,
        compiler_params=params(),
        name="level0",
    )(leaf, message)
    d2, d3 = d23[:, :2048], d23[:, 2048:]

    def forward(level, part, d, ys):
        own, other = reduce_over(part, level)
        return pl.pallas_call(
            functools.partial(forward_kernel, level),
            out_shape=(shape((8, 512)), shape((8, 512 * 2 ** (level + 1)))),
            in_specs=[SMEM] + [VMEM] * (5 + len(ys)),
            out_specs=(VMEM,) * 2,
            compiler_params=params(),
            name="forward%d" % level,
        )(leaf, own, other, d, b, bd, *ys)

    y1, p2 = forward(1, p1, d1, (y0,))
    y2, p3 = forward(2, p2, d2, (y0, y1))
    own, other = reduce_over(p3, 3)
    xp = pl.pallas_call(
        top_kernel,
        out_shape=shape((8, 4096)),
        in_specs=[VMEM] * 3,
        out_specs=VMEM,
        compiler_params=params(),
        name="level3",
    )(own, other, d3)

    def back(level, part, d, y, pending):
        own, other = reduce_over(part, level + 1)
        out = [shape((8, 512), F32)]
        out.append(shape((8, 512 * 2**level), BF if level else F32))
        out += [shape((8, 512), F32)] * level
        return pl.pallas_call(
            functools.partial(back_kernel, level),
            out_shape=tuple(out),
            in_specs=[SMEM] + [VMEM] * (5 + len(pending)),
            out_specs=(VMEM,) * len(out),
            compiler_params=params(),
            name="back%d" % level,
        )(leaf, own, other, d, y, bd, *pending)

    x3, xp, *pending = back(2, xp, d2, y2, ())
    x2, xp, *pending = back(1, xp, d1, y1, pending)
    x1, x0 = back(0, xp, d0, y0, pending)
    packed = pl.pallas_call(
        pack_kernel,
        out_shape=shape((16, 8, 128), F32),
        in_specs=[VMEM] * 4,
        out_specs=VMEM,
        compiler_params=params(),
        name="pack",
    )(x0, x1, x2, x3)
    packed = lax.all_to_all(packed, "tile", 0, 0, tiled=True)
    return jnp.transpose(packed.reshape(128, 128)).reshape(4, 32, 128)


def solution(mesh):
    placed = (
        P(None, ("leaf", "tile"), None),
        P(("leaf", "tile"), None),
        P(("leaf", "tile"), None),
        P(("leaf", "tile"), None),
    )
    return jax.shard_map(
        local,
        mesh=mesh,
        in_specs=placed,
        out_specs=P(None, ("leaf", "tile"), None),
        check_vma=False,
    )
```

time: 745 us -> 155 us (0.21)
  waiting for transfers between devices: 553 us -> 42.2 us
  blocking collectives: 148 us -> 56.3 us
  Pallas kernels: 0 us -> 17.3 us
  starting transfers between devices: 0.42 us -> 12.8 us
  matrix products: 8.43 us -> 0 us
    reduce_scatter x7 -> x0, waiting for transfers between devices: 256 us -> none  [the longest x3 91.7 us: group_sum(): lax.psum_scatter(padded.astype(jnp.bfloat16), 'leaf', scatter_dimension=1...]
    unnamed x14 -> x1, waiting for transfers between devices: 255 us -> 0.02 us
    all_gather x9 -> x0, blocking collectives: 148 us -> none  [the longest x3 70.3 us: local(): lax.all_gather(group_rows, 'tile', axis=1, tiled=True)]
    all_to_all x0 -> x2, blocking collectives: none -> 56.3 us  [the longest x1 44 us: local(): message = lax.all_to_all(message, 'tile', 0, 0, tiled=True)]
    all_gather x1, waiting for transfers between devices: 41.9 us -> 14.5 us  [local(): d23 = lax.all_gather(diag_inverse[:, 1536:], 'tile', axis=0, tiled=True)]
    ppermute x0 -> x12, waiting for transfers between devices: none -> 21.6 us  [reduce_over(): other = lax.ppermute(part, 'leaf', hops[n])]
    pallas_call x0 -> x10, Pallas kernels: none -> 17.3 us  [the longest x2 5.54 us: forward(): pl.pallas_call(functools.partial(forward_kernel, level), out_shape=(shape...]
    ppermute x0 -> x12, starting transfers between devices: none -> 8.21 us  [reduce_over(): other = lax.ppermute(part, 'leaf', hops[n])]
  transfers between devices with their start and end apart: 11 -> 14, of which waited for: 11 -> 13; matrix products, arithmetic and copies ran while one was open for 0% -> 3% of each run, Pallas kernels for 0% -> 4%
where the time goes in v1:
time: 155 us
  blocking collectives  56.3 us (36%)
  waiting for transfers between devices  42.2 us (27%)
  Pallas kernels  17.3 us (11%)
  between operations  13.5 us (9%)
  starting transfers between devices  12.8 us (8%)
  local copies, waits for them, and re-layouts  12.7 us (8%)
    all_to_all x1, blocking collectives, local(): message = lax.all_to_all(message, 'tile', 0, 0, tiled=True)  44 us
    ppermute x12, waiting for transfers between devices, reduce_over(): other = lax.ppermute(part, 'leaf', hops[n])  21.6 us
    all_gather x1, waiting for transfers between devices, local(): d23 = lax.all_gather(diag_inverse[:, 1536:], 'tile', axis=0, tiled=True)  14.5 us
    all_to_all x1, blocking collectives, local(): packed = lax.all_to_all(packed, 'tile', 0, 0, tiled=True)  12.4 us
    ppermute x12, starting transfers between devices, reduce_over(): other = lax.ppermute(part, 'leaf', hops[n])  8.21 us
    all_to_all x1, waiting for transfers between devices, local(): columns = lax.all_to_all(split, 'leaf', 0, 0, tiled=True)  6.1 us
    unnamed x14, local copies, waits for them, and re-layouts  5.73 us
    pallas_call x2, Pallas kernels, forward(): pl.pallas_call(functools.partial(forward_kernel, level), out_shape=(shape...  5.54 us
  transfers between devices with their start and end apart: 14, of which 13 were waited for; matrix products, arithmetic and copies ran while one was open for 3% of the time, Pallas kernels for 4%

profile of v1, /device:TPU:0, one launch (start us, length us, event | category | flops | bytes accessed | tf_op | source)
XLA Modules:
  0.0 154.8 jit_solution(7368262479496035206)
XLA Ops:
  6.5 1.8 %slice.9 = bf16[32,6144]{1,0:T(8,128)(2,1)} slice(bf16[32,7680]{1,0:T(8,128)(2,1)} %diag_ref.1), slice={[0:32], [1536:7680]} | slice | bytes 786432 | tf_op jit(solution)/shard_map/slice | solution.py:255
  8.3 0.0 all-gather.2.cloned.1.call-update
  8.3 0.0 copy-start.2
  8.3 0.9 copy-done.2
  9.2 0.7 copy-done.4
  9.9 1.3 split_couplings.1
  11.2 4.6 %all-to-all-start = ((bf16[8,32,256]{2,1,0:T(8,128)(2,1)}), bf16[8,32,256]{2,1,0:T(8,128)(2,1)S(1)}, u32[]{:S(2)}, u32[]{:S(2)}) async-start(bf16[8,32,256]{2,1,0:T(8,128)(2,1)} %split_couplings.1), calls=%async_computation | async-start | bytes 262144 | tf_op jit(solution)/shard_map/all_to_all | solution.py:264
  15.8 6.1 %all-to-all-done.columns_ref = bf16[8,32,256]{2,1,0:T(8,128)(2,1)S(1)} async-done(((bf16[8,32,256]{2,1,0:T(8,128)(2,1)}), bf16[8,32,256]{2,1,0:T(8,128)(2,1)S(1)}, u32[]{:S(2)}, u32[]{:S(2)}) %all-to-all-start) | async-done | bytes 131104 | tf_op jit(solution)/shard_map/all_to_all | solution.py:264
  21.9 1.0 copy-done.1
  22.9 0.8 copy-done.3
  23.8 0.4 message.1
  24.1 44.0 %all_to_all.15.msg_ref = bf16[16,688,128]{2,1,0:T(8,128)(2,1)S(1)} all-to-all(bf16[16,688,128]{2,1,0:T(8,128)(2,1)S(1)} %message.1), channel_id=1, replica_groups=mesh['leaf'=8,'tile'=16] {'tile'}, dimensions={0} | all-to-all | bytes 5636096 | tf_op jit(solution)/shard_map/all_to_all | solution.py:279
  68.1 3.8 %level0.1 = (f32[4,8,512]{2,1,0:T(8,128)S(1)}, bf16[34,4,128,128]{3,2,1,0:T(8,128)(2,1)}, bf16[512,512]{1,0:T(8,128)(2,1)S(1)}, bf16[512,1024]{1,0:T(8,128)(2,1)...) custom-call(s32[1]{0:T(128)} %bitcast.leaf_ref, bf16[16,688,128]{2,1,0:T(8,128)(2,1)S(1)} %all_to_all.15.msg_ref), custom_call_target="tpu_custom_call" | custom-call | tf_op jit(solution)/shard_map/level0/pallas_call | solution.py:280
  71.8 1.2 collective-permute-done.other_ref
  73.0 2.3 %copy-done = bf16[34,4,128,128]{3,2,1,0:T(8,128)(2,1)S(1)} copy-done((bf16[34,4,128,128]{3,2,1,0:T(8,128)(2,1)S(1)}, bf16[34,4,128,128]{3,2,1,0:T(8,128)(2,1)}, u32[]{:S(2)}) %copy-start) | copy-done | bytes 4456472
  75.3 1.0 forward1.1
  76.3 0.2 collective-permute-start.1
  76.5 1.0 collective-permute-done.1
  77.5 1.3 collective-permute-start.2
  78.8 14.5 %all-gather.2.cloned.1.call-done = bf16[512,6144]{1,0:T(8,128)(2,1)} async-done(((bf16[32,6144]{1,0:T(8,128)(2,1)}), bf16[512,6144]{1,0:T(8,128)(2,1)}) %all-gather.2.cloned.1.call-update) | async-done | bytes 6291472 | tf_op jit(solution)/shard_map/all_gather | solution.py:255
  93.3 1.8 %slice.12.d_ref = bf16[512,2048]{1,0:T(8,128)(2,1)S(1)} slice(bf16[512,6144]{1,0:T(8,128)(2,1)} %all-gather.2.cloned.1.call-done), slice={[0:512], [0:2048]} | slice | bytes 4194304 | tf_op jit(solution)/shard_map/slice | solution.py:295
  95.1 0.0 collective-permute-done.2.other_ref
  95.1 4.5 %forward2.1 = (bf16[8,512]{1,0:T(8,128)(2,1)S(1)}, bf16[8,4096]{1,0:T(8,128)(2,1)S(1)}) custom-call(s32[1]{0:T(128)} %bitcast.leaf_ref, bf16[8,2048]{1,0:T(8,128)(2,1)S(1)} %add_convert_fusion.5.own_ref, bf16[8,2048]{1,0:T(8,128)(2,1)S(1)} %collective-permute-done.2.other_ref, bf16[512,2048]{1,0:T(8,128)(2,1)S(1)} %slice.12.d_ref, ...), custom_call_target="tpu_custom_call" | custom-call | tf_op jit(solution)/shard_map/forward2/pallas_call | solution.py:299
  99.7 0.0 collective-permute-start.3
  99.7 1.3 collective-permute-done.3
  101.0 1.3 collective-permute-start.4
  102.3 3.0 %collective-permute-done.4 = bf16[8,4096]{1,0:T(8,128)(2,1)S(1)} collective-permute-done((bf16[8,4096]{1,0:T(8,128)(2,1)S(1)}, bf16[8,4096]{1,0:T(8,128)(2,1)S(1)}, u32[]{:S(2)}, u32[]{:S(2)}) %collective-permute-start.4) | collective-permute-done | bytes 65568 | tf_op jit(solution)/shard_map/ppermute | solution.py:247
  105.4 2.6 %collective-permute-start.5 = (bf16[8,4096]{1,0:T(8,128)(2,1)S(1)}, bf16[8,4096]{1,0:T(8,128)(2,1)S(1)}, u32[]{:S(2)}, u32[]{:S(2)}) collective-permute-start(bf16[8,4096]{1,0:T(8,128)(2,1)S(1)} %add_convert_fusion.2.own_ref), channel_id=1, source_target_pairs={{0,96},{16,112},{32,64},{48,80},{64,32},{80,48},{96,0},{112,16},{1... | collective-permute-start | bytes 196616 | tf_op jit(solution)/shard_map/ppermute | solution.py:247
  107.9 2.6 %slice.13.d_ref = bf16[512,4096]{1,0:T(8,128)(2,1)S(1)} slice(bf16[512,6144]{1,0:T(8,128)(2,1)} %all-gather.2.cloned.1.call-done), slice={[0:512], [2048:6144]} | slice | bytes 8388608 | tf_op jit(solution)/shard_map/slice | solution.py:295
  110.6 0.0 slice-start.1
  110.6 0.3 collective-permute-done.5.other_ref
  110.9 1.8 %level3.1 = bf16[8,4096]{1,0:T(8,128)(2,1)S(1)} custom-call(bf16[8,4096]{1,0:T(8,128)(2,1)S(1)} %add_convert_fusion.2.own_ref, bf16[8,4096]{1,0:T(8,128)(2,1)S(1)} %collective-permute-done.5.other_ref, bf16[512,4096]{1,0:T(8,128)(2,1)S(1)} %slice.13.d_ref), custom_call_target="tpu_custom_call" | custom-call | tf_op jit(solution)/shard_map/level3/pallas_call | solution.py:311
  112.7 0.0 collective-permute-start.6
  112.7 1.3 collective-permute-done.6
  114.0 0.1 collective-permute-start.7
  114.1 4.2 %collective-permute-done.7 = bf16[8,4096]{1,0:T(8,128)(2,1)S(1)} collective-permute-done((bf16[8,4096]{1,0:T(8,128)(2,1)S(1)}, bf16[8,4096]{1,0:T(8,128)(2,1)S(1)}, u32[]{:S(2)}, u32[]{:S(2)}) %collective-permute-start.7) | collective-permute-done | bytes 65568 | tf_op jit(solution)/shard_map/ppermute | solution.py:247
  118.4 2.6 %collective-permute-start.8 = (bf16[8,4096]{1,0:T(8,128)(2,1)S(1)}, bf16[8,4096]{1,0:T(8,128)(2,1)S(1)}, u32[]{:S(2)}, u32[]{:S(2)}) collective-permute-start(bf16[8,4096]{1,0:T(8,128)(2,1)S(1)} %add_convert_fusion.own_ref), channel_id=1, source_target_pairs={{0,96},{16,112},{32,64},{48,80},{64,32},{80,48},{96,0},{112,16},{1... | collective-permute-start | bytes 196616 | tf_op jit(solution)/shard_map/ppermute | solution.py:247
  121.0 3.0 %collective-permute-done.8.other_ref = bf16[8,4096]{1,0:T(8,128)(2,1)S(1)} collective-permute-done((bf16[8,4096]{1,0:T(8,128)(2,1)S(1)}, bf16[8,4096]{1,0:T(8,128)(2,1)S(1)}, u32[]{:S(2)}, u32[]{:S(2)}) %collective-permute-start.8) | collective-permute-done | bytes 65568 | tf_op jit(solution)/shard_map/ppermute | solution.py:247
  123.9 3.5 %back2.1 = (f32[8,512]{1,0:T(8,128)S(1)}, bf16[8,2048]{1,0:T(8,128)(2,1)S(1)}, f32[8,512]{1,0:T(8,128)S(1)}, f32[8,512]{1,0:T(8,128)S(1)}) custom-call(s32[1]{0:T(128)} %bitcast.leaf_ref, bf16[8,4096]{1,0:T(8,128)(2,1)S(1)} %add_convert_fusion.own_ref, bf16[8,4096]{1,0:T(8,128)(2,1)S(1)} %collective-permute-done.8.other_ref, ...), custom_call_target="tpu_custom_call" | custom-call | tf_op jit(solution)/shard_map/back2/pallas_call | solution.py:325
  127.4 1.2 collective-permute-done.9
  128.7 0.1 collective-permute-start.10
  128.8 3.9 %collective-permute-done.10.other_ref = bf16[8,2048]{1,0:T(8,128)(2,1)S(1)} collective-permute-done((bf16[8,2048]{1,0:T(8,128)(2,1)S(1)}, bf16[8,2048]{1,0:T(8,128)(2,1)S(1)}, u32[]{:S(2)}, u32[]{:S(2)}) %collective-permute-start.10) | collective-permute-done | bytes 32800 | tf_op jit(solution)/shard_map/ppermute | solution.py:247
  132.7 0.6 back1.1
  133.2 1.2 collective-permute-done.11.other_ref
  134.4 0.3 back0.1
  134.7 0.1 pack.1
  134.9 12.4 %all_to_all.16 = f32[16,8,128]{2,1,0:T(8,128)S(1)} all-to-all(f32[16,8,128]{2,1,0:T(8,128)S(1)} %pack.1), channel_id=1, replica_groups=mesh['leaf'=8,'tile'=16] {'tile'}, dimensions={0} | all-to-all | bytes 131072 | tf_op jit(solution)/shard_map/all_to_all | solution.py:345
  147.2 0.7 copy.5
  (18 shorter events, 0.1 us)
Async XLA Ops:
  6.5 86.8 %all-gather.2.cloned.1.call-start = ((), (), s32[]{:S(2)}) async-start(), calls=%async_computation.3 | async-start | bytes 6684672 | tf_op jit(solution)/shard_map/all_gather | solution.py:255
  8.3 0.9 copy-start.2
  9.2 0.7 copy-start.4
  11.2 10.7 %all-to-all-start = ((bf16[8,32,256]{2,1,0:T(8,128)(2,1)}), bf16[8,32,256]{2,1,0:T(8,128)(2,1)S(1)}, u32[]{:S(2)}, u32[]{:S(2)}) async-start(bf16[8,32,256]{2,1,0:T(8,128)(2,1)} %split_couplings.1), calls=%async_computation | async-start | bytes 262144 | tf_op jit(solution)/shard_map/all_to_all | solution.py:264
  21.9 1.0 copy-start.1
  22.9 0.8 copy-start.3
  71.8 1.2 collective-permute-start
  73.0 2.3 %copy-start = (bf16[34,4,128,128]{3,2,1,0:T(8,128)(2,1)S(1)}, bf16[34,4,128,128]{3,2,1,0:T(8,128)(2,1)}, u32[]{:S(2)}) copy-start(bf16[34,4,128,128]{3,2,1,0:T(8,128)(2,1)} %get-tuple-element.27.bd_ref) | copy-start | bytes 13369348
  76.3 1.2 collective-permute-start.1
  77.5 17.6 %collective-permute-start.2 = (bf16[8,2048]{1,0:T(8,128)(2,1)S(1)}, bf16[8,2048]{1,0:T(8,128)(2,1)S(1)}, u32[]{:S(2)}, u32[]{:S(2)}) collective-permute-start(bf16[8,2048]{1,0:T(8,128)(2,1)S(1)} %add_convert_fusion.5.own_ref), channel_id=1, source_target_pairs={{0,32},{16,48},{32,0},{48,16},{64,96},{80,112},{96,64},{112,80},{1... | collective-permute-start | bytes 98312 | tf_op jit(solution)/shard_map/ppermute | solution.py:247
  99.7 1.3 collective-permute-start.3
  101.0 4.3 %collective-permute-start.4 = (bf16[8,4096]{1,0:T(8,128)(2,1)S(1)}, bf16[8,4096]{1,0:T(8,128)(2,1)S(1)}, u32[]{:S(2)}, u32[]{:S(2)}) collective-permute-start(bf16[8,4096]{1,0:T(8,128)(2,1)S(1)} %add_convert_fusion.3), channel_id=1, source_target_pairs={{0,32},{16,48},{32,0},{48,16},{64,96},{80,112},{96,64},{112,80},{1... | collective-permute-start | bytes 196616 | tf_op jit(solution)/shard_map/ppermute | solution.py:247
  105.4 5.6 %collective-permute-start.5 = (bf16[8,4096]{1,0:T(8,128)(2,1)S(1)}, bf16[8,4096]{1,0:T(8,128)(2,1)S(1)}, u32[]{:S(2)}, u32[]{:S(2)}) collective-permute-start(bf16[8,4096]{1,0:T(8,128)(2,1)S(1)} %add_convert_fusion.2.own_ref), channel_id=1, source_target_pairs={{0,96},{16,112},{32,64},{48,80},{64,32},{80,48},{96,0},{112,16},{1... | collective-permute-start | bytes 196616 | tf_op jit(solution)/shard_map/ppermute | solution.py:247
  107.9 24.7 %slice-start = ((s8[4456448]{0:T(1024)(128)(4,1)}), s8[4194304]{0:T(1024)(128)(4,1)S(1)}, s32[]{:S(2)}) async-start(s8[4456448]{0:T(1024)(128)(4,1)} %bitcast.5), calls=%async_computation.4 | async-start | bytes 8388608
  110.6 22.1 %slice-start.1 = ((s8[4456448]{0:T(1024)(128)(4,1)}), s8[262144]{0:T(1024)(128)(4,1)S(1)}, s32[]{:S(2)}) async-start(s8[4456448]{0:T(1024)(128)(4,1)} %bitcast.5), calls=%async_computation.5 | async-start | bytes 524288
  112.7 1.3 collective-permute-start.6
  114.0 4.3 %collective-permute-start.7 = (bf16[8,4096]{1,0:T(8,128)(2,1)S(1)}, bf16[8,4096]{1,0:T(8,128)(2,1)S(1)}, u32[]{:S(2)}, u32[]{:S(2)}) collective-permute-start(bf16[8,4096]{1,0:T(8,128)(2,1)S(1)} %add_convert_fusion.1), channel_id=1, source_target_pairs={{0,32},{16,48},{32,0},{48,16},{64,96},{80,112},{96,64},{112,80},{1... | collective-permute-start | bytes 196616 | tf_op jit(solution)/shard_map/ppermute | solution.py:247
  118.4 5.6 %collective-permute-start.8 = (bf16[8,4096]{1,0:T(8,128)(2,1)S(1)}, bf16[8,4096]{1,0:T(8,128)(2,1)S(1)}, u32[]{:S(2)}, u32[]{:S(2)}) collective-permute-start(bf16[8,4096]{1,0:T(8,128)(2,1)S(1)} %add_convert_fusion.own_ref), channel_id=1, source_target_pairs={{0,96},{16,112},{32,64},{48,80},{64,32},{80,48},{96,0},{112,16},{1... | collective-permute-start | bytes 196616 | tf_op jit(solution)/shard_map/ppermute | solution.py:247
  127.4 1.2 collective-permute-start.9
  128.7 4.0 %collective-permute-start.10 = (bf16[8,2048]{1,0:T(8,128)(2,1)S(1)}, bf16[8,2048]{1,0:T(8,128)(2,1)S(1)}, u32[]{:S(2)}, u32[]{:S(2)}) collective-permute-start(bf16[8,2048]{1,0:T(8,128)(2,1)S(1)} %add_convert_fusion.4.own_ref), channel_id=1, source_target_pairs={{0,32},{16,48},{32,0},{48,16},{64,96},{80,112},{96,64},{112,80},{1... | collective-permute-start | bytes 98312 | tf_op jit(solution)/shard_map/ppermute | solution.py:247
  133.2 1.2 collective-permute-start.11
Sparse Core Ops, SparseCore 0:
  9.5 83.7 all-gather.1

commit v2 on v1

--- a/solution.py
+++ b/solution.py
@@ -6,6 +6,7 @@
 from jax.experimental import pallas as pl
 from jax.experimental.pallas import tpu as pltpu
 from jax.sharding import PartitionSpec as P
+
 
 BF = jnp.bfloat16
 F32 = jnp.float32
@@ -14,11 +15,12 @@
 BLOCKS = 34
 VMEM = pl.BlockSpec(memory_space=pltpu.VMEM)
 SMEM = pl.BlockSpec(memory_space=pltpu.SMEM)
-RHS_ROWS, C_TILES, D0_TILES, D1_TILES = 16, 9, 4, 8
+RHS_ROWS, C_TILES, D0_TILES, D1_TILES, D2_TILES = 16, 9, 4, 8, 16
 C_AT = RHS_ROWS
 D0_AT = C_AT + 32 * C_TILES
 D1_AT = D0_AT + 32 * D0_TILES
-MESSAGE = D1_AT + 32 * D1_TILES
+D2_AT = D1_AT + 32 * D1_TILES
+MESSAGE = D2_AT + 32 * D2_TILES
 
 
 def params(mib=48):
@@ -100,7 +102,7 @@
                 shift = (c - q) % 4 * 32
                 parts.append(values if shift == 0 else pltpu.roll(values, shift, 1))
         common.append(merge(parts, chunk).astype(BF))
-    for tile in range(D0_TILES + D1_TILES):
+    for tile in range(D0_TILES + D1_TILES + D2_TILES):
         common.append(diag_ref[:, 128 * tile : 128 * tile + 128])
     rhs = jnp.transpose(rhs_ref[...].reshape(128, 128))
     high = rhs.astype(BF).astype(F32)
@@ -123,7 +125,7 @@
     return jnp.concatenate(out, 1)
 
 
-def first_kernel(leaf_ref, msg_ref, b_ref, bd_ref, d0_ref, d1_ref, y0_ref, p1_ref):
+def first_kernel(leaf_ref, msg_ref, b_ref, bd_ref, d0_ref, d1_ref, d2_ref, y0_ref, p1_ref):
     leaf = leaf_ref[0]
     chunk8 = lane_chunk(8)
     rhs = Rolled(
@@ -146,12 +148,14 @@
             block = msg_ref[4 * j : 4 * j + 4, at : at + 32, :].reshape(128, 128)
             spread = dot_nn(block, pick[m % 4])
             bd_ref[m, j] = jnp.where(same, spread, 0.0).astype(BF)
-    for tile in range(D0_TILES):
-        at = D0_AT + 32 * tile
-        d0_ref[:, 128 * tile : 128 * tile + 128] = msg_ref[:, at : at + 32, :].reshape(512, 128)
-    for tile in range(D1_TILES):
-        at = D1_AT + 32 * tile
-        d1_ref[:, 128 * tile : 128 * tile + 128] = msg_ref[:, at : at + 32, :].reshape(512, 128)
+    for ref, first, tiles in (
+        (d0_ref, D0_AT, D0_TILES),
+        (d1_ref, D1_AT, D1_TILES),
+        (d2_ref, D2_AT, D2_TILES),
+    ):
+        for tile in range(tiles):
+            at = first + 32 * tile
+            ref[:, 128 * tile : 128 * tile + 128] = msg_ref[:, at : at + 32, :].reshape(512, 128)
     y0 = dot_nt(b_ref[0].astype(BF), d0_ref[...]).astype(BF)
     y0_ref[...] = y0
     for i in range(2):
@@ -180,11 +184,19 @@
         p_ref[:, 512 * i : 512 * i + 512] = (couple(parts, bd_ref) + mine).astype(BF)
 
 
-def top_kernel(own_ref, other_ref, d_ref, x_ref):
+def top_kernel(own_ref, other_ref, *rest):
+    pieces, x_ref = rest[:-1], rest[-1]
+
+    def rows(at):
+        return jnp.concatenate([p[:, at : at + 512] for p in pieces], 0)
+
     z = (own_ref[...].astype(F32) + other_ref[...].astype(F32)).astype(BF)
-    y = times_rows(z, d_ref, 4096).astype(BF)
-    for at in range(0, 4096, 1024):
-        x_ref[:, at : at + 1024] = dot_nn(y, d_ref[:, at : at + 1024]).astype(BF)
+    y = jnp.zeros((8, 512), F32)
+    for at in range(0, 4096, 512):
+        y = y + dot_nt(z[:, at : at + 512], rows(at))
+    y = y.astype(BF)
+    for at in range(0, 4096, 512):
+        x_ref[:, at : at + 512] = dot_nn(y, rows(at)).astype(BF)
 
 
 def back_kernel(level, leaf_ref, own_ref, other_ref, d_ref, y_ref, bd_ref, *rest):
@@ -250,9 +262,20 @@
         part = (part.astype(F32) + other.astype(F32)).astype(BF)
 
 
+def shift_x(values, by):
+    return lax.ppermute(values, "tile", [(t, t // 4 * 4 + (t + by) % 4) for t in range(16)])
+
+
+def shift_z(values, by):
+    return lax.ppermute(values, "tile", [(t, (t + 4 * by) % 16) for t in range(16)])
+
+
 def local(right_sides, diag_inverse, coupling, pattern):
     leaf = lax.axis_index("leaf").astype(jnp.int32).reshape(1)
-    d23 = lax.all_gather(diag_inverse[:, 1536:], "tile", axis=0, tiled=True)
+    upper, lower = diag_inverse[0:16, 3584:], diag_inverse[16:32, 3584:]
+    upper = [upper] + [shift_x(upper, k) for k in (1, 2, 3)]
+    lower = [lower] + [shift_z(lower, k) for k in (1, 2, 3)]
+    upper, lower = jnp.concatenate(upper, 0), jnp.concatenate(lower, 0)
     split = pl.pallas_call(
         split_kernel,
         out_shape=shape((8, 32, 256)),
@@ -262,7 +285,7 @@
         name="split_couplings",
     )(coupling, pattern)
     columns = lax.all_to_all(split, "leaf", 0, 0, tiled=True)
-    message = pl.pallas_call(
+    message_call = pl.pallas_call(
         message_kernel,
         out_shape=shape((16, MESSAGE, 128)),
         grid=(1,),
@@ -270,29 +293,34 @@
             SMEM,
             pl.BlockSpec((8, 32, 256), lambda i: (0, 0, 0)),
             pl.BlockSpec((4, 32, 128), lambda i: (0, 0, 0)),
-            pl.BlockSpec((32, 1536), lambda i: (0, 0)),
+            pl.BlockSpec((32, 3584), lambda i: (0, 0)),
         ],
         out_specs=pl.BlockSpec((16, MESSAGE, 128), lambda i: (0, 0, 0)),
         compiler_params=params(),
         name="message",
-    )(leaf, columns, right_sides, diag_inverse)
+    )
+    message = message_call(leaf, columns, right_sides, diag_inverse)
     message = lax.all_to_all(message, "tile", 0, 0, tiled=True)
-    b, bd, d0, d1, y0, p1 = pl.pallas_call(
+    upper, lower, message = lax.optimization_barrier((upper, lower, message))
+    pieces = [upper] + [shift_z(upper, k) for k in (1, 2, 3)]
+    pieces += [lower] + [shift_x(lower, k) for k in (1, 2, 3)]
+    first_call = pl.pallas_call(
         first_kernel,
         out_shape=(
             shape((4, 8, 512), F32),
             shape((BLOCKS, 4, 128, 128)),
             shape((512, 512)),
             shape((512, 1024)),
+            shape((512, 2048)),
             shape((8, 512)),
             shape((8, 1024)),
         ),
         in_specs=[SMEM, VMEM],
-        out_specs=(VMEM,) * 6,
+        out_specs=(VMEM,) * 7,
         compiler_params=params(),
         name="level0",
-    )(leaf, message)
-    d2, d3 = d23[:, :2048], d23[:, 2048:]
+    )
+    b, bd, d0, d1, d2, y0, p1 = first_call(leaf, message)
 
     def forward(level, part, d, ys):
         own, other = reduce_over(part, level)
@@ -302,7 +330,6 @@
             in_specs=[SMEM] + [VMEM] * (5 + len(ys)),
             out_specs=(VMEM,) * 2,
             compiler_params=params(),
-            name="forward%d" % level,
         )(leaf, own, other, d, b, bd, *ys)
 
     y1, p2 = forward(1, p1, d1, (y0,))
@@ -311,11 +338,11 @@
     xp = pl.pallas_call(
         top_kernel,
         out_shape=shape((8, 4096)),
-        in_specs=[VMEM] * 3,
+        in_specs=[VMEM] * 10,
         out_specs=VMEM,
         compiler_params=params(),
         name="level3",
-    )(own, other, d3)
+    )(own, other, *pieces)
 
     def back(level, part, d, y, pending):
         own, other = reduce_over(part, level + 1)
@@ -328,7 +355,6 @@
             in_specs=[SMEM] + [VMEM] * (5 + len(pending)),
             out_specs=(VMEM,) * len(out),
             compiler_params=params(),
-            name="back%d" % level,
         )(leaf, own, other, d, y, bd, *pending)
 
     x3, xp, *pending = back(2, xp, d2, y2, ())

time: 155 us -> 203 us (1.31)
  waiting for transfers between devices: 42.2 us -> 114 us
  blocking collectives: 56.3 us -> 17.3 us
  starting transfers between devices: 12.8 us -> 41.6 us
  between operations: 13.5 us -> 0.14 us
  local copies, waits for them, and re-layouts: 12.7 us -> 8.66 us
  Pallas kernels: 17.3 us -> 20.6 us
    ppermute x0 -> x12, waiting for transfers between devices: none -> 81.3 us  [the longest x6 60.9 us: shift_z(): lax.ppermute(values, 'tile', [(t, (t + 4 * by) % 16) for t in range(16)])]
    all_to_all x1 -> x0, blocking collectives: 44 us -> none  [local(): message = lax.all_to_all(message, 'tile', 0, 0, tiled=True)]
    ppermute x0 -> x12, starting transfers between devices: none -> 23.8 us  [the longest x6 14.4 us: shift_x(): lax.ppermute(values, 'tile', [(t, t // 4 * 4 + (t + by) % 4) for t in ran...]
    all_gather x1 -> x0, waiting for transfers between devices: 14.5 us -> none  [local(): d23 = lax.all_gather(diag_inverse[:, 1536:], 'tile', axis=0, tiled=True)]
    all_to_all x0 -> x1, starting transfers between devices: none -> 8.05 us  [local(): message = lax.all_to_all(message, 'tile', 0, 0, tiled=True)]
    slice x3 -> x1, local copies, waits for them, and re-layouts: 6.2 us -> 0.02 us  [local(): upper, lower = (diag_inverse[0:16, 3584:], diag_inverse[16:32, 3584:])]
    ppermute x12, waiting for transfers between devices: 21.6 us -> 26.6 us  [reduce_over(): other = lax.ppermute(part, 'leaf', hops[n])]
    all_to_all x1, blocking collectives: 12.4 us -> 17.3 us  [local(): packed = lax.all_to_all(packed, 'tile', 0, 0, tiled=True)]
  transfers between devices with their start and end apart: 14 -> 26, of which waited for: 13 -> 21; matrix products, arithmetic and copies ran while one was open for 3% -> 0% of each run, Pallas kernels for 4% -> 0%
where the time goes in v2:
time: 203 us; the launch traced here: 202 us
  waiting for transfers between devices  114 us (56%)
  starting transfers between devices  41.6 us (20%)
  Pallas kernels  20.6 us (10%)
  blocking collectives  17.3 us (9%)
  local copies, waits for them, and re-layouts  8.66 us (4%)
    ppermute x6, waiting for transfers between devices, shift_z(): lax.ppermute(values, 'tile', [(t, (t + 4 * by) % 16) for t in range(16)])  60.9 us
    ppermute x12, waiting for transfers between devices, reduce_over(): other = lax.ppermute(part, 'leaf', hops[n])  26.6 us
    ppermute x6, waiting for transfers between devices, shift_x(): lax.ppermute(values, 'tile', [(t, t // 4 * 4 + (t + by) % 4) for t in ran...  20.4 us
    all_to_all x1, blocking collectives, local(): packed = lax.all_to_all(packed, 'tile', 0, 0, tiled=True)  17.3 us
    ppermute x6, starting transfers between devices, shift_x(): lax.ppermute(values, 'tile', [(t, t // 4 * 4 + (t + by) % 4) for t in ran...  14.4 us
    ppermute x6, starting transfers between devices, shift_z(): lax.ppermute(values, 'tile', [(t, (t + 4 * by) % 16) for t in range(16)])  9.39 us
    all_to_all x1, starting transfers between devices, local(): message = lax.all_to_all(message, 'tile', 0, 0, tiled=True)  8.05 us
    unnamed x18, local copies, waits for them, and re-layouts  7.91 us
  transfers between devices with their start and end apart: 26, of which 21 were waited for; matrix products, arithmetic and copies ran while one was open for 0% of the time, Pallas kernels for 0%

profile of v2, /device:TPU:0, one launch (start us, length us, event | category | flops | bytes accessed | tf_op | source)
XLA Modules:
  0.0 202.5 jit_solution(16554074608115349503)
XLA Ops:
  0.0 0.9 copy-done.4
  0.9 0.7 copy-done.6
  1.5 1.3 split_couplings.1
  2.8 4.6 %all-to-all-start = ((bf16[8,32,256]{2,1,0:T(8,128)(2,1)}), bf16[8,32,256]{2,1,0:T(8,128)(2,1)S(1)}, u32[]{:S(2)}, u32[]{:S(2)}) async-start(bf16[8,32,256]{2,1,0:T(8,128)(2,1)} %split_couplings.1), calls=%async_computation | async-start | bytes 262144 | tf_op jit(solution)/shard_map/all_to_all | solution.py:287
  7.4 6.1 %all-to-all-done.columns_ref = bf16[8,32,256]{2,1,0:T(8,128)(2,1)S(1)} async-done(((bf16[8,32,256]{2,1,0:T(8,128)(2,1)}), bf16[8,32,256]{2,1,0:T(8,128)(2,1)S(1)}, u32[]{:S(2)}, u32[]{:S(2)}) %all-to-all-start) | async-done | bytes 131104 | tf_op jit(solution)/shard_map/all_to_all | solution.py:287
  13.5 1.0 copy-done.2
  14.6 0.8 copy-done.5
  16.1 2.2 %copy-done.1 = bf16[16,1200,128]{2,1,0:T(8,128)(2,1)} copy-done((bf16[16,1200,128]{2,1,0:T(8,128)(2,1)}, bf16[16,1200,128]{2,1,0:T(8,128)(2,1)S(1)}, u32[]{:S(2)}) %copy-start.1) | copy-done | bytes 4915224
  18.3 8.1 %all-to-all-start.1 = ((bf16[16,1200,128]{2,1,0:T(8,128)(2,1)}), bf16[16,1200,128]{2,1,0:T(8,128)(2,1)}, u32[]{:S(2)}, u32[]{:S(2)}) async-start(bf16[16,1200,128]{2,1,0:T(8,128)(2,1)} %copy-done.1), calls=%async_computation.1 | async-start | bytes 9830400 | tf_op jit(solution)/shard_map/all_to_all | solution.py:303
  26.4 1.9 collective-permute-start.3
  28.4 2.7 %collective-permute-start.4 = (bf16[16,4096]{1,0:T(8,128)(2,1)S(1)}, bf16[16,4096]{1,0:T(8,128)(2,1)S(1)}, u32[]{:S(2)}, u32[]{:S(2)}) collective-permute-start(bf16[16,4096]{1,0:T(8,128)(2,1)S(1)} %get-tuple-element.51), channel_id=1, source_target_pairs={{0,8},{1,9},{2,10},{3,11},{4,12},{5,13},{6,14},{7,15},{8,0},{9,1},... | collective-permute-start | bytes 393224 | tf_op jit(solution)/shard_map/ppermute | solution.py:270
  31.0 1.5 collective-permute-start.5
  32.5 1.5 collective-permute-start
  34.0 2.7 %collective-permute-start.1 = (bf16[16,4096]{1,0:T(8,128)(2,1)S(1)}, bf16[16,4096]{1,0:T(8,128)(2,1)S(1)}, u32[]{:S(2)}, u32[]{:S(2)}) collective-permute-start(bf16[16,4096]{1,0:T(8,128)(2,1)S(1)} %get-tuple-element.52), channel_id=1, source_target_pairs={{0,2},{1,3},{2,0},{3,1},{4,6},{5,7},{6,4},{7,5},{8,10},{9,11},{10,... | collective-permute-start | bytes 393224 | tf_op jit(solution)/shard_map/ppermute | solution.py:266
  36.6 42.5 %collective-permute-done.3 = bf16[16,4096]{1,0:T(8,128)(2,1)S(1)} collective-permute-done((bf16[16,4096]{1,0:T(8,128)(2,1)S(1)}, bf16[16,4096]{1,0:T(8,128)(2,1)S(1)}, u32[]{:S(2)}, u32[]{:S(2)}) %collective-permute-start.3) | collective-permute-done | bytes 131104 | tf_op jit(solution)/shard_map/ppermute | solution.py:270
  79.1 8.6 %collective-permute-start.2 = (bf16[16,4096]{1,0:T(8,128)(2,1)S(1)}, bf16[16,4096]{1,0:T(8,128)(2,1)S(1)}, u32[]{:S(2)}, u32[]{:S(2)}) collective-permute-start(bf16[16,4096]{1,0:T(8,128)(2,1)S(1)} %get-tuple-element.52), channel_id=1, source_target_pairs={{0,3},{1,0},{2,1},{3,2},{4,7},{5,4},{6,5},{7,6},{8,11},{9,8},{10,9... | collective-permute-start | bytes 393224 | tf_op jit(solution)/shard_map/ppermute | solution.py:266
  87.8 7.6 %collective-permute-done = bf16[16,4096]{1,0:T(8,128)(2,1)S(1)} collective-permute-done((bf16[16,4096]{1,0:T(8,128)(2,1)S(1)}, bf16[16,4096]{1,0:T(8,128)(2,1)S(1)}, u32[]{:S(2)}, u32[]{:S(2)}) %collective-permute-start) | collective-permute-done | bytes 131104 | tf_op jit(solution)/shard_map/ppermute | solution.py:266
  95.4 8.7 %collective-permute-done.1 = bf16[16,4096]{1,0:T(8,128)(2,1)S(1)} collective-permute-done((bf16[16,4096]{1,0:T(8,128)(2,1)S(1)}, bf16[16,4096]{1,0:T(8,128)(2,1)S(1)}, u32[]{:S(2)}, u32[]{:S(2)}) %collective-permute-start.1) | collective-permute-done | bytes 131104 | tf_op jit(solution)/shard_map/ppermute | solution.py:266
  104.1 6.7 %level0.1 = (f32[4,8,512]{2,1,0:T(8,128)S(1)}, bf16[34,4,128,128]{3,2,1,0:T(8,128)(2,1)}, bf16[512,512]{1,0:T(8,128)(2,1)S(1)}, bf16[512,1024]{1,0:T(8,128)(2,1)...) custom-call(s32[1]{0:T(128)} %bitcast.leaf_ref, ...), custom_call_target="tpu_custom_call" | custom-call | tf_op jit(solution)/shard_map/level0/pallas_call | solution.py:323
  110.8 1.2 collective-permute-done.6.other_ref
  112.0 2.3 %copy-done = bf16[34,4,128,128]{3,2,1,0:T(8,128)(2,1)S(1)} copy-done((bf16[34,4,128,128]{3,2,1,0:T(8,128)(2,1)S(1)}, bf16[34,4,128,128]{3,2,1,0:T(8,128)(2,1)}, u32[]{:S(2)}) %copy-start) | copy-done | bytes 4456472
  114.3 1.0 shard_map.46
  115.4 1.0 collective-permute-done.7
  116.5 0.7 collective-permute-start.8
  117.1 3.3 %collective-permute-done.8.other_ref = bf16[8,2048]{1,0:T(8,128)(2,1)S(1)} collective-permute-done((bf16[8,2048]{1,0:T(8,128)(2,1)S(1)}, bf16[8,2048]{1,0:T(8,128)(2,1)S(1)}, u32[]{:S(2)}, u32[]{:S(2)}) %collective-permute-start.8) | collective-permute-done | bytes 32800 | tf_op jit(solution)/shard_map/ppermute | solution.py:259
  120.5 4.7 %shard_map.47 = (bf16[8,512]{1,0:T(8,128)(2,1)S(1)}, bf16[8,4096]{1,0:T(8,128)(2,1)S(1)}) custom-call(s32[1]{0:T(128)} %bitcast.leaf_ref, bf16[8,2048]{1,0:T(8,128)(2,1)S(1)} %add_convert_fusion.5.own_ref, bf16[8,2048]{1,0:T(8,128)(2,1)S(1)} %collective-permute-done.8.other_ref, bf16[512,2048]{1,0:T(8,128)(2,1)S(1)} %get-tuple-element.35.d_ref, ...), custom_call_target="tpu_custom_call" | custom-call | tf_op jit(solution)/shard_map/pallas_call | solution.py:327
  125.2 1.3 collective-permute-done.9
  127.3 3.5 %collective-permute-done.10 = bf16[8,4096]{1,0:T(8,128)(2,1)S(1)} collective-permute-done((bf16[8,4096]{1,0:T(8,128)(2,1)S(1)}, bf16[8,4096]{1,0:T(8,128)(2,1)S(1)}, u32[]{:S(2)}, u32[]{:S(2)}) %collective-permute-start.10) | collective-permute-done | bytes 65568 | tf_op jit(solution)/shard_map/ppermute | solution.py:259
  130.9 1.3 collective-permute-start.11
  132.1 3.1 %collective-permute-start.13 = (bf16[64,4096]{1,0:T(8,128)(2,1)S(1)}, bf16[64,4096]{1,0:T(8,128)(2,1)S(1)}, u32[]{:S(2)}, u32[]{:S(2)}) collective-permute-start(bf16[64,4096]{1,0:T(8,128)(2,1)S(1)} %pad_maximum_fusion.rest_0_), channel_id=1, source_target_pairs={{0,8},{1,9},{2,10},{3,11},{4,12},{5,13},{6,14},{7,15},{8,0},{9,1},... | collective-permute-start | bytes 1572872 | tf_op jit(solution)/shard_map/ppermute | solution.py:270
  135.2 1.2 collective-permute-done.11.other_ref
  136.4 0.8 collective-permute-start.16
  137.2 5.5 %collective-permute-done.12.rest_1_ = bf16[64,4096]{1,0:T(8,128)(2,1)S(1)} collective-permute-done((bf16[64,4096]{1,0:T(8,128)(2,1)S(1)}, bf16[64,4096]{1,0:T(8,128)(2,1)S(1)}, u32[]{:S(2)}, u32[]{:S(2)}) %collective-permute-start.12) | collective-permute-done | bytes 524320 | tf_op jit(solution)/shard_map/ppermute | solution.py:270
  142.7 0.9 collective-permute-start.17
  143.6 9.8 %collective-permute-done.13.rest_2_ = bf16[64,4096]{1,0:T(8,128)(2,1)S(1)} collective-permute-done((bf16[64,4096]{1,0:T(8,128)(2,1)S(1)}, bf16[64,4096]{1,0:T(8,128)(2,1)S(1)}, u32[]{:S(2)}, u32[]{:S(2)}) %collective-permute-start.13) | collective-permute-done | bytes 524320 | tf_op jit(solution)/shard_map/ppermute | solution.py:270
  153.4 3.0 %collective-permute-done.14.rest_3_ = bf16[64,4096]{1,0:T(8,128)(2,1)S(1)} collective-permute-done((bf16[64,4096]{1,0:T(8,128)(2,1)S(1)}, bf16[64,4096]{1,0:T(8,128)(2,1)S(1)}, u32[]{:S(2)}, u32[]{:S(2)}) %collective-permute-start.14) | collective-permute-done | bytes 524320 | tf_op jit(solution)/shard_map/ppermute | solution.py:270
  156.5 3.5 %collective-permute-done.15.rest_5_ = bf16[64,4096]{1,0:T(8,128)(2,1)S(1)} collective-permute-done((bf16[64,4096]{1,0:T(8,128)(2,1)S(1)}, bf16[64,4096]{1,0:T(8,128)(2,1)S(1)}, u32[]{:S(2)}, u32[]{:S(2)}) %collective-permute-start.15) | collective-permute-done | bytes 524320 | tf_op jit(solution)/shard_map/ppermute | solution.py:266
  160.6 1.8 level3.1
  162.4 1.3 collective-permute-done.18
  163.8 4.2 %collective-permute-done.19 = bf16[8,4096]{1,0:T(8,128)(2,1)S(1)} collective-permute-done((bf16[8,4096]{1,0:T(8,128)(2,1)S(1)}, bf16[8,4096]{1,0:T(8,128)(2,1)S(1)}, u32[]{:S(2)}, u32[]{:S(2)}) %collective-permute-start.19) | collective-permute-done | bytes 65568 | tf_op jit(solution)/shard_map/ppermute | solution.py:259
  168.0 2.2 %collective-permute-start.20 = (bf16[8,4096]{1,0:T(8,128)(2,1)S(1)}, bf16[8,4096]{1,0:T(8,128)(2,1)S(1)}, u32[]{:S(2)}, u32[]{:S(2)}) collective-permute-start(bf16[8,4096]{1,0:T(8,128)(2,1)S(1)} %add_convert_fusion.own_ref), channel_id=1, source_target_pairs={{0,96},{16,112},{32,64},{48,80},{64,32},{80,48},{96,0},{112,16},{1... | collective-permute-start | bytes 196616 | tf_op jit(solution)/shard_map/ppermute | solution.py:259
  170.2 3.4 %collective-permute-done.20.other_ref = bf16[8,4096]{1,0:T(8,128)(2,1)S(1)} collective-permute-done((bf16[8,4096]{1,0:T(8,128)(2,1)S(1)}, bf16[8,4096]{1,0:T(8,128)(2,1)S(1)}, u32[]{:S(2)}, u32[]{:S(2)}) %collective-permute-start.20) | collective-permute-done | bytes 65568 | tf_op jit(solution)/shard_map/ppermute | solution.py:259
  173.6 3.5 %shard_map.48 = (f32[8,512]{1,0:T(8,128)S(1)}, bf16[8,2048]{1,0:T(8,128)(2,1)S(1)}, f32[8,512]{1,0:T(8,128)S(1)}, f32[8,512]{1,0:T(8,128)S(1)}) custom-call(s32[1]{0:T(128)} %bitcast.leaf_ref, bf16[8,4096]{1,0:T(8,128)(2,1)S(1)} %add_convert_fusion.own_ref, bf16[8,4096]{1,0:T(8,128)(2,1)S(1)} %collective-permute-done.20.other_ref, ...), custom_call_target="tpu_custom_call" | custom-call | tf_op jit(solution)/shard_map/pallas_call | solution.py:352
  177.1 1.2 collective-permute-done.21
  178.4 3.9 %collective-permute-done.22.other_ref = bf16[8,2048]{1,0:T(8,128)(2,1)S(1)} collective-permute-done((bf16[8,2048]{1,0:T(8,128)(2,1)S(1)}, bf16[8,2048]{1,0:T(8,128)(2,1)S(1)}, u32[]{:S(2)}, u32[]{:S(2)}) %collective-permute-start.22) | collective-permute-done | bytes 32800 | tf_op jit(solution)/shard_map/ppermute | solution.py:259
  182.9 1.2 collective-permute-done.23.other_ref
  184.5 17.3 %all_to_all.15 = f32[16,8,128]{2,1,0:T(8,128)S(1)} all-to-all(f32[16,8,128]{2,1,0:T(8,128)S(1)} %pack.1), channel_id=1, replica_groups=mesh['leaf'=8,'tile'=16] {'tile'}, dimensions={0} | all-to-all | bytes 131072 | tf_op jit(solution)/shard_map/all_to_all | solution.py:371
  201.8 0.7 copy.5
  (44 shorter events, 3.8 us)
Async XLA Ops:
  0.0 0.9 copy-start.4
  0.9 0.7 copy-start.6
  2.8 10.7 %all-to-all-start = ((bf16[8,32,256]{2,1,0:T(8,128)(2,1)}), bf16[8,32,256]{2,1,0:T(8,128)(2,1)S(1)}, u32[]{:S(2)}, u32[]{:S(2)}) async-start(bf16[8,32,256]{2,1,0:T(8,128)(2,1)} %split_couplings.1), calls=%async_computation | async-start | bytes 262144 | tf_op jit(solution)/shard_map/all_to_all | solution.py:287
  13.5 1.0 copy-start.2
  14.6 0.8 copy-start.5
  16.1 2.2 %copy-start.1 = (bf16[16,1200,128]{2,1,0:T(8,128)(2,1)}, bf16[16,1200,128]{2,1,0:T(8,128)(2,1)S(1)}, u32[]{:S(2)}) copy-start(bf16[16,1200,128]{2,1,0:T(8,128)(2,1)S(1)} %message.1) | copy-start | bytes 14745604
  18.3 8.1 %copy-start.3 = (bf16[32,7680]{1,0:T(8,128)(2,1)S(1)}, bf16[32,7680]{1,0:T(8,128)(2,1)}, u32[]{:S(2)}) copy-start(bf16[32,7680]{1,0:T(8,128)(2,1)} %diag_ref.1) | copy-start | bytes 1474564
  18.3 85.8 %all-to-all-start.1 = ((bf16[16,1200,128]{2,1,0:T(8,128)(2,1)}), bf16[16,1200,128]{2,1,0:T(8,128)(2,1)}, u32[]{:S(2)}, u32[]{:S(2)}) async-start(bf16[16,1200,128]{2,1,0:T(8,128)(2,1)} %copy-done.1), calls=%async_computation.1 | async-start | bytes 9830400 | tf_op jit(solution)/shard_map/all_to_all | solution.py:303
  26.4 52.7 %collective-permute-start.3 = (bf16[16,4096]{1,0:T(8,128)(2,1)S(1)}, bf16[16,4096]{1,0:T(8,128)(2,1)S(1)}, u32[]{:S(2)}, u32[]{:S(2)}) collective-permute-start(bf16[16,4096]{1,0:T(8,128)(2,1)S(1)} %get-tuple-element.51), channel_id=1, source_target_pairs={{0,4},{1,5},{2,6},{3,7},{4,8},{5,9},{6,10},{7,11},{8,12},{9,13},{1... | collective-permute-start | bytes 393224 | tf_op jit(solution)/shard_map/ppermute | solution.py:270
  28.4 59.4 %collective-permute-start.4 = (bf16[16,4096]{1,0:T(8,128)(2,1)S(1)}, bf16[16,4096]{1,0:T(8,128)(2,1)S(1)}, u32[]{:S(2)}, u32[]{:S(2)}) collective-permute-start(bf16[16,4096]{1,0:T(8,128)(2,1)S(1)} %get-tuple-element.51), channel_id=1, source_target_pairs={{0,8},{1,9},{2,10},{3,11},{4,12},{5,13},{6,14},{7,15},{8,0},{9,1},... | collective-permute-start | bytes 393224 | tf_op jit(solution)/shard_map/ppermute | solution.py:270
  31.0 56.7 %collective-permute-start.5 = (bf16[16,4096]{1,0:T(8,128)(2,1)S(1)}, bf16[16,4096]{1,0:T(8,128)(2,1)S(1)}, u32[]{:S(2)}, u32[]{:S(2)}) collective-permute-start(bf16[16,4096]{1,0:T(8,128)(2,1)S(1)} %get-tuple-element.51), channel_id=1, source_target_pairs={{0,12},{1,13},{2,14},{3,15},{4,0},{5,1},{6,2},{7,3},{8,4},{9,5},{1... | collective-permute-start | bytes 393224 | tf_op jit(solution)/shard_map/ppermute | solution.py:270
  32.5 62.9 %collective-permute-start = (bf16[16,4096]{1,0:T(8,128)(2,1)S(1)}, bf16[16,4096]{1,0:T(8,128)(2,1)S(1)}, u32[]{:S(2)}, u32[]{:S(2)}) collective-permute-start(bf16[16,4096]{1,0:T(8,128)(2,1)S(1)} %get-tuple-element.52), channel_id=1, source_target_pairs={{0,1},{1,2},{2,3},{3,0},{4,5},{5,6},{6,7},{7,4},{8,9},{9,10},{10,1... | collective-permute-start | bytes 393224 | tf_op jit(solution)/shard_map/ppermute | solution.py:266
  34.0 70.1 %collective-permute-start.1 = (bf16[16,4096]{1,0:T(8,128)(2,1)S(1)}, bf16[16,4096]{1,0:T(8,128)(2,1)S(1)}, u32[]{:S(2)}, u32[]{:S(2)}) collective-permute-start(bf16[16,4096]{1,0:T(8,128)(2,1)S(1)} %get-tuple-element.52), channel_id=1, source_target_pairs={{0,2},{1,3},{2,0},{3,1},{4,6},{5,7},{6,4},{7,5},{8,10},{9,11},{10,... | collective-permute-start | bytes 393224 | tf_op jit(solution)/shard_map/ppermute | solution.py:266
  79.1 24.9 %collective-permute-start.2 = (bf16[16,4096]{1,0:T(8,128)(2,1)S(1)}, bf16[16,4096]{1,0:T(8,128)(2,1)S(1)}, u32[]{:S(2)}, u32[]{:S(2)}) collective-permute-start(bf16[16,4096]{1,0:T(8,128)(2,1)S(1)} %get-tuple-element.52), channel_id=1, source_target_pairs={{0,3},{1,0},{2,1},{3,2},{4,7},{5,4},{6,5},{7,6},{8,11},{9,8},{10,9... | collective-permute-start | bytes 393224 | tf_op jit(solution)/shard_map/ppermute | solution.py:266
  110.8 1.2 collective-permute-start.6
  112.0 2.3 %copy-start = (bf16[34,4,128,128]{3,2,1,0:T(8,128)(2,1)S(1)}, bf16[34,4,128,128]{3,2,1,0:T(8,128)(2,1)}, u32[]{:S(2)}) copy-start(bf16[34,4,128,128]{3,2,1,0:T(8,128)(2,1)} %get-tuple-element.32.bd_ref) | copy-start | bytes 13369348
  115.3 1.2 collective-permute-start.7
  116.5 4.0 %collective-permute-start.8 = (bf16[8,2048]{1,0:T(8,128)(2,1)S(1)}, bf16[8,2048]{1,0:T(8,128)(2,1)S(1)}, u32[]{:S(2)}, u32[]{:S(2)}) collective-permute-start(bf16[8,2048]{1,0:T(8,128)(2,1)S(1)} %add_convert_fusion.5.own_ref), channel_id=1, source_target_pairs={{0,32},{16,48},{32,0},{48,16},{64,96},{80,112},{96,64},{112,80},{1... | collective-permute-start | bytes 98312 | tf_op jit(solution)/shard_map/ppermute | solution.py:259
  120.5 61.8 %slice-start = ((s8[4456448]{0:T(1024)(128)(4,1)}), s8[4194304]{0:T(1024)(128)(4,1)S(1)}, s32[]{:S(2)}) async-start(s8[4456448]{0:T(1024)(128)(4,1)} %bitcast.5), calls=%async_computation.3 | async-start | bytes 8388608
  125.2 1.3 collective-permute-start.9
  126.5 4.3 %collective-permute-start.10 = (bf16[8,4096]{1,0:T(8,128)(2,1)S(1)}, bf16[8,4096]{1,0:T(8,128)(2,1)S(1)}, u32[]{:S(2)}, u32[]{:S(2)}) collective-permute-start(bf16[8,4096]{1,0:T(8,128)(2,1)S(1)} %add_convert_fusion.3), channel_id=1, source_target_pairs={{0,32},{16,48},{32,0},{48,16},{64,96},{80,112},{96,64},{112,80},{1... | collective-permute-start | bytes 196616 | tf_op jit(solution)/shard_map/ppermute | solution.py:259
  127.1 15.6 %collective-permute-start.12 = (bf16[64,4096]{1,0:T(8,128)(2,1)S(1)}, bf16[64,4096]{1,0:T(8,128)(2,1)S(1)}, u32[]{:S(2)}, u32[]{:S(2)}) collective-permute-start(bf16[64,4096]{1,0:T(8,128)(2,1)S(1)} %pad_maximum_fusion.rest_0_), channel_id=1, source_target_pairs={{0,4},{1,5},{2,6},{3,7},{4,8},{5,9},{6,10},{7,11},{8,12},{9,13},{1... | collective-permute-start | bytes 1572872 | tf_op jit(solution)/shard_map/ppermute | solution.py:270
  130.8 51.5 %slice-start.1 = ((s8[4456448]{0:T(1024)(128)(4,1)}), s8[262144]{0:T(1024)(128)(4,1)S(1)}, s32[]{:S(2)}) async-start(s8[4456448]{0:T(1024)(128)(4,1)} %bitcast.5), calls=%async_computation.4 | async-start | bytes 524288
  130.9 5.6 %collective-permute-start.11 = (bf16[8,4096]{1,0:T(8,128)(2,1)S(1)}, bf16[8,4096]{1,0:T(8,128)(2,1)S(1)}, u32[]{:S(2)}, u32[]{:S(2)}) collective-permute-start(bf16[8,4096]{1,0:T(8,128)(2,1)S(1)} %add_convert_fusion.2.own_ref), channel_id=1, source_target_pairs={{0,96},{16,112},{32,64},{48,80},{64,32},{80,48},{96,0},{112,16},{1... | collective-permute-start | bytes 196616 | tf_op jit(solution)/shard_map/ppermute | solution.py:259
  132.1 21.3 %collective-permute-start.13 = (bf16[64,4096]{1,0:T(8,128)(2,1)S(1)}, bf16[64,4096]{1,0:T(8,128)(2,1)S(1)}, u32[]{:S(2)}, u32[]{:S(2)}) collective-permute-start(bf16[64,4096]{1,0:T(8,128)(2,1)S(1)} %pad_maximum_fusion.rest_0_), channel_id=1, source_target_pairs={{0,8},{1,9},{2,10},{3,11},{4,12},{5,13},{6,14},{7,15},{8,0},{9,1},... | collective-permute-start | bytes 1572872 | tf_op jit(solution)/shard_map/ppermute | solution.py:270
  135.2 21.3 %collective-permute-start.14 = (bf16[64,4096]{1,0:T(8,128)(2,1)S(1)}, bf16[64,4096]{1,0:T(8,128)(2,1)S(1)}, u32[]{:S(2)}, u32[]{:S(2)}) collective-permute-start(bf16[64,4096]{1,0:T(8,128)(2,1)S(1)} %pad_maximum_fusion.rest_0_), channel_id=1, source_target_pairs={{0,12},{1,13},{2,14},{3,15},{4,0},{5,1},{6,2},{7,3},{8,4},{9,5},{1... | collective-permute-start | bytes 1572872 | tf_op jit(solution)/shard_map/ppermute | solution.py:270
  135.2 24.7 %collective-permute-start.15 = (bf16[64,4096]{1,0:T(8,128)(2,1)S(1)}, bf16[64,4096]{1,0:T(8,128)(2,1)S(1)}, u32[]{:S(2)}, u32[]{:S(2)}) collective-permute-start(bf16[64,4096]{1,0:T(8,128)(2,1)S(1)} %pad_maximum_fusion.1.rest_4_), channel_id=1, source_target_pairs={{0,1},{1,2},{2,3},{3,0},{4,5},{5,6},{6,7},{7,4},{8,9},{9,10},{10,1... | collective-permute-start | bytes 1572872 | tf_op jit(solution)/shard_map/ppermute | solution.py:266
  136.4 23.5 %collective-permute-start.16 = (bf16[64,4096]{1,0:T(8,128)(2,1)S(1)}, bf16[64,4096]{1,0:T(8,128)(2,1)S(1)}, u32[]{:S(2)}, u32[]{:S(2)}) collective-permute-start(bf16[64,4096]{1,0:T(8,128)(2,1)S(1)} %pad_maximum_fusion.1.rest_4_), channel_id=1, source_target_pairs={{0,2},{1,3},{2,0},{3,1},{4,6},{5,7},{6,4},{7,5},{8,10},{9,11},{10,... | collective-permute-start | bytes 1572872 | tf_op jit(solution)/shard_map/ppermute | solution.py:266
  142.7 17.8 %collective-permute-start.17 = (bf16[64,4096]{1,0:T(8,128)(2,1)S(1)}, bf16[64,4096]{1,0:T(8,128)(2,1)S(1)}, u32[]{:S(2)}, u32[]{:S(2)}) collective-permute-start(bf16[64,4096]{1,0:T(8,128)(2,1)S(1)} %pad_maximum_fusion.1.rest_4_), channel_id=1, source_target_pairs={{0,3},{1,0},{2,1},{3,2},{4,7},{5,4},{6,5},{7,6},{8,11},{9,8},{10,9... | collective-permute-start | bytes 1572872 | tf_op jit(solution)/shard_map/ppermute | solution.py:266
  162.4 1.3 collective-permute-start.18
  163.7 4.3 %collective-permute-start.19 = (bf16[8,4096]{1,0:T(8,128)(2,1)S(1)}, bf16[8,4096]{1,0:T(8,128)(2,1)S(1)}, u32[]{:S(2)}, u32[]{:S(2)}) collective-permute-start(bf16[8,4096]{1,0:T(8,128)(2,1)S(1)} %add_convert_fusion.1), channel_id=1, source_target_pairs={{0,32},{16,48},{32,0},{48,16},{64,96},{80,112},{96,64},{112,80},{1... | collective-permute-start | bytes 196616 | tf_op jit(solution)/shard_map/ppermute | solution.py:259
  168.0 5.6 %collective-permute-start.20 = (bf16[8,4096]{1,0:T(8,128)(2,1)S(1)}, bf16[8,4096]{1,0:T(8,128)(2,1)S(1)}, u32[]{:S(2)}, u32[]{:S(2)}) collective-permute-start(bf16[8,4096]{1,0:T(8,128)(2,1)S(1)} %add_convert_fusion.own_ref), channel_id=1, source_target_pairs={{0,96},{16,112},{32,64},{48,80},{64,32},{80,48},{96,0},{112,16},{1... | collective-permute-start | bytes 196616 | tf_op jit(solution)/shard_map/ppermute | solution.py:259
  177.1 1.2 collective-permute-start.21
  178.3 4.0 %collective-permute-start.22 = (bf16[8,2048]{1,0:T(8,128)(2,1)S(1)}, bf16[8,2048]{1,0:T(8,128)(2,1)S(1)}, u32[]{:S(2)}, u32[]{:S(2)}) collective-permute-start(bf16[8,2048]{1,0:T(8,128)(2,1)S(1)} %add_convert_fusion.4.own_ref), channel_id=1, source_target_pairs={{0,32},{16,48},{32,0},{48,16},{64,96},{80,112},{96,64},{112,80},{1... | collective-permute-start | bytes 98312 | tf_op jit(solution)/shard_map/ppermute | solution.py:259
  182.9 1.2 collective-permute-start.23

commit v3 on v2

--- a/solution.py
+++ b/solution.py
@@ -15,12 +15,11 @@
 BLOCKS = 34
 VMEM = pl.BlockSpec(memory_space=pltpu.VMEM)
 SMEM = pl.BlockSpec(memory_space=pltpu.SMEM)
-RHS_ROWS, C_TILES, D0_TILES, D1_TILES, D2_TILES = 16, 9, 4, 8, 16
+RHS_ROWS, C_TILES, D0_TILES, D1_TILES = 16, 9, 4, 8
 C_AT = RHS_ROWS
 D0_AT = C_AT + 32 * C_TILES
 D1_AT = D0_AT + 32 * D0_TILES
-D2_AT = D1_AT + 32 * D1_TILES
-MESSAGE = D2_AT + 32 * D2_TILES
+MESSAGE = D1_AT + 32 * D1_TILES
 
 
 def params(mib=48):
@@ -102,7 +101,7 @@
                 shift = (c - q) % 4 * 32
                 parts.append(values if shift == 0 else pltpu.roll(values, shift, 1))
         common.append(merge(parts, chunk).astype(BF))
-    for tile in range(D0_TILES + D1_TILES + D2_TILES):
+    for tile in range(D0_TILES + D1_TILES):
         common.append(diag_ref[:, 128 * tile : 128 * tile + 128])
     rhs = jnp.transpose(rhs_ref[...].reshape(128, 128))
     high = rhs.astype(BF).astype(F32)
@@ -125,7 +124,7 @@
     return jnp.concatenate(out, 1)
 
 
-def first_kernel(leaf_ref, msg_ref, b_ref, bd_ref, d0_ref, d1_ref, d2_ref, y0_ref, p1_ref):
+def first_kernel(leaf_ref, msg_ref, b_ref, bd_ref, d0_ref, d1_ref, y0_ref, p1_ref):
     leaf = leaf_ref[0]
     chunk8 = lane_chunk(8)
     rhs = Rolled(
@@ -151,7 +150,6 @@
     for ref, first, tiles in (
         (d0_ref, D0_AT, D0_TILES),
         (d1_ref, D1_AT, D1_TILES),
-        (d2_ref, D2_AT, D2_TILES),
     ):
         for tile in range(tiles):
             at = first + 32 * tile
@@ -168,6 +166,18 @@
     for at in range(0, width, 1024):
         total = total + dot_nt(z[:, at : at + 1024], d_ref[:, at : at + 1024])
     return total
+
+
+def order_kernel(place_ref, *rest):
+    pieces, d_ref = rest[:-1], rest[-1]
+    z, x = place_ref[0] // 4, place_ref[0] % 4
+    for half in range(2):
+        for n in range(4):
+            for m in range(4):
+                dz, dx = (n, m) if half == 0 else (m, n)
+                tile = (z - dz + 4) % 4 * 4 + (x - dx + 4) % 4
+                at = pl.multiple_of(tile * 32 + 16 * half, 16)
+                d_ref[pl.ds(at, 16), :] = pieces[4 * half + n][16 * m : 16 * m + 16, :]
 
 
 def forward_kernel(level, leaf_ref, own_ref, other_ref, d_ref, b_ref, bd_ref, *rest):
@@ -272,10 +282,19 @@
 
 def local(right_sides, diag_inverse, coupling, pattern):
     leaf = lax.axis_index("leaf").astype(jnp.int32).reshape(1)
-    upper, lower = diag_inverse[0:16, 3584:], diag_inverse[16:32, 3584:]
+    upper, lower = diag_inverse[0:16, 1536:], diag_inverse[16:32, 1536:]
     upper = [upper] + [shift_x(upper, k) for k in (1, 2, 3)]
     lower = [lower] + [shift_z(lower, k) for k in (1, 2, 3)]
-    upper, lower = jnp.concatenate(upper, 0), jnp.concatenate(lower, 0)
+
+    def joined(parts, first, stop):
+        return jnp.concatenate([p[:, first:stop] for p in parts], 0)
+
+    def far(upper, lower):
+        pieces = [upper] + [shift_z(upper, k) for k in (1, 2, 3)]
+        return pieces + [lower] + [shift_x(lower, k) for k in (1, 2, 3)]
+
+    pieces2 = far(joined(upper, 0, 2048), joined(lower, 0, 2048))
+    upper, lower = joined(upper, 2048, 6144), joined(lower, 2048, 6144)
     split = pl.pallas_call(
         split_kernel,
         out_shape=shape((8, 32, 256)),
@@ -293,7 +312,7 @@
             SMEM,
             pl.BlockSpec((8, 32, 256), lambda i: (0, 0, 0)),
             pl.BlockSpec((4, 32, 128), lambda i: (0, 0, 0)),
-            pl.BlockSpec((32, 3584), lambda i: (0, 0)),
+            pl.BlockSpec((32, 1536), lambda i: (0, 0)),
         ],
         out_specs=pl.BlockSpec((16, MESSAGE, 128), lambda i: (0, 0, 0)),
         compiler_params=params(),
@@ -302,8 +321,7 @@
     message = message_call(leaf, columns, right_sides, diag_inverse)
     message = lax.all_to_all(message, "tile", 0, 0, tiled=True)
     upper, lower, message = lax.optimization_barrier((upper, lower, message))
-    pieces = [upper] + [shift_z(upper, k) for k in (1, 2, 3)]
-    pieces += [lower] + [shift_x(lower, k) for k in (1, 2, 3)]
+    pieces3 = far(upper, lower)
     first_call = pl.pallas_call(
         first_kernel,
         out_shape=(
@@ -311,16 +329,26 @@
             shape((BLOCKS, 4, 128, 128)),
             shape((512, 512)),
             shape((512, 1024)),
-            shape((512, 2048)),
             shape((8, 512)),
             shape((8, 1024)),
         ),
         in_specs=[SMEM, VMEM],
-        out_specs=(VMEM,) * 7,
+        out_specs=(VMEM,) * 6,
         compiler_params=params(),
         name="level0",
     )
-    b, bd, d0, d1, d2, y0, p1 = first_call(leaf, message)
+    b, bd, d0, d1, y0, p1 = first_call(leaf, message)
+
+    place = lax.axis_index("tile").astype(jnp.int32).reshape(1)
+    order_call = pl.pallas_call(
+        order_kernel,
+        out_shape=shape((512, 2048)),
+        in_specs=[SMEM] + [VMEM] * 8,
+        out_specs=VMEM,
+        compiler_params=params(),
+        name="order2",
+    )
+    d2 = order_call(place, *pieces2)
 
     def forward(level, part, d, ys):
         own, other = reduce_over(part, level)
@@ -342,7 +370,7 @@
         out_specs=VMEM,
         compiler_params=params(),
         name="level3",
-    )(own, other, *pieces)
+    )(own, other, *pieces3)
 
     def back(level, part, d, y, pending):
         own, other = reduce_over(part, level + 1)

time: 203 us -> 190 us (0.936)
  waiting for transfers between devices: 114 us -> 94 us
  starting transfers between devices: 41.6 us -> 53.4 us
  blocking collectives: 17.3 us -> 11.9 us
    ppermute x6 -> x9, waiting for transfers between devices: 60.9 us -> 13.4 us  [shift_z(): lax.ppermute(values, 'tile', [(t, (t + 4 * by) % 16) for t in range(16)])]
    ppermute x6 -> x9, waiting for transfers between devices: 20.4 us -> 53.7 us  [shift_x(): lax.ppermute(values, 'tile', [(t, t // 4 * 4 + (t + by) % 4) for t in ran...]
    ppermute x6 -> x9, starting transfers between devices: 14.4 us -> 24.2 us  [shift_x(): lax.ppermute(values, 'tile', [(t, t // 4 * 4 + (t + by) % 4) for t in ran...]
    ppermute x12, waiting for transfers between devices: 26.6 us -> 20.8 us  [reduce_over(): other = lax.ppermute(part, 'leaf', hops[n])]
    all_to_all x1, blocking collectives: 17.3 us -> 11.9 us  [local(): packed = lax.all_to_all(packed, 'tile', 0, 0, tiled=True)]
    pallas_call x1 -> x2, Pallas kernels: 6.69 us -> 4.89 us  [the longest x1 3.7 us: local(): b, bd, d0, d1, y0, p1 = first_call(leaf, message)]
    ppermute x6 -> x9, starting transfers between devices: 9.39 us -> 10.7 us  [shift_z(): lax.ppermute(values, 'tile', [(t, (t + 4 * by) % 16) for t in range(16)])]
    unnamed x18 -> x34, local copies, waits for them, and re-layouts: 7.91 us -> 8.78 us
  transfers between devices with their start and end apart: 26 -> 32, of which waited for: 21 -> 19; matrix products, arithmetic and copies ran while one was open for 0% -> 1% of each run, Pallas kernels for 0% -> 3%
where the time goes in v3:
time: 190 us
  waiting for transfers between devices  94 us (49%)
  starting transfers between devices  53.4 us (28%)
  Pallas kernels  18.6 us (10%)
  blocking collectives  11.9 us (6%)
  local copies, waits for them, and re-layouts  9.66 us (5%)
    ppermute x9, waiting for transfers between devices, shift_x(): lax.ppermute(values, 'tile', [(t, t // 4 * 4 + (t + by) % 4) for t in ran...  53.7 us
    ppermute x9, starting transfers between devices, shift_x(): lax.ppermute(values, 'tile', [(t, t // 4 * 4 + (t + by) % 4) for t in ran...  24.2 us
    ppermute x12, waiting for transfers between devices, reduce_over(): other = lax.ppermute(part, 'leaf', hops[n])  20.8 us
    ppermute x9, waiting for transfers between devices, shift_z(): lax.ppermute(values, 'tile', [(t, (t + 4 * by) % 16) for t in range(16)])  13.4 us
    all_to_all x1, blocking collectives, local(): packed = lax.all_to_all(packed, 'tile', 0, 0, tiled=True)  11.9 us
    ppermute x9, starting transfers between devices, shift_z(): lax.ppermute(values, 'tile', [(t, (t + 4 * by) % 16) for t in range(16)])  10.7 us
    unnamed x34, local copies, waits for them, and re-layouts  8.78 us
    all_to_all x1, starting transfers between devices, local(): message = lax.all_to_all(message, 'tile', 0, 0, tiled=True)  8.01 us
  transfers between devices with their start and end apart: 32, of which 19 were waited for; matrix products, arithmetic and copies ran while one was open for 1% of the time, Pallas kernels for 3%

profile of v3, /device:TPU:0, one launch (start us, length us, event | category | flops | bytes accessed | tf_op | source)
XLA Modules:
  0.0 189.7 jit_solution(16436896736278586081)
XLA Ops:
  0.0 0.9 copy-done.9
  1.5 1.3 split_couplings.1
  2.9 4.6 %all-to-all-start = ((bf16[8,32,256]{2,1,0:T(8,128)(2,1)}), bf16[8,32,256]{2,1,0:T(8,128)(2,1)S(1)}, u32[]{:S(2)}, u32[]{:S(2)}) async-start(bf16[8,32,256]{2,1,0:T(8,128)(2,1)} %split_couplings.1), calls=%async_computation | async-start | bytes 262144 | tf_op jit(solution)/shard_map/all_to_all | solution.py:306
  7.4 6.1 %all-to-all-done.columns_ref = bf16[8,32,256]{2,1,0:T(8,128)(2,1)S(1)} async-done(((bf16[8,32,256]{2,1,0:T(8,128)(2,1)}), bf16[8,32,256]{2,1,0:T(8,128)(2,1)S(1)}, u32[]{:S(2)}, u32[]{:S(2)}) %all-to-all-start) | async-done | bytes 131104 | tf_op jit(solution)/shard_map/all_to_all | solution.py:306
  13.5 1.0 copy-done.4
  14.6 0.8 copy-done.10
  15.8 1.5 copy-done.1
  17.3 8.0 %all-to-all-start.1 = ((bf16[16,688,128]{2,1,0:T(8,128)(2,1)}), bf16[16,688,128]{2,1,0:T(8,128)(2,1)S(1)}, u32[]{:S(2)}, u32[]{:S(2)}) async-start(bf16[16,688,128]{2,1,0:T(8,128)(2,1)} %copy-done.1), calls=%async_computation.1 | async-start | bytes 5636096 | tf_op jit(solution)/shard_map/all_to_all | solution.py:322
  25.4 2.0 %collective-permute-start.3 = (bf16[16,6144]{1,0:T(8,128)(2,1)S(1)}, bf16[16,6144]{1,0:T(8,128)(2,1)S(1)}, u32[]{:S(2)}, u32[]{:S(2)}) collective-permute-start(bf16[16,6144]{1,0:T(8,128)(2,1)S(1)} %get-tuple-element.53), channel_id=1, source_target_pairs={{0,4},{1,5},{2,6},{3,7},{4,8},{5,9},{6,10},{7,11},{8,12},{9,13},{1... | collective-permute-start | bytes 589832 | tf_op jit(solution)/shard_map/ppermute | solution.py:280
  27.4 2.7 %collective-permute-start.4 = (bf16[16,6144]{1,0:T(8,128)(2,1)S(1)}, bf16[16,6144]{1,0:T(8,128)(2,1)S(1)}, u32[]{:S(2)}, u32[]{:S(2)}) collective-permute-start(bf16[16,6144]{1,0:T(8,128)(2,1)S(1)} %get-tuple-element.53), channel_id=1, source_target_pairs={{0,8},{1,9},{2,10},{3,11},{4,12},{5,13},{6,14},{7,15},{8,0},{9,1},... | collective-permute-start | bytes 589832 | tf_op jit(solution)/shard_map/ppermute | solution.py:280
  30.0 1.5 collective-permute-start
  31.5 2.7 %collective-permute-start.1 = (bf16[16,6144]{1,0:T(8,128)(2,1)S(1)}, bf16[16,6144]{1,0:T(8,128)(2,1)S(1)}, u32[]{:S(2)}, u32[]{:S(2)}) collective-permute-start(bf16[16,6144]{1,0:T(8,128)(2,1)S(1)} %get-tuple-element.54), channel_id=1, source_target_pairs={{0,2},{1,3},{2,0},{3,1},{4,6},{5,7},{6,4},{7,5},{8,10},{9,11},{10,... | collective-permute-start | bytes 589832 | tf_op jit(solution)/shard_map/ppermute | solution.py:276
  34.2 1.5 collective-permute-start.2
  35.7 31.4 %collective-permute-done = bf16[16,6144]{1,0:T(8,128)(2,1)S(1)} collective-permute-done((bf16[16,6144]{1,0:T(8,128)(2,1)S(1)}, bf16[16,6144]{1,0:T(8,128)(2,1)S(1)}, u32[]{:S(2)}, u32[]{:S(2)}) %collective-permute-start) | collective-permute-done | bytes 196640 | tf_op jit(solution)/shard_map/ppermute | solution.py:276
  67.1 1.4 collective-permute-start.5
  68.5 5.9 %collective-permute-done.1 = bf16[16,6144]{1,0:T(8,128)(2,1)S(1)} collective-permute-done((bf16[16,6144]{1,0:T(8,128)(2,1)S(1)}, bf16[16,6144]{1,0:T(8,128)(2,1)S(1)}, u32[]{:S(2)}, u32[]{:S(2)}) %collective-permute-start.1) | collective-permute-done | bytes 196640 | tf_op jit(solution)/shard_map/ppermute | solution.py:276
  75.2 3.1 %collective-permute-start.10 = (bf16[64,2048]{1,0:T(8,128)(2,1)}, bf16[64,2048]{1,0:T(8,128)(2,1)}, u32[]{:S(2)}, u32[]{:S(2)}) collective-permute-start(bf16[64,2048]{1,0:T(8,128)(2,1)} %pad_maximum_fusion.2.rest_0_), channel_id=1, source_target_pairs={{0,8},{1,9},{2,10},{3,11},{4,12},{5,13},{6,14},{7,15},{8,0},{9,1},... | collective-permute-start | bytes 786440 | tf_op jit(solution)/shard_map/ppermute | solution.py:280
  80.1 3.7 %level0.1 = (f32[4,8,512]{2,1,0:T(8,128)S(1)}, bf16[34,4,128,128]{3,2,1,0:T(8,128)(2,1)}, bf16[512,512]{1,0:T(8,128)(2,1)S(1)}, bf16[512,1024]{1,0:T(8,128)(2,1)...) custom-call(s32[1]{0:T(128)} %bitcast.leaf_ref, bf16[16,688,128]{2,1,0:T(8,128)(2,1)S(1)} %all-to-all-done.1.msg_ref), custom_call_target="tpu_custom_call" | custom-call | tf_op jit(solution)/shard_map/level0/pallas_call | solution.py:340
  84.9 0.9 collective-permute-done.6.other_ref
  85.8 2.3 %copy-done = bf16[34,4,128,128]{3,2,1,0:T(8,128)(2,1)S(1)} copy-done((bf16[34,4,128,128]{3,2,1,0:T(8,128)(2,1)S(1)}, bf16[34,4,128,128]{3,2,1,0:T(8,128)(2,1)}, u32[]{:S(2)}) %copy-start) | copy-done | bytes 4456472
  88.0 1.0 shard_map.46
  89.3 7.2 %collective-permute-start.12 = (bf16[64,2048]{1,0:T(8,128)(2,1)S(1)}, bf16[64,2048]{1,0:T(8,128)(2,1)S(1)}, u32[]{:S(2)}, u32[]{:S(2)}) collective-permute-start(bf16[64,2048]{1,0:T(8,128)(2,1)S(1)} %pad_maximum_fusion.3.rest_4_), channel_id=1, source_target_pairs={{0,1},{1,2},{2,3},{3,0},{4,5},{5,6},{6,7},{7,4},{8,9},{9,10},{10,1... | collective-permute-start | bytes 786440 | tf_op jit(solution)/shard_map/ppermute | solution.py:276
  97.1 2.1 %collective-permute-start.14 = (bf16[64,2048]{1,0:T(8,128)(2,1)S(1)}, bf16[64,2048]{1,0:T(8,128)(2,1)S(1)}, u32[]{:S(2)}, u32[]{:S(2)}) collective-permute-start(bf16[64,2048]{1,0:T(8,128)(2,1)S(1)} %pad_maximum_fusion.3.rest_4_), channel_id=1, source_target_pairs={{0,3},{1,0},{2,1},{3,2},{4,7},{5,4},{6,5},{7,6},{8,11},{9,8},{10,9... | collective-permute-start | bytes 786440 | tf_op jit(solution)/shard_map/ppermute | solution.py:276
  99.9 3.2 %collective-permute-done.12.rest_5_ = bf16[64,2048]{1,0:T(8,128)(2,1)S(1)} collective-permute-done((bf16[64,2048]{1,0:T(8,128)(2,1)S(1)}, bf16[64,2048]{1,0:T(8,128)(2,1)S(1)}, u32[]{:S(2)}, u32[]{:S(2)}) %collective-permute-start.12) | collective-permute-done | bytes 262176 | tf_op jit(solution)/shard_map/ppermute | solution.py:276
  103.1 6.0 %collective-permute-done.13.rest_6_ = bf16[64,2048]{1,0:T(8,128)(2,1)S(1)} collective-permute-done((bf16[64,2048]{1,0:T(8,128)(2,1)S(1)}, bf16[64,2048]{1,0:T(8,128)(2,1)S(1)}, u32[]{:S(2)}, u32[]{:S(2)}) %collective-permute-start.13) | collective-permute-done | bytes 262176 | tf_op jit(solution)/shard_map/ppermute | solution.py:276
  109.2 1.2 order2.1.d_ref
  110.4 4.7 %shard_map.47 = (bf16[8,512]{1,0:T(8,128)(2,1)S(1)}, bf16[8,4096]{1,0:T(8,128)(2,1)S(1)}) custom-call(s32[1]{0:T(128)} %bitcast.leaf_ref, bf16[8,2048]{1,0:T(8,128)(2,1)S(1)} %add_convert_fusion.5.own_ref, bf16[8,2048]{1,0:T(8,128)(2,1)S(1)} %collective-permute-done.8.other_ref, bf16[512,2048]{1,0:T(8,128)(2,1)S(1)} %order2.1.d_ref, ...), custom_call_target="tpu_custom_call" | custom-call | tf_op jit(solution)/shard_map/pallas_call | solution.py:355
  115.1 1.3 collective-permute-done.15
  117.0 3.7 %collective-permute-done.16 = bf16[8,4096]{1,0:T(8,128)(2,1)S(1)} collective-permute-done((bf16[8,4096]{1,0:T(8,128)(2,1)S(1)}, bf16[8,4096]{1,0:T(8,128)(2,1)S(1)}, u32[]{:S(2)}, u32[]{:S(2)}) %collective-permute-start.16) | collective-permute-done | bytes 65568 | tf_op jit(solution)/shard_map/ppermute | solution.py:269
  120.8 1.2 collective-permute-start.17
  122.0 1.2 collective-permute-start.20
  123.2 2.6 %collective-permute-start.21 = (bf16[64,4096]{1,0:T(8,128)(2,1)S(1)}, bf16[64,4096]{1,0:T(8,128)(2,1)S(1)}, u32[]{:S(2)}, u32[]{:S(2)}) collective-permute-start(bf16[64,4096]{1,0:T(8,128)(2,1)S(1)} %pad_maximum_fusion.1.rest_4_), channel_id=1, source_target_pairs={{0,1},{1,2},{2,3},{3,0},{4,5},{5,6},{6,7},{7,4},{8,9},{9,10},{10,1... | collective-permute-start | bytes 1572872 | tf_op jit(solution)/shard_map/ppermute | solution.py:276
  126.3 3.6 %collective-permute-start.22 = (bf16[64,4096]{1,0:T(8,128)(2,1)S(1)}, bf16[64,4096]{1,0:T(8,128)(2,1)S(1)}, u32[]{:S(2)}, u32[]{:S(2)}) collective-permute-start(bf16[64,4096]{1,0:T(8,128)(2,1)S(1)} %pad_maximum_fusion.1.rest_4_), channel_id=1, source_target_pairs={{0,2},{1,3},{2,0},{3,1},{4,6},{5,7},{6,4},{7,5},{8,10},{9,11},{10,... | collective-permute-start | bytes 1572872 | tf_op jit(solution)/shard_map/ppermute | solution.py:276
  130.0 13.2 %collective-permute-done.18.rest_1_ = bf16[64,4096]{1,0:T(8,128)(2,1)S(1)} collective-permute-done((bf16[64,4096]{1,0:T(8,128)(2,1)S(1)}, bf16[64,4096]{1,0:T(8,128)(2,1)S(1)}, u32[]{:S(2)}, u32[]{:S(2)}) %collective-permute-start.18) | collective-permute-done | bytes 524320 | tf_op jit(solution)/shard_map/ppermute | solution.py:280
  143.2 2.4 %collective-permute-start.23 = (bf16[64,4096]{1,0:T(8,128)(2,1)S(1)}, bf16[64,4096]{1,0:T(8,128)(2,1)S(1)}, u32[]{:S(2)}, u32[]{:S(2)}) collective-permute-start(bf16[64,4096]{1,0:T(8,128)(2,1)S(1)} %pad_maximum_fusion.1.rest_4_), channel_id=1, source_target_pairs={{0,3},{1,0},{2,1},{3,2},{4,7},{5,4},{6,5},{7,6},{8,11},{9,8},{10,9... | collective-permute-start | bytes 1572872 | tf_op jit(solution)/shard_map/ppermute | solution.py:276
  145.8 2.8 %collective-permute-done.22.rest_6_ = bf16[64,4096]{1,0:T(8,128)(2,1)S(1)} collective-permute-done((bf16[64,4096]{1,0:T(8,128)(2,1)S(1)}, bf16[64,4096]{1,0:T(8,128)(2,1)S(1)}, u32[]{:S(2)}, u32[]{:S(2)}) %collective-permute-start.22) | collective-permute-done | bytes 524320 | tf_op jit(solution)/shard_map/ppermute | solution.py:276
  148.6 4.4 %collective-permute-done.23.rest_7_ = bf16[64,4096]{1,0:T(8,128)(2,1)S(1)} collective-permute-done((bf16[64,4096]{1,0:T(8,128)(2,1)S(1)}, bf16[64,4096]{1,0:T(8,128)(2,1)S(1)}, u32[]{:S(2)}, u32[]{:S(2)}) %collective-permute-start.23) | collective-permute-done | bytes 524320 | tf_op jit(solution)/shard_map/ppermute | solution.py:276
  152.9 1.8 level3.1
  154.7 1.3 collective-permute-done.24
  156.0 1.5 collective-permute-start.25
  157.6 2.8 %collective-permute-done.25 = bf16[8,4096]{1,0:T(8,128)(2,1)S(1)} collective-permute-done((bf16[8,4096]{1,0:T(8,128)(2,1)S(1)}, bf16[8,4096]{1,0:T(8,128)(2,1)S(1)}, u32[]{:S(2)}, u32[]{:S(2)}) %collective-permute-start.25) | collective-permute-done | bytes 65568 | tf_op jit(solution)/shard_map/ppermute | solution.py:269
  160.4 1.3 collective-permute-start.26
  161.7 4.3 %collective-permute-done.26.other_ref = bf16[8,4096]{1,0:T(8,128)(2,1)S(1)} collective-permute-done((bf16[8,4096]{1,0:T(8,128)(2,1)S(1)}, bf16[8,4096]{1,0:T(8,128)(2,1)S(1)}, u32[]{:S(2)}, u32[]{:S(2)}) %collective-permute-start.26) | collective-permute-done | bytes 65568 | tf_op jit(solution)/shard_map/ppermute | solution.py:269
  166.0 3.6 %shard_map.48 = (f32[8,512]{1,0:T(8,128)S(1)}, bf16[8,2048]{1,0:T(8,128)(2,1)S(1)}, f32[8,512]{1,0:T(8,128)S(1)}, f32[8,512]{1,0:T(8,128)S(1)}) custom-call(s32[1]{0:T(128)} %bitcast.leaf_ref, bf16[8,4096]{1,0:T(8,128)(2,1)S(1)} %add_convert_fusion.own_ref, bf16[8,4096]{1,0:T(8,128)(2,1)S(1)} %collective-permute-done.26.other_ref, ...), custom_call_target="tpu_custom_call" | custom-call | tf_op jit(solution)/shard_map/pallas_call | solution.py:380
  169.5 1.2 collective-permute-done.27
  171.1 3.7 %collective-permute-done.28.other_ref = bf16[8,2048]{1,0:T(8,128)(2,1)S(1)} collective-permute-done((bf16[8,2048]{1,0:T(8,128)(2,1)S(1)}, bf16[8,2048]{1,0:T(8,128)(2,1)S(1)}, u32[]{:S(2)}, u32[]{:S(2)}) %collective-permute-start.28) | collective-permute-done | bytes 32800 | tf_op jit(solution)/shard_map/ppermute | solution.py:269
  175.4 1.2 collective-permute-done.29.other_ref
  177.0 11.9 %all_to_all.15 = f32[16,8,128]{2,1,0:T(8,128)S(1)} all-to-all(f32[16,8,128]{2,1,0:T(8,128)S(1)} %pack.1), channel_id=1, replica_groups=mesh['leaf'=8,'tile'=16] {'tile'}, dimensions={0} | all-to-all | bytes 131072 | tf_op jit(solution)/shard_map/all_to_all | solution.py:399
  (92 shorter events, 9.7 us)
Async XLA Ops:
  0.0 0.9 copy-start.9
  2.9 10.7 %all-to-all-start = ((bf16[8,32,256]{2,1,0:T(8,128)(2,1)}), bf16[8,32,256]{2,1,0:T(8,128)(2,1)S(1)}, u32[]{:S(2)}, u32[]{:S(2)}) async-start(bf16[8,32,256]{2,1,0:T(8,128)(2,1)} %split_couplings.1), calls=%async_computation | async-start | bytes 262144 | tf_op jit(solution)/shard_map/all_to_all | solution.py:306
  13.5 1.0 copy-start.4
  14.6 0.8 copy-start.10
  15.8 1.5 copy-start.1
  17.3 8.0 %copy-start.5 = (bf16[32,7680]{1,0:T(8,128)(2,1)S(1)}, bf16[32,7680]{1,0:T(8,128)(2,1)}, u32[]{:S(2)}) copy-start(bf16[32,7680]{1,0:T(8,128)(2,1)} %diag_ref.1) | copy-start | bytes 1474564
  17.3 62.8 %all-to-all-start.1 = ((bf16[16,688,128]{2,1,0:T(8,128)(2,1)}), bf16[16,688,128]{2,1,0:T(8,128)(2,1)S(1)}, u32[]{:S(2)}, u32[]{:S(2)}) async-start(bf16[16,688,128]{2,1,0:T(8,128)(2,1)} %copy-done.1), calls=%async_computation.1 | async-start | bytes 5636096 | tf_op jit(solution)/shard_map/all_to_all | solution.py:322
  25.4 53.0 %collective-permute-start.3 = (bf16[16,6144]{1,0:T(8,128)(2,1)S(1)}, bf16[16,6144]{1,0:T(8,128)(2,1)S(1)}, u32[]{:S(2)}, u32[]{:S(2)}) collective-permute-start(bf16[16,6144]{1,0:T(8,128)(2,1)S(1)} %get-tuple-element.53), channel_id=1, source_target_pairs={{0,4},{1,5},{2,6},{3,7},{4,8},{5,9},{6,10},{7,11},{8,12},{9,13},{1... | collective-permute-start | bytes 589832 | tf_op jit(solution)/shard_map/ppermute | solution.py:280
  27.4 51.0 %collective-permute-start.4 = (bf16[16,6144]{1,0:T(8,128)(2,1)S(1)}, bf16[16,6144]{1,0:T(8,128)(2,1)S(1)}, u32[]{:S(2)}, u32[]{:S(2)}) collective-permute-start(bf16[16,6144]{1,0:T(8,128)(2,1)S(1)} %get-tuple-element.53), channel_id=1, source_target_pairs={{0,8},{1,9},{2,10},{3,11},{4,12},{5,13},{6,14},{7,15},{8,0},{9,1},... | collective-permute-start | bytes 589832 | tf_op jit(solution)/shard_map/ppermute | solution.py:280
  30.0 37.0 %collective-permute-start = (bf16[16,6144]{1,0:T(8,128)(2,1)S(1)}, bf16[16,6144]{1,0:T(8,128)(2,1)S(1)}, u32[]{:S(2)}, u32[]{:S(2)}) collective-permute-start(bf16[16,6144]{1,0:T(8,128)(2,1)S(1)} %get-tuple-element.54), channel_id=1, source_target_pairs={{0,1},{1,2},{2,3},{3,0},{4,5},{5,6},{6,7},{7,4},{8,9},{9,10},{10,1... | collective-permute-start | bytes 589832 | tf_op jit(solution)/shard_map/ppermute | solution.py:276
  31.5 42.9 %collective-permute-start.1 = (bf16[16,6144]{1,0:T(8,128)(2,1)S(1)}, bf16[16,6144]{1,0:T(8,128)(2,1)S(1)}, u32[]{:S(2)}, u32[]{:S(2)}) collective-permute-start(bf16[16,6144]{1,0:T(8,128)(2,1)S(1)} %get-tuple-element.54), channel_id=1, source_target_pairs={{0,2},{1,3},{2,0},{3,1},{4,6},{5,7},{6,4},{7,5},{8,10},{9,11},{10,... | collective-permute-start | bytes 589832 | tf_op jit(solution)/shard_map/ppermute | solution.py:276
  34.2 40.2 %collective-permute-start.2 = (bf16[16,6144]{1,0:T(8,128)(2,1)S(1)}, bf16[16,6144]{1,0:T(8,128)(2,1)S(1)}, u32[]{:S(2)}, u32[]{:S(2)}) collective-permute-start(bf16[16,6144]{1,0:T(8,128)(2,1)S(1)} %get-tuple-element.54), channel_id=1, source_target_pairs={{0,3},{1,0},{2,1},{3,2},{4,7},{5,4},{6,5},{7,6},{8,11},{9,8},{10,9... | collective-permute-start | bytes 589832 | tf_op jit(solution)/shard_map/ppermute | solution.py:276
  67.1 11.4 %collective-permute-start.5 = (bf16[16,6144]{1,0:T(8,128)(2,1)S(1)}, bf16[16,6144]{1,0:T(8,128)(2,1)S(1)}, u32[]{:S(2)}, u32[]{:S(2)}) collective-permute-start(bf16[16,6144]{1,0:T(8,128)(2,1)S(1)} %get-tuple-element.53), channel_id=1, source_target_pairs={{0,12},{1,13},{2,14},{3,15},{4,0},{5,1},{6,2},{7,3},{8,4},{9,5},{1... | collective-permute-start | bytes 589832 | tf_op jit(solution)/shard_map/ppermute | solution.py:280
  75.2 21.9 %collective-permute-start.10 = (bf16[64,2048]{1,0:T(8,128)(2,1)}, bf16[64,2048]{1,0:T(8,128)(2,1)}, u32[]{:S(2)}, u32[]{:S(2)}) collective-permute-start(bf16[64,2048]{1,0:T(8,128)(2,1)} %pad_maximum_fusion.2.rest_0_), channel_id=1, source_target_pairs={{0,8},{1,9},{2,10},{3,11},{4,12},{5,13},{6,14},{7,15},{8,0},{9,1},... | collective-permute-start | bytes 786440 | tf_op jit(solution)/shard_map/ppermute | solution.py:280
  83.8 0.8 copy-start.7
  84.6 4.4 %copy-start.2 = (bf16[512,1024]{1,0:T(8,128)(2,1)}, bf16[512,1024]{1,0:T(8,128)(2,1)S(1)}, u32[]{:S(2)}) copy-start(bf16[512,1024]{1,0:T(8,128)(2,1)S(1)} %get-tuple-element.29.d_ref) | copy-start | bytes 3145732
  84.6 1.2 collective-permute-start.6
  84.6 14.7 %collective-permute-start.11 = (bf16[64,2048]{1,0:T(8,128)(2,1)}, bf16[64,2048]{1,0:T(8,128)(2,1)S(1)}, u32[]{:S(2)}, u32[]{:S(2)}) collective-permute-start(bf16[64,2048]{1,0:T(8,128)(2,1)} %pad_maximum_fusion.2.rest_0_), channel_id=1, source_target_pairs={{0,12},{1,13},{2,14},{3,15},{4,0},{5,1},{6,2},{7,3},{8,4},{9,5},{1... | collective-permute-start | bytes 786440 | tf_op jit(solution)/shard_map/ppermute | solution.py:280
  84.9 4.3 %slice-start.4 = ((bf16[16,6144]{1,0:T(8,128)(2,1)}), bf16[16,2048]{1,0:T(8,128)(2,1)S(1)}, s32[]{:S(2)}) async-start(bf16[16,6144]{1,0:T(8,128)(2,1)} %copy-done.14), calls=%async_computation.7 | async-start | bytes 131072 | tf_op jit(solution)/shard_map/slice | solution.py:290
  84.9 4.3 %slice-start.2 = ((bf16[16,6144]{1,0:T(8,128)(2,1)}), bf16[16,2048]{1,0:T(8,128)(2,1)S(1)}, s32[]{:S(2)}) async-start(bf16[16,6144]{1,0:T(8,128)(2,1)} %copy-done.12), calls=%async_computation.5 | async-start | bytes 131072 | tf_op jit(solution)/shard_map/slice | solution.py:290
  84.9 4.3 %slice-start.3 = ((bf16[16,6144]{1,0:T(8,128)(2,1)}), bf16[16,2048]{1,0:T(8,128)(2,1)S(1)}, s32[]{:S(2)}) async-start(bf16[16,6144]{1,0:T(8,128)(2,1)} %copy-done.13), calls=%async_computation.6 | async-start | bytes 131072 | tf_op jit(solution)/shard_map/slice | solution.py:290
  85.8 2.3 %copy-start = (bf16[34,4,128,128]{3,2,1,0:T(8,128)(2,1)S(1)}, bf16[34,4,128,128]{3,2,1,0:T(8,128)(2,1)}, u32[]{:S(2)}) copy-start(bf16[34,4,128,128]{3,2,1,0:T(8,128)(2,1)} %get-tuple-element.31.bd_ref) | copy-start | bytes 13369348
  89.0 10.2 %collective-permute-start.7 = (bf16[8,2048]{1,0:T(8,128)(2,1)S(1)}, bf16[8,2048]{1,0:T(8,128)(2,1)S(1)}, u32[]{:S(2)}, u32[]{:S(2)}) collective-permute-start(bf16[8,2048]{1,0:T(8,128)(2,1)S(1)} %get-tuple-element.33), channel_id=1, source_target_pairs={{0,16},{16,0},{32,48},{48,32},{64,80},{80,64},{96,112},{112,96},{1... | collective-permute-start | bytes 98312 | tf_op jit(solution)/shard_map/ppermute | solution.py:269
  89.3 13.9 %collective-permute-start.12 = (bf16[64,2048]{1,0:T(8,128)(2,1)S(1)}, bf16[64,2048]{1,0:T(8,128)(2,1)S(1)}, u32[]{:S(2)}, u32[]{:S(2)}) collective-permute-start(bf16[64,2048]{1,0:T(8,128)(2,1)S(1)} %pad_maximum_fusion.3.rest_4_), channel_id=1, source_target_pairs={{0,1},{1,2},{2,3},{3,0},{4,5},{5,6},{6,7},{7,4},{8,9},{9,10},{10,1... | collective-permute-start | bytes 786440 | tf_op jit(solution)/shard_map/ppermute | solution.py:276
  96.4 12.7 %collective-permute-start.13 = (bf16[64,2048]{1,0:T(8,128)(2,1)S(1)}, bf16[64,2048]{1,0:T(8,128)(2,1)S(1)}, u32[]{:S(2)}, u32[]{:S(2)}) collective-permute-start(bf16[64,2048]{1,0:T(8,128)(2,1)S(1)} %pad_maximum_fusion.3.rest_4_), channel_id=1, source_target_pairs={{0,2},{1,3},{2,0},{3,1},{4,6},{5,7},{6,4},{7,5},{8,10},{9,11},{10,... | collective-permute-start | bytes 786440 | tf_op jit(solution)/shard_map/ppermute | solution.py:276
  97.1 12.1 %collective-permute-start.14 = (bf16[64,2048]{1,0:T(8,128)(2,1)S(1)}, bf16[64,2048]{1,0:T(8,128)(2,1)S(1)}, u32[]{:S(2)}, u32[]{:S(2)}) collective-permute-start(bf16[64,2048]{1,0:T(8,128)(2,1)S(1)} %pad_maximum_fusion.3.rest_4_), channel_id=1, source_target_pairs={{0,3},{1,0},{2,1},{3,2},{4,7},{5,4},{6,5},{7,6},{8,11},{9,8},{10,9... | collective-permute-start | bytes 786440 | tf_op jit(solution)/shard_map/ppermute | solution.py:276
  99.2 9.9 %collective-permute-start.9 = (bf16[64,2048]{1,0:T(8,128)(2,1)}, bf16[64,2048]{1,0:T(8,128)(2,1)S(1)}, u32[]{:S(2)}, u32[]{:S(2)}) collective-permute-start(bf16[64,2048]{1,0:T(8,128)(2,1)} %pad_maximum_fusion.2.rest_0_), channel_id=1, source_target_pairs={{0,4},{1,5},{2,6},{3,7},{4,8},{5,9},{6,10},{7,11},{8,12},{9,13},{1... | collective-permute-start | bytes 786440 | tf_op jit(solution)/shard_map/ppermute | solution.py:280
  99.2 11.1 %collective-permute-start.8 = (bf16[8,2048]{1,0:T(8,128)(2,1)S(1)}, bf16[8,2048]{1,0:T(8,128)(2,1)S(1)}, u32[]{:S(2)}, u32[]{:S(2)}) collective-permute-start(bf16[8,2048]{1,0:T(8,128)(2,1)S(1)} %add_convert_fusion.5.own_ref), channel_id=1, source_target_pairs={{0,32},{16,48},{32,0},{48,16},{64,96},{80,112},{96,64},{112,80},{1... | collective-permute-start | bytes 98312 | tf_op jit(solution)/shard_map/ppermute | solution.py:269
  110.4 6.7 %copy-start.6 = (bf16[64,4096]{1,0:T(8,128)(2,1)S(1)}, bf16[64,4096]{1,0:T(8,128)(2,1)}, u32[]{:S(2)}) copy-start(bf16[64,4096]{1,0:T(8,128)(2,1)} %pad_maximum_fusion.rest_0_) | copy-start | bytes 1572868
  110.4 64.4 %slice-start = ((s8[4456448]{0:T(1024)(128)(4,1)}), s8[4194304]{0:T(1024)(128)(4,1)S(1)}, s32[]{:S(2)}) async-start(s8[4456448]{0:T(1024)(128)(4,1)} %bitcast.6), calls=%async_computation.3 | async-start | bytes 8388608
  115.1 1.3 collective-permute-start.15
  116.4 4.3 %collective-permute-start.16 = (bf16[8,4096]{1,0:T(8,128)(2,1)S(1)}, bf16[8,4096]{1,0:T(8,128)(2,1)S(1)}, u32[]{:S(2)}, u32[]{:S(2)}) collective-permute-start(bf16[8,4096]{1,0:T(8,128)(2,1)S(1)} %add_convert_fusion.3), channel_id=1, source_target_pairs={{0,32},{16,48},{32,0},{48,16},{64,96},{80,112},{96,64},{112,80},{1... | collective-permute-start | bytes 196616 | tf_op jit(solution)/shard_map/ppermute | solution.py:269
  117.0 26.2 %collective-permute-start.18 = (bf16[64,4096]{1,0:T(8,128)(2,1)S(1)}, bf16[64,4096]{1,0:T(8,128)(2,1)S(1)}, u32[]{:S(2)}, u32[]{:S(2)}) collective-permute-start(bf16[64,4096]{1,0:T(8,128)(2,1)S(1)} %copy-done.6), channel_id=1, source_target_pairs={{0,4},{1,5},{2,6},{3,7},{4,8},{5,9},{6,10},{7,11},{8,12},{9,13},{1... | collective-permute-start | bytes 1572872 | tf_op jit(solution)/shard_map/ppermute | solution.py:280
  120.7 54.0 %slice-start.1 = ((s8[4456448]{0:T(1024)(128)(4,1)}), s8[262144]{0:T(1024)(128)(4,1)S(1)}, s32[]{:S(2)}) async-start(s8[4456448]{0:T(1024)(128)(4,1)} %bitcast.6), calls=%async_computation.4 | async-start | bytes 524288
  120.8 5.6 %collective-permute-start.17 = (bf16[8,4096]{1,0:T(8,128)(2,1)S(1)}, bf16[8,4096]{1,0:T(8,128)(2,1)S(1)}, u32[]{:S(2)}, u32[]{:S(2)}) collective-permute-start(bf16[8,4096]{1,0:T(8,128)(2,1)S(1)} %add_convert_fusion.2.own_ref), channel_id=1, source_target_pairs={{0,96},{16,112},{32,64},{48,80},{64,32},{80,48},{96,0},{112,16},{1... | collective-permute-start | bytes 196616 | tf_op jit(solution)/shard_map/ppermute | solution.py:269
  122.0 23.6 %collective-permute-start.19 = (bf16[64,4096]{1,0:T(8,128)(2,1)S(1)}, bf16[64,4096]{1,0:T(8,128)(2,1)S(1)}, u32[]{:S(2)}, u32[]{:S(2)}) collective-permute-start(bf16[64,4096]{1,0:T(8,128)(2,1)S(1)} %copy-done.6), channel_id=1, source_target_pairs={{0,8},{1,9},{2,10},{3,11},{4,12},{5,13},{6,14},{7,15},{8,0},{9,1},... | collective-permute-start | bytes 1572872 | tf_op jit(solution)/shard_map/ppermute | solution.py:280
  122.0 23.8 %collective-permute-start.20 = (bf16[64,4096]{1,0:T(8,128)(2,1)S(1)}, bf16[64,4096]{1,0:T(8,128)(2,1)S(1)}, u32[]{:S(2)}, u32[]{:S(2)}) collective-permute-start(bf16[64,4096]{1,0:T(8,128)(2,1)S(1)} %copy-done.6), channel_id=1, source_target_pairs={{0,12},{1,13},{2,14},{3,15},{4,0},{5,1},{6,2},{7,3},{8,4},{9,5},{1... | collective-permute-start | bytes 1572872 | tf_op jit(solution)/shard_map/ppermute | solution.py:280
  123.2 22.6 %collective-permute-start.21 = (bf16[64,4096]{1,0:T(8,128)(2,1)S(1)}, bf16[64,4096]{1,0:T(8,128)(2,1)S(1)}, u32[]{:S(2)}, u32[]{:S(2)}) collective-permute-start(bf16[64,4096]{1,0:T(8,128)(2,1)S(1)} %pad_maximum_fusion.1.rest_4_), channel_id=1, source_target_pairs={{0,1},{1,2},{2,3},{3,0},{4,5},{5,6},{6,7},{7,4},{8,9},{9,10},{10,1... | collective-permute-start | bytes 1572872 | tf_op jit(solution)/shard_map/ppermute | solution.py:276
  126.3 22.3 %collective-permute-start.22 = (bf16[64,4096]{1,0:T(8,128)(2,1)S(1)}, bf16[64,4096]{1,0:T(8,128)(2,1)S(1)}, u32[]{:S(2)}, u32[]{:S(2)}) collective-permute-start(bf16[64,4096]{1,0:T(8,128)(2,1)S(1)} %pad_maximum_fusion.1.rest_4_), channel_id=1, source_target_pairs={{0,2},{1,3},{2,0},{3,1},{4,6},{5,7},{6,4},{7,5},{8,10},{9,11},{10,... | collective-permute-start | bytes 1572872 | tf_op jit(solution)/shard_map/ppermute | solution.py:276
  143.2 9.8 %collective-permute-start.23 = (bf16[64,4096]{1,0:T(8,128)(2,1)S(1)}, bf16[64,4096]{1,0:T(8,128)(2,1)S(1)}, u32[]{:S(2)}, u32[]{:S(2)}) collective-permute-start(bf16[64,4096]{1,0:T(8,128)(2,1)S(1)} %pad_maximum_fusion.1.rest_4_), channel_id=1, source_target_pairs={{0,3},{1,0},{2,1},{3,2},{4,7},{5,4},{6,5},{7,6},{8,11},{9,8},{10,9... | collective-permute-start | bytes 1572872 | tf_op jit(solution)/shard_map/ppermute | solution.py:276
  154.7 1.3 collective-permute-start.24
  156.0 4.3 %collective-permute-start.25 = (bf16[8,4096]{1,0:T(8,128)(2,1)S(1)}, bf16[8,4096]{1,0:T(8,128)(2,1)S(1)}, u32[]{:S(2)}, u32[]{:S(2)}) collective-permute-start(bf16[8,4096]{1,0:T(8,128)(2,1)S(1)} %add_convert_fusion.1), channel_id=1, source_target_pairs={{0,32},{16,48},{32,0},{48,16},{64,96},{80,112},{96,64},{112,80},{1... | collective-permute-start | bytes 196616 | tf_op jit(solution)/shard_map/ppermute | solution.py:269
  160.4 5.6 %collective-permute-start.26 = (bf16[8,4096]{1,0:T(8,128)(2,1)S(1)}, bf16[8,4096]{1,0:T(8,128)(2,1)S(1)}, u32[]{:S(2)}, u32[]{:S(2)}) collective-permute-start(bf16[8,4096]{1,0:T(8,128)(2,1)S(1)} %add_convert_fusion.own_ref), channel_id=1, source_target_pairs={{0,96},{16,112},{32,64},{48,80},{64,32},{80,48},{96,0},{112,16},{1... | collective-permute-start | bytes 196616 | tf_op jit(solution)/shard_map/ppermute | solution.py:269
  165.9 8.8 %copy-start.3 = (bf16[512,1024]{1,0:T(8,128)(2,1)S(1)}, bf16[512,1024]{1,0:T(8,128)(2,1)}, u32[]{:S(2)}) copy-start(bf16[512,1024]{1,0:T(8,128)(2,1)} %copy-done.2) | copy-start | bytes 3145732
  169.5 1.2 collective-permute-start.27
  170.8 5.8 %copy-start.8 = (bf16[512,512]{1,0:T(8,128)(2,1)S(1)}, bf16[512,512]{1,0:T(8,128)(2,1)}, u32[]{:S(2)}) copy-start(bf16[512,512]{1,0:T(8,128)(2,1)} %copy-done.7) | copy-start | bytes 1572868
  170.8 4.0 %collective-permute-start.28 = (bf16[8,2048]{1,0:T(8,128)(2,1)S(1)}, bf16[8,2048]{1,0:T(8,128)(2,1)S(1)}, u32[]{:S(2)}, u32[]{:S(2)}) collective-permute-start(bf16[8,2048]{1,0:T(8,128)(2,1)S(1)} %add_convert_fusion.4.own_ref), channel_id=1, source_target_pairs={{0,32},{16,48},{32,0},{48,16},{64,96},{80,112},{96,64},{112,80},{1... | collective-permute-start | bytes 98312 | tf_op jit(solution)/shard_map/ppermute | solution.py:269
  175.4 1.2 collective-permute-start.29
  (4 other events, 2.9 us)

commit v4 on v3

--- a/solution.py
+++ b/solution.py
@@ -15,14 +15,12 @@
 BLOCKS = 34
 VMEM = pl.BlockSpec(memory_space=pltpu.VMEM)
 SMEM = pl.BlockSpec(memory_space=pltpu.SMEM)
-RHS_ROWS, C_TILES, D0_TILES, D1_TILES = 16, 9, 4, 8
+RHS_ROWS, C_TILES = 16, 9
 C_AT = RHS_ROWS
-D0_AT = C_AT + 32 * C_TILES
-D1_AT = D0_AT + 32 * D0_TILES
-MESSAGE = D1_AT + 32 * D1_TILES
-
-
-def params(mib=48):
+MESSAGE = C_AT + 32 * C_TILES
+
+
+def params(mib=20):
     return pltpu.CompilerParams(vmem_limit_bytes=mib * 2**20)
 
 
@@ -83,7 +81,7 @@
         out_ref[leaf, :, 128:256] = merge(parts[4:], chunk).astype(BF)
 
 
-def message_kernel(leaf_ref, columns_ref, rhs_ref, diag_ref, out_ref):
+def message_kernel(leaf_ref, columns_ref, rhs_ref, out_ref):
     leaf = leaf_ref[0]
     chunk = lane_chunk(32)
     common = []
@@ -101,8 +99,6 @@
                 shift = (c - q) % 4 * 32
                 parts.append(values if shift == 0 else pltpu.roll(values, shift, 1))
         common.append(merge(parts, chunk).astype(BF))
-    for tile in range(D0_TILES + D1_TILES):
-        common.append(diag_ref[:, 128 * tile : 128 * tile + 128])
     rhs = jnp.transpose(rhs_ref[...].reshape(128, 128))
     high = rhs.astype(BF).astype(F32)
     low = rhs - high
@@ -124,7 +120,39 @@
     return jnp.concatenate(out, 1)
 
 
-def first_kernel(leaf_ref, msg_ref, b_ref, bd_ref, d0_ref, d1_ref, y0_ref, p1_ref):
+def put_in_order(place_ref, pieces, refs):
+    z, x = place_ref[0] // 4, place_ref[0] % 4
+    for half in range(2):
+        for n in range(4):
+            for m in range(4):
+                dz, dx = (n, m) if half == 0 else (m, n)
+                tile = (z - dz + 4) % 4 * 4 + (x - dx + 4) % 4
+                at = pl.multiple_of(tile * 32 + 16 * half, 16)
+                first = 0
+                for ref in refs:
+                    last = first + ref.shape[1]
+                    rows = pieces[4 * half + n][16 * m : 16 * m + 16, first:last]
+                    ref[pl.ds(at, 16), :] = rows
+                    first = last
+
+
+def order_kernel(place_ref, *rest):
+    put_in_order(place_ref, rest[:-1], rest[-1:])
+
+
+def stack_kernel(*refs):
+    parts, outs = refs[:4], refs[4:]
+    first = 0
+    for out in outs:
+        last = first + out.shape[1]
+        for n, part in enumerate(parts):
+            out[16 * n : 16 * n + 16, :] = part[:, first:last]
+        first = last
+
+
+def first_kernel(leaf_ref, place_ref, msg_ref, *rest):
+    pieces, outs = rest[:8], rest[8:]
+    b_ref, bd_ref, d0_ref, d1_ref, y0_ref, p1_ref = outs
     leaf = leaf_ref[0]
     chunk8 = lane_chunk(8)
     rhs = Rolled(
@@ -147,13 +175,7 @@
             block = msg_ref[4 * j : 4 * j + 4, at : at + 32, :].reshape(128, 128)
             spread = dot_nn(block, pick[m % 4])
             bd_ref[m, j] = jnp.where(same, spread, 0.0).astype(BF)
-    for ref, first, tiles in (
-        (d0_ref, D0_AT, D0_TILES),
-        (d1_ref, D1_AT, D1_TILES),
-    ):
-        for tile in range(tiles):
-            at = first + 32 * tile
-            ref[:, 128 * tile : 128 * tile + 128] = msg_ref[:, at : at + 32, :].reshape(512, 128)
+    put_in_order(place_ref, pieces, (d0_ref, d1_ref))
     y0 = dot_nt(b_ref[0].astype(BF), d0_ref[...]).astype(BF)
     y0_ref[...] = y0
     for i in range(2):
@@ -166,18 +188,6 @@
     for at in range(0, width, 1024):
         total = total + dot_nt(z[:, at : at + 1024], d_ref[:, at : at + 1024])
     return total
-
-
-def order_kernel(place_ref, *rest):
-    pieces, d_ref = rest[:-1], rest[-1]
-    z, x = place_ref[0] // 4, place_ref[0] % 4
-    for half in range(2):
-        for n in range(4):
-            for m in range(4):
-                dz, dx = (n, m) if half == 0 else (m, n)
-                tile = (z - dz + 4) % 4 * 4 + (x - dx + 4) % 4
-                at = pl.multiple_of(tile * 32 + 16 * half, 16)
-                d_ref[pl.ds(at, 16), :] = pieces[4 * half + n][16 * m : 16 * m + 16, :]
 
 
 def forward_kernel(level, leaf_ref, own_ref, other_ref, d_ref, b_ref, bd_ref, *rest):
@@ -282,19 +292,28 @@
 
 def local(right_sides, diag_inverse, coupling, pattern):
     leaf = lax.axis_index("leaf").astype(jnp.int32).reshape(1)
-    upper, lower = diag_inverse[0:16, 1536:], diag_inverse[16:32, 1536:]
+    place = lax.axis_index("tile").astype(jnp.int32).reshape(1)
+    upper, lower = diag_inverse[0:16], diag_inverse[16:32]
     upper = [upper] + [shift_x(upper, k) for k in (1, 2, 3)]
     lower = [lower] + [shift_z(lower, k) for k in (1, 2, 3)]
 
-    def joined(parts, first, stop):
-        return jnp.concatenate([p[:, first:stop] for p in parts], 0)
+    stack = pl.pallas_call(
+        stack_kernel,
+        out_shape=(shape((64, 1536)), shape((64, 2048)), shape((64, 4096))),
+        in_specs=[VMEM] * 4,
+        out_specs=(VMEM,) * 3,
+        compiler_params=params(),
+        name="stack",
+    )
+    upper1, upper2, upper = stack(*upper)
+    lower1, lower2, lower = stack(*lower)
 
     def far(upper, lower):
         pieces = [upper] + [shift_z(upper, k) for k in (1, 2, 3)]
         return pieces + [lower] + [shift_x(lower, k) for k in (1, 2, 3)]
 
-    pieces2 = far(joined(upper, 0, 2048), joined(lower, 0, 2048))
-    upper, lower = joined(upper, 2048, 6144), joined(lower, 2048, 6144)
+    pieces1 = far(upper1, lower1)
+    pieces2 = far(upper2, lower2)
     split = pl.pallas_call(
         split_kernel,
         out_shape=shape((8, 32, 256)),
@@ -307,18 +326,12 @@
     message_call = pl.pallas_call(
         message_kernel,
         out_shape=shape((16, MESSAGE, 128)),
-        grid=(1,),
-        in_specs=[
-            SMEM,
-            pl.BlockSpec((8, 32, 256), lambda i: (0, 0, 0)),
-            pl.BlockSpec((4, 32, 128), lambda i: (0, 0, 0)),
-            pl.BlockSpec((32, 1536), lambda i: (0, 0)),
-        ],
-        out_specs=pl.BlockSpec((16, MESSAGE, 128), lambda i: (0, 0, 0)),
+        in_specs=[SMEM, VMEM, VMEM],
+        out_specs=VMEM,
         compiler_params=params(),
         name="message",
     )
-    message = message_call(leaf, columns, right_sides, diag_inverse)
+    message = message_call(leaf, columns, right_sides)
     message = lax.all_to_all(message, "tile", 0, 0, tiled=True)
     upper, lower, message = lax.optimization_barrier((upper, lower, message))
     pieces3 = far(upper, lower)
@@ -332,14 +345,13 @@
             shape((8, 512)),
             shape((8, 1024)),
         ),
-        in_specs=[SMEM, VMEM],
+        in_specs=[SMEM, SMEM] + [VMEM] * 9,
         out_specs=(VMEM,) * 6,
         compiler_params=params(),
         name="level0",
     )
-    b, bd, d0, d1, y0, p1 = first_call(leaf, message)
-
-    place = lax.axis_index("tile").astype(jnp.int32).reshape(1)
+    b, bd, d0, d1, y0, p1 = first_call(leaf, place, message, *pieces1)
+
     order_call = pl.pallas_call(
         order_kernel,
         out_shape=shape((512, 2048)),

time: 190 us -> 170 us (0.89)
  waiting for transfers between devices: 94 us -> 81.8 us
  local copies, waits for them, and re-layouts: 9.66 us -> 4.75 us
  Pallas kernels: 18.6 us -> 13.9 us
  starting transfers between devices: 53.4 us -> 57.6 us
    ppermute x9 -> x12, waiting for transfers between devices: 53.7 us -> 18.4 us  [shift_x(): lax.ppermute(values, 'tile', [(t, t // 4 * 4 + (t + by) % 4) for t in ran...]
    ppermute x9 -> x12, waiting for transfers between devices: 13.4 us -> 38 us  [shift_z(): lax.ppermute(values, 'tile', [(t, (t + 4 * by) % 16) for t in range(16)])]
    ppermute x9 -> x12, starting transfers between devices: 10.7 us -> 21.2 us  [shift_z(): lax.ppermute(values, 'tile', [(t, (t + 4 * by) % 16) for t in range(16)])]
    ppermute x9 -> x12, starting transfers between devices: 24.2 us -> 18.9 us  [shift_x(): lax.ppermute(values, 'tile', [(t, t // 4 * 4 + (t + by) % 4) for t in ran...]
    unnamed x34 -> x12, local copies, waits for them, and re-layouts: 8.78 us -> 3.99 us
    pallas_call x2, Pallas kernels: 5.69 us -> 3.28 us  [forward(): pl.pallas_call(functools.partial(forward_kernel, level), out_shape=(shape...]
    pallas_call x3, Pallas kernels: 4.45 us -> 2.11 us  [back(): pl.pallas_call(functools.partial(back_kernel, level), out_shape=tuple(out...]
    pallas_call x2 -> x4, Pallas kernels: 4.07 us -> 5.05 us  [the longest x1 2.98 us: local(): b, bd, d0, d1, y0, p1 = first_call(leaf, place, message, *pieces1)]
  transfers between devices with their start and end apart: 32 -> 38, of which waited for: 19 -> 23; matrix products, arithmetic and copies ran while one was open for 1% -> 0% of each run, Pallas kernels for 3% -> 3%
where the time goes in v4:
time: 170 us
  waiting for transfers between devices  81.8 us (48%)
  starting transfers between devices  57.6 us (34%)
  Pallas kernels  13.9 us (8%)
  blocking collectives  11.7 us (7%)
  local copies, waits for them, and re-layouts  4.75 us (3%)
    ppermute x12, waiting for transfers between devices, shift_z(): lax.ppermute(values, 'tile', [(t, (t + 4 * by) % 16) for t in range(16)])  38 us
    ppermute x12, starting transfers between devices, shift_z(): lax.ppermute(values, 'tile', [(t, (t + 4 * by) % 16) for t in range(16)])  21.2 us
    ppermute x12, waiting for transfers between devices, reduce_over(): other = lax.ppermute(part, 'leaf', hops[n])  19.3 us
    ppermute x12, starting transfers between devices, shift_x(): lax.ppermute(values, 'tile', [(t, t // 4 * 4 + (t + by) % 4) for t in ran...  18.9 us
    ppermute x12, waiting for transfers between devices, shift_x(): lax.ppermute(values, 'tile', [(t, t // 4 * 4 + (t + by) % 4) for t in ran...  18.4 us
    all_to_all x1, blocking collectives, local(): packed = lax.all_to_all(packed, 'tile', 0, 0, tiled=True)  11.7 us
    all_to_all x1, starting transfers between devices, local(): message = lax.all_to_all(message, 'tile', 0, 0, tiled=True)  7.88 us
    all_to_all x1, waiting for transfers between devices, local(): columns = lax.all_to_all(split, 'leaf', 0, 0, tiled=True)  6.1 us
  transfers between devices with their start and end apart: 38, of which 23 were waited for; matrix products, arithmetic and copies ran while one was open for 0% of the time, Pallas kernels for 3%

profile of v4, /device:TPU:0, one launch (start us, length us, event | category | flops | bytes accessed | tf_op | source)
XLA Modules:
  0.0 169.9 jit_solution(16237424147435483315)
XLA Ops:
  1.5 1.3 split_couplings.1
  2.9 4.6 %all-to-all-start = ((bf16[8,32,256]{2,1,0:T(8,128)(2,1)}), bf16[8,32,256]{2,1,0:T(8,128)(2,1)S(1)}, u32[]{:S(2)}, u32[]{:S(2)}) async-start(bf16[8,32,256]{2,1,0:T(8,128)(2,1)} %split_couplings.1), calls=%async_computation | async-start | bytes 262144 | tf_op jit(solution)/shard_map/all_to_all | solution.py:325
  7.4 6.1 %all-to-all-done.columns_ref = bf16[8,32,256]{2,1,0:T(8,128)(2,1)S(1)} async-done(((bf16[8,32,256]{2,1,0:T(8,128)(2,1)}), bf16[8,32,256]{2,1,0:T(8,128)(2,1)S(1)}, u32[]{:S(2)}, u32[]{:S(2)}) %all-to-all-start) | async-done | bytes 131104 | tf_op jit(solution)/shard_map/all_to_all | solution.py:325
  14.4 1.3 message.1
  15.6 7.9 %all-to-all-start.1 = ((bf16[16,304,128]{2,1,0:T(8,128)(2,1)}), bf16[16,304,128]{2,1,0:T(8,128)(2,1)S(1)}, u32[]{:S(2)}, u32[]{:S(2)}) async-start(bf16[16,304,128]{2,1,0:T(8,128)(2,1)} %message.1), calls=%async_computation.1 | async-start | bytes 2490368 | tf_op jit(solution)/shard_map/all_to_all | solution.py:335
  23.6 2.0 %collective-permute-start.3 = (bf16[16,7680]{1,0:T(8,128)(2,1)S(1)}, bf16[16,7680]{1,0:T(8,128)(2,1)S(1)}, u32[]{:S(2)}, u32[]{:S(2)}) collective-permute-start(bf16[16,7680]{1,0:T(8,128)(2,1)S(1)} %get-tuple-element.61.refs_0_), channel_id=1, source_target_pairs={{0,4},{1,5},{2,6},{3,7},{4,8},{5,9},{6,10},{7,11},{8,12},{9,13},{1... | collective-permute-start | bytes 737288 | tf_op jit(solution)/shard_map/ppermute | solution.py:290
  25.6 2.7 %collective-permute-start.4 = (bf16[16,7680]{1,0:T(8,128)(2,1)S(1)}, bf16[16,7680]{1,0:T(8,128)(2,1)S(1)}, u32[]{:S(2)}, u32[]{:S(2)}) collective-permute-start(bf16[16,7680]{1,0:T(8,128)(2,1)S(1)} %get-tuple-element.61.refs_0_), channel_id=1, source_target_pairs={{0,8},{1,9},{2,10},{3,11},{4,12},{5,13},{6,14},{7,15},{8,0},{9,1},... | collective-permute-start | bytes 737288 | tf_op jit(solution)/shard_map/ppermute | solution.py:290
  28.2 1.5 collective-permute-start.5
  29.7 1.5 collective-permute-start
  31.2 2.7 %collective-permute-start.1 = (bf16[16,7680]{1,0:T(8,128)(2,1)S(1)}, bf16[16,7680]{1,0:T(8,128)(2,1)S(1)}, u32[]{:S(2)}, u32[]{:S(2)}) collective-permute-start(bf16[16,7680]{1,0:T(8,128)(2,1)S(1)} %get-tuple-element.62.refs_0_), channel_id=1, source_target_pairs={{0,2},{1,3},{2,0},{3,1},{4,6},{5,7},{6,4},{7,5},{8,10},{9,11},{10,... | collective-permute-start | bytes 737288 | tf_op jit(solution)/shard_map/ppermute | solution.py:286
  33.8 12.9 %collective-permute-done.3.refs_1_ = bf16[16,7680]{1,0:T(8,128)(2,1)S(1)} collective-permute-done((bf16[16,7680]{1,0:T(8,128)(2,1)S(1)}, bf16[16,7680]{1,0:T(8,128)(2,1)S(1)}, u32[]{:S(2)}, u32[]{:S(2)}) %collective-permute-start.3) | collective-permute-done | bytes 245792 | tf_op jit(solution)/shard_map/ppermute | solution.py:290
  46.7 2.0 %collective-permute-start.2 = (bf16[16,7680]{1,0:T(8,128)(2,1)S(1)}, bf16[16,7680]{1,0:T(8,128)(2,1)S(1)}, u32[]{:S(2)}, u32[]{:S(2)}) collective-permute-start(bf16[16,7680]{1,0:T(8,128)(2,1)S(1)} %get-tuple-element.62.refs_0_), channel_id=1, source_target_pairs={{0,3},{1,0},{2,1},{3,2},{4,7},{5,4},{6,5},{7,6},{8,11},{9,8},{10,9... | collective-permute-start | bytes 737288 | tf_op jit(solution)/shard_map/ppermute | solution.py:286
  48.7 2.2 %collective-permute-done.4.refs_2_ = bf16[16,7680]{1,0:T(8,128)(2,1)S(1)} collective-permute-done((bf16[16,7680]{1,0:T(8,128)(2,1)S(1)}, bf16[16,7680]{1,0:T(8,128)(2,1)S(1)}, u32[]{:S(2)}, u32[]{:S(2)}) %collective-permute-start.4) | collective-permute-done | bytes 245792 | tf_op jit(solution)/shard_map/ppermute | solution.py:290
  51.0 3.0 %collective-permute-start.10 = (bf16[64,1536]{1,0:T(8,128)(2,1)S(1)}, bf16[64,1536]{1,0:T(8,128)(2,1)S(1)}, u32[]{:S(2)}, u32[]{:S(2)}) collective-permute-start(bf16[64,1536]{1,0:T(8,128)(2,1)S(1)} %get-tuple-element.37.rest_4_), channel_id=1, source_target_pairs={{0,2},{1,3},{2,0},{3,1},{4,6},{5,7},{6,4},{7,5},{8,10},{9,11},{10,... | collective-permute-start | bytes 589832 | tf_op jit(solution)/shard_map/ppermute | solution.py:286
  57.4 3.0 %collective-permute-done.10.rest_6_ = bf16[64,1536]{1,0:T(8,128)(2,1)S(1)} collective-permute-done((bf16[64,1536]{1,0:T(8,128)(2,1)S(1)}, bf16[64,1536]{1,0:T(8,128)(2,1)S(1)}, u32[]{:S(2)}, u32[]{:S(2)}) %collective-permute-start.10) | collective-permute-done | bytes 196640 | tf_op jit(solution)/shard_map/ppermute | solution.py:286
  60.4 1.2 collective-permute-start.7
  61.6 1.2 collective-permute-done.11.rest_7_
  63.5 1.3 collective-permute-start.8
  64.8 4.3 %collective-permute-done.9.rest_5_ = bf16[64,1536]{1,0:T(8,128)(2,1)} collective-permute-done((bf16[64,1536]{1,0:T(8,128)(2,1)S(1)}, bf16[64,1536]{1,0:T(8,128)(2,1)}, u32[]{:S(2)}, u32[]{:S(2)}) %collective-permute-start.9) | collective-permute-done | bytes 196640 | tf_op jit(solution)/shard_map/ppermute | solution.py:286
  70.7 3.0 %level0.1 = (f32[4,8,512]{2,1,0:T(8,128)S(1)}, bf16[34,4,128,128]{3,2,1,0:T(8,128)(2,1)S(1)}, bf16[512,512]{1,0:T(8,128)(2,1)S(1)}, bf16[512,1024]{1,0:T(8,128)(...) custom-call(s32[1]{0:T(128)} %bitcast.leaf_ref, s32[1]{0:T(128)} %bitcast.1.place_ref, ...), custom_call_target="tpu_custom_call" | custom-call | tf_op jit(solution)/shard_map/level0/pallas_call | solution.py:353
  76.1 3.2 %collective-permute-start.19 = (bf16[64,2048]{1,0:T(8,128)(2,1)S(1)}, bf16[64,2048]{1,0:T(8,128)(2,1)S(1)}, u32[]{:S(2)}, u32[]{:S(2)}) collective-permute-start(bf16[64,2048]{1,0:T(8,128)(2,1)S(1)} %get-tuple-element.45.rest_4_), channel_id=1, source_target_pairs={{0,2},{1,3},{2,0},{3,1},{4,6},{5,7},{6,4},{7,5},{8,10},{9,11},{10,... | collective-permute-start | bytes 786440 | tf_op jit(solution)/shard_map/ppermute | solution.py:286
  79.3 1.8 %collective-permute-start.20 = (bf16[64,2048]{1,0:T(8,128)(2,1)S(1)}, bf16[64,2048]{1,0:T(8,128)(2,1)S(1)}, u32[]{:S(2)}, u32[]{:S(2)}) collective-permute-start(bf16[64,2048]{1,0:T(8,128)(2,1)S(1)} %get-tuple-element.45.rest_4_), channel_id=1, source_target_pairs={{0,3},{1,0},{2,1},{3,2},{4,7},{5,4},{6,5},{7,6},{8,11},{9,8},{10,9... | collective-permute-start | bytes 786440 | tf_op jit(solution)/shard_map/ppermute | solution.py:286
  81.1 2.8 %collective-permute-start.15 = (bf16[64,2048]{1,0:T(8,128)(2,1)S(1)}, bf16[64,2048]{1,0:T(8,128)(2,1)S(1)}, u32[]{:S(2)}, u32[]{:S(2)}) collective-permute-start(bf16[64,2048]{1,0:T(8,128)(2,1)S(1)} %get-tuple-element.44.rest_0_), channel_id=1, source_target_pairs={{0,4},{1,5},{2,6},{3,7},{4,8},{5,9},{6,10},{7,11},{8,12},{9,13},{1... | collective-permute-start | bytes 786440 | tf_op jit(solution)/shard_map/ppermute | solution.py:290
  85.1 1.8 %collective-permute-start.17 = (bf16[64,2048]{1,0:T(8,128)(2,1)S(1)}, bf16[64,2048]{1,0:T(8,128)(2,1)S(1)}, u32[]{:S(2)}, u32[]{:S(2)}) collective-permute-start(bf16[64,2048]{1,0:T(8,128)(2,1)S(1)} %get-tuple-element.44.rest_0_), channel_id=1, source_target_pairs={{0,12},{1,13},{2,14},{3,15},{4,0},{5,1},{6,2},{7,3},{8,4},{9,5},{1... | collective-permute-start | bytes 786440 | tf_op jit(solution)/shard_map/ppermute | solution.py:290
  87.5 5.4 %collective-permute-done.20.rest_7_ = bf16[64,2048]{1,0:T(8,128)(2,1)S(1)} collective-permute-done((bf16[64,2048]{1,0:T(8,128)(2,1)S(1)}, bf16[64,2048]{1,0:T(8,128)(2,1)S(1)}, u32[]{:S(2)}, u32[]{:S(2)}) %collective-permute-start.20) | collective-permute-done | bytes 262176 | tf_op jit(solution)/shard_map/ppermute | solution.py:286
  92.9 3.8 %collective-permute-done.16.rest_2_ = bf16[64,2048]{1,0:T(8,128)(2,1)S(1)} collective-permute-done((bf16[64,2048]{1,0:T(8,128)(2,1)S(1)}, bf16[64,2048]{1,0:T(8,128)(2,1)S(1)}, u32[]{:S(2)}, u32[]{:S(2)}) %collective-permute-start.16) | collective-permute-done | bytes 262176 | tf_op jit(solution)/shard_map/ppermute | solution.py:290
  96.8 2.3 %shard_map.47 = (bf16[8,512]{1,0:T(8,128)(2,1)S(1)}, bf16[8,4096]{1,0:T(8,128)(2,1)S(1)}) custom-call(s32[1]{0:T(128)} %bitcast.leaf_ref, bf16[8,2048]{1,0:T(8,128)(2,1)S(1)} %add_convert_fusion.5.own_ref, bf16[8,2048]{1,0:T(8,128)(2,1)S(1)} %collective-permute-done.14.other_ref, bf16[512,2048]{1,0:T(8,128)(2,1)S(1)} %order2.1.d_ref, ...), custom_call_target="tpu_custom_call" | custom-call | tf_op jit(solution)/shard_map/pallas_call | solution.py:367
  99.1 1.3 collective-permute-done.21
  101.0 2.1 %collective-permute-start.24 = (bf16[64,4096]{1,0:T(8,128)(2,1)S(1)}, bf16[64,4096]{1,0:T(8,128)(2,1)S(1)}, u32[]{:S(2)}, u32[]{:S(2)}) collective-permute-start(bf16[64,4096]{1,0:T(8,128)(2,1)S(1)} %get-tuple-element.48.rest_0_), channel_id=1, source_target_pairs={{0,4},{1,5},{2,6},{3,7},{4,8},{5,9},{6,10},{7,11},{8,12},{9,13},{1... | collective-permute-start | bytes 1572872 | tf_op jit(solution)/shard_map/ppermute | solution.py:290
  103.1 1.6 collective-permute-done.22
  104.8 1.2 collective-permute-start.23
  106.0 3.1 %collective-permute-start.25 = (bf16[64,4096]{1,0:T(8,128)(2,1)S(1)}, bf16[64,4096]{1,0:T(8,128)(2,1)S(1)}, u32[]{:S(2)}, u32[]{:S(2)}) collective-permute-start(bf16[64,4096]{1,0:T(8,128)(2,1)S(1)} %get-tuple-element.48.rest_0_), channel_id=1, source_target_pairs={{0,8},{1,9},{2,10},{3,11},{4,12},{5,13},{6,14},{7,15},{8,0},{9,1},... | collective-permute-start | bytes 1572872 | tf_op jit(solution)/shard_map/ppermute | solution.py:290
  109.1 1.7 %collective-permute-start.26 = (bf16[64,4096]{1,0:T(8,128)(2,1)S(1)}, bf16[64,4096]{1,0:T(8,128)(2,1)S(1)}, u32[]{:S(2)}, u32[]{:S(2)}) collective-permute-start(bf16[64,4096]{1,0:T(8,128)(2,1)S(1)} %get-tuple-element.48.rest_0_), channel_id=1, source_target_pairs={{0,12},{1,13},{2,14},{3,15},{4,0},{5,1},{6,2},{7,3},{8,4},{9,5},{1... | collective-permute-start | bytes 1572872 | tf_op jit(solution)/shard_map/ppermute | solution.py:290
  110.8 1.7 %collective-permute-start.28 = (bf16[64,4096]{1,0:T(8,128)(2,1)S(1)}, bf16[64,4096]{1,0:T(8,128)(2,1)S(1)}, u32[]{:S(2)}, u32[]{:S(2)}) collective-permute-start(bf16[64,4096]{1,0:T(8,128)(2,1)S(1)} %get-tuple-element.49.rest_4_), channel_id=1, source_target_pairs={{0,2},{1,3},{2,0},{3,1},{4,6},{5,7},{6,4},{7,5},{8,10},{9,11},{10,... | collective-permute-start | bytes 1572872 | tf_op jit(solution)/shard_map/ppermute | solution.py:286
  112.5 3.7 %collective-permute-done.24.rest_1_ = bf16[64,4096]{1,0:T(8,128)(2,1)S(1)} collective-permute-done((bf16[64,4096]{1,0:T(8,128)(2,1)S(1)}, bf16[64,4096]{1,0:T(8,128)(2,1)S(1)}, u32[]{:S(2)}, u32[]{:S(2)}) %collective-permute-start.24) | collective-permute-done | bytes 524320 | tf_op jit(solution)/shard_map/ppermute | solution.py:290
  116.5 11.5 %collective-permute-done.25.rest_2_ = bf16[64,4096]{1,0:T(8,128)(2,1)S(1)} collective-permute-done((bf16[64,4096]{1,0:T(8,128)(2,1)S(1)}, bf16[64,4096]{1,0:T(8,128)(2,1)S(1)}, u32[]{:S(2)}, u32[]{:S(2)}) %collective-permute-start.25) | collective-permute-done | bytes 524320 | tf_op jit(solution)/shard_map/ppermute | solution.py:290
  128.0 3.3 %collective-permute-done.26.rest_3_ = bf16[64,4096]{1,0:T(8,128)(2,1)S(1)} collective-permute-done((bf16[64,4096]{1,0:T(8,128)(2,1)S(1)}, bf16[64,4096]{1,0:T(8,128)(2,1)S(1)}, u32[]{:S(2)}, u32[]{:S(2)}) %collective-permute-start.26) | collective-permute-done | bytes 524320 | tf_op jit(solution)/shard_map/ppermute | solution.py:290
  131.3 4.0 %collective-permute-done.27.rest_5_ = bf16[64,4096]{1,0:T(8,128)(2,1)S(1)} collective-permute-done((bf16[64,4096]{1,0:T(8,128)(2,1)S(1)}, bf16[64,4096]{1,0:T(8,128)(2,1)S(1)}, u32[]{:S(2)}, u32[]{:S(2)}) %collective-permute-start.27) | collective-permute-done | bytes 524320 | tf_op jit(solution)/shard_map/ppermute | solution.py:286
  135.9 1.8 %level3.1 = bf16[8,4096]{1,0:T(8,128)(2,1)S(1)} custom-call(bf16[8,4096]{1,0:T(8,128)(2,1)S(1)} %add_convert_fusion.2.own_ref, bf16[8,4096]{1,0:T(8,128)(2,1)S(1)} %collective-permute-done.23.other_ref, bf16[64,4096]{1,0:T(8,128)(2,1)S(1)} %get-tuple-element.48.rest_0_, bf16[64,4096]{1,0:T(8,128)(2,1)S(1)} %collective-permute-done.24.rest_1_, ...), custom_call_target="tpu_custom_call" | custom-call | tf_op jit(solution)/shard_map/level3/pallas_call | solution.py:378
  137.7 1.3 collective-permute-done.30
  139.0 4.3 %collective-permute-done.31 = bf16[8,4096]{1,0:T(8,128)(2,1)S(1)} collective-permute-done((bf16[8,4096]{1,0:T(8,128)(2,1)S(1)}, bf16[8,4096]{1,0:T(8,128)(2,1)S(1)}, u32[]{:S(2)}, u32[]{:S(2)}) %collective-permute-start.31) | collective-permute-done | bytes 65568 | tf_op jit(solution)/shard_map/ppermute | solution.py:279
  143.3 2.1 %collective-permute-start.32 = (bf16[8,4096]{1,0:T(8,128)(2,1)S(1)}, bf16[8,4096]{1,0:T(8,128)(2,1)S(1)}, u32[]{:S(2)}, u32[]{:S(2)}) collective-permute-start(bf16[8,4096]{1,0:T(8,128)(2,1)S(1)} %add_convert_fusion.own_ref), channel_id=1, source_target_pairs={{0,96},{16,112},{32,64},{48,80},{64,32},{80,48},{96,0},{112,16},{1... | collective-permute-start | bytes 196616 | tf_op jit(solution)/shard_map/ppermute | solution.py:279
  145.5 3.4 %collective-permute-done.32.other_ref = bf16[8,4096]{1,0:T(8,128)(2,1)S(1)} collective-permute-done((bf16[8,4096]{1,0:T(8,128)(2,1)S(1)}, bf16[8,4096]{1,0:T(8,128)(2,1)S(1)}, u32[]{:S(2)}, u32[]{:S(2)}) %collective-permute-start.32) | collective-permute-done | bytes 65568 | tf_op jit(solution)/shard_map/ppermute | solution.py:279
  148.9 1.2 shard_map.48
  150.1 1.2 collective-permute-done.33
  151.4 3.9 %collective-permute-done.34.other_ref = bf16[8,2048]{1,0:T(8,128)(2,1)S(1)} collective-permute-done((bf16[8,2048]{1,0:T(8,128)(2,1)S(1)}, bf16[8,2048]{1,0:T(8,128)(2,1)S(1)}, u32[]{:S(2)}, u32[]{:S(2)}) %collective-permute-start.34) | collective-permute-done | bytes 32800 | tf_op jit(solution)/shard_map/ppermute | solution.py:279
  155.9 1.2 collective-permute-done.35.other_ref
  157.5 11.7 %all_to_all.15 = f32[16,8,128]{2,1,0:T(8,128)S(1)} all-to-all(f32[16,8,128]{2,1,0:T(8,128)S(1)} %pack.1), channel_id=1, replica_groups=mesh['leaf'=8,'tile'=16] {'tile'}, dimensions={0} | all-to-all | bytes 131072 | tf_op jit(solution)/shard_map/all_to_all | solution.py:411
  (62 shorter events, 16.0 us)
Async XLA Ops:
  0.0 0.9 copy-start.2
  0.9 0.7 copy-start.4
  2.9 10.7 %all-to-all-start = ((bf16[8,32,256]{2,1,0:T(8,128)(2,1)}), bf16[8,32,256]{2,1,0:T(8,128)(2,1)S(1)}, u32[]{:S(2)}, u32[]{:S(2)}) async-start(bf16[8,32,256]{2,1,0:T(8,128)(2,1)} %split_couplings.1), calls=%async_computation | async-start | bytes 262144 | tf_op jit(solution)/shard_map/all_to_all | solution.py:325
  13.5 0.8 copy-start.3
  14.4 9.1 %copy-start.5 = (bf16[32,7680]{1,0:T(8,128)(2,1)S(1)}, bf16[32,7680]{1,0:T(8,128)(2,1)}, u32[]{:S(2)}) copy-start(bf16[32,7680]{1,0:T(8,128)(2,1)} %param.5) | copy-start | bytes 1474564
  15.6 49.2 %all-to-all-start.1 = ((bf16[16,304,128]{2,1,0:T(8,128)(2,1)}), bf16[16,304,128]{2,1,0:T(8,128)(2,1)S(1)}, u32[]{:S(2)}, u32[]{:S(2)}) async-start(bf16[16,304,128]{2,1,0:T(8,128)(2,1)} %message.1), calls=%async_computation.1 | async-start | bytes 2490368 | tf_op jit(solution)/shard_map/all_to_all | solution.py:335
  23.6 23.1 %collective-permute-start.3 = (bf16[16,7680]{1,0:T(8,128)(2,1)S(1)}, bf16[16,7680]{1,0:T(8,128)(2,1)S(1)}, u32[]{:S(2)}, u32[]{:S(2)}) collective-permute-start(bf16[16,7680]{1,0:T(8,128)(2,1)S(1)} %get-tuple-element.61.refs_0_), channel_id=1, source_target_pairs={{0,4},{1,5},{2,6},{3,7},{4,8},{5,9},{6,10},{7,11},{8,12},{9,13},{1... | collective-permute-start | bytes 737288 | tf_op jit(solution)/shard_map/ppermute | solution.py:290
  25.6 25.4 %collective-permute-start.4 = (bf16[16,7680]{1,0:T(8,128)(2,1)S(1)}, bf16[16,7680]{1,0:T(8,128)(2,1)S(1)}, u32[]{:S(2)}, u32[]{:S(2)}) collective-permute-start(bf16[16,7680]{1,0:T(8,128)(2,1)S(1)} %get-tuple-element.61.refs_0_), channel_id=1, source_target_pairs={{0,8},{1,9},{2,10},{3,11},{4,12},{5,13},{6,14},{7,15},{8,0},{9,1},... | collective-permute-start | bytes 737288 | tf_op jit(solution)/shard_map/ppermute | solution.py:290
  28.2 22.7 %collective-permute-start.5 = (bf16[16,7680]{1,0:T(8,128)(2,1)S(1)}, bf16[16,7680]{1,0:T(8,128)(2,1)S(1)}, u32[]{:S(2)}, u32[]{:S(2)}) collective-permute-start(bf16[16,7680]{1,0:T(8,128)(2,1)S(1)} %get-tuple-element.61.refs_0_), channel_id=1, source_target_pairs={{0,12},{1,13},{2,14},{3,15},{4,0},{5,1},{6,2},{7,3},{8,4},{9,5},{1... | collective-permute-start | bytes 737288 | tf_op jit(solution)/shard_map/ppermute | solution.py:290
  29.7 25.6 %collective-permute-start = (bf16[16,7680]{1,0:T(8,128)(2,1)S(1)}, bf16[16,7680]{1,0:T(8,128)(2,1)S(1)}, u32[]{:S(2)}, u32[]{:S(2)}) collective-permute-start(bf16[16,7680]{1,0:T(8,128)(2,1)S(1)} %get-tuple-element.62.refs_0_), channel_id=1, source_target_pairs={{0,1},{1,2},{2,3},{3,0},{4,5},{5,6},{6,7},{7,4},{8,9},{9,10},{10,1... | collective-permute-start | bytes 737288 | tf_op jit(solution)/shard_map/ppermute | solution.py:286
  31.2 24.9 %collective-permute-start.1 = (bf16[16,7680]{1,0:T(8,128)(2,1)S(1)}, bf16[16,7680]{1,0:T(8,128)(2,1)S(1)}, u32[]{:S(2)}, u32[]{:S(2)}) collective-permute-start(bf16[16,7680]{1,0:T(8,128)(2,1)S(1)} %get-tuple-element.62.refs_0_), channel_id=1, source_target_pairs={{0,2},{1,3},{2,0},{3,1},{4,6},{5,7},{6,4},{7,5},{8,10},{9,11},{10,... | collective-permute-start | bytes 737288 | tf_op jit(solution)/shard_map/ppermute | solution.py:286
  46.7 10.0 %collective-permute-start.2 = (bf16[16,7680]{1,0:T(8,128)(2,1)S(1)}, bf16[16,7680]{1,0:T(8,128)(2,1)S(1)}, u32[]{:S(2)}, u32[]{:S(2)}) collective-permute-start(bf16[16,7680]{1,0:T(8,128)(2,1)S(1)} %get-tuple-element.62.refs_0_), channel_id=1, source_target_pairs={{0,3},{1,0},{2,1},{3,2},{4,7},{5,4},{6,5},{7,6},{8,11},{9,8},{10,9... | collective-permute-start | bytes 737288 | tf_op jit(solution)/shard_map/ppermute | solution.py:286
  51.0 9.4 %collective-permute-start.10 = (bf16[64,1536]{1,0:T(8,128)(2,1)S(1)}, bf16[64,1536]{1,0:T(8,128)(2,1)S(1)}, u32[]{:S(2)}, u32[]{:S(2)}) collective-permute-start(bf16[64,1536]{1,0:T(8,128)(2,1)S(1)} %get-tuple-element.37.rest_4_), channel_id=1, source_target_pairs={{0,2},{1,3},{2,0},{3,1},{4,6},{5,7},{6,4},{7,5},{8,10},{9,11},{10,... | collective-permute-start | bytes 589832 | tf_op jit(solution)/shard_map/ppermute | solution.py:286
  54.1 8.7 %collective-permute-start.11 = (bf16[64,1536]{1,0:T(8,128)(2,1)S(1)}, bf16[64,1536]{1,0:T(8,128)(2,1)S(1)}, u32[]{:S(2)}, u32[]{:S(2)}) collective-permute-start(bf16[64,1536]{1,0:T(8,128)(2,1)S(1)} %get-tuple-element.37.rest_4_), channel_id=1, source_target_pairs={{0,3},{1,0},{2,1},{3,2},{4,7},{5,4},{6,5},{7,6},{8,11},{9,8},{10,9... | collective-permute-start | bytes 589832 | tf_op jit(solution)/shard_map/ppermute | solution.py:286
  55.3 28.7 %collective-permute-start.18 = (bf16[64,2048]{1,0:T(8,128)(2,1)S(1)}, bf16[64,2048]{1,0:T(8,128)(2,1)S(1)}, u32[]{:S(2)}, u32[]{:S(2)}) collective-permute-start(bf16[64,2048]{1,0:T(8,128)(2,1)S(1)} %get-tuple-element.45.rest_4_), channel_id=1, source_target_pairs={{0,1},{1,2},{2,3},{3,0},{4,5},{5,6},{6,7},{7,4},{8,9},{9,10},{10,1... | collective-permute-start | bytes 786440 | tf_op jit(solution)/shard_map/ppermute | solution.py:286
  56.1 13.0 %collective-permute-start.9 = (bf16[64,1536]{1,0:T(8,128)(2,1)S(1)}, bf16[64,1536]{1,0:T(8,128)(2,1)}, u32[]{:S(2)}, u32[]{:S(2)}) collective-permute-start(bf16[64,1536]{1,0:T(8,128)(2,1)S(1)} %get-tuple-element.37.rest_4_), channel_id=1, source_target_pairs={{0,1},{1,2},{2,3},{3,0},{4,5},{5,6},{6,7},{7,4},{8,9},{9,10},{10,1... | collective-permute-start | bytes 589832 | tf_op jit(solution)/shard_map/ppermute | solution.py:286
  57.4 11.7 %collective-permute-start.6 = (bf16[64,1536]{1,0:T(8,128)(2,1)}, bf16[64,1536]{1,0:T(8,128)(2,1)}, u32[]{:S(2)}, u32[]{:S(2)}) collective-permute-start(bf16[64,1536]{1,0:T(8,128)(2,1)} %get-tuple-element.36.rest_0_), channel_id=1, source_target_pairs={{0,4},{1,5},{2,6},{3,7},{4,8},{5,9},{6,10},{7,11},{8,12},{9,13},{1... | collective-permute-start | bytes 589832 | tf_op jit(solution)/shard_map/ppermute | solution.py:290
  60.4 8.7 %collective-permute-start.7 = (bf16[64,1536]{1,0:T(8,128)(2,1)}, bf16[64,1536]{1,0:T(8,128)(2,1)}, u32[]{:S(2)}, u32[]{:S(2)}) collective-permute-start(bf16[64,1536]{1,0:T(8,128)(2,1)} %get-tuple-element.36.rest_0_), channel_id=1, source_target_pairs={{0,8},{1,9},{2,10},{3,11},{4,12},{5,13},{6,14},{7,15},{8,0},{9,1},... | collective-permute-start | bytes 589832 | tf_op jit(solution)/shard_map/ppermute | solution.py:290
  62.8 0.7 copy-start
  63.5 6.2 %collective-permute-start.8 = (bf16[64,1536]{1,0:T(8,128)(2,1)}, bf16[64,1536]{1,0:T(8,128)(2,1)}, u32[]{:S(2)}, u32[]{:S(2)}) collective-permute-start(bf16[64,1536]{1,0:T(8,128)(2,1)} %get-tuple-element.36.rest_0_), channel_id=1, source_target_pairs={{0,12},{1,13},{2,14},{3,15},{4,0},{5,1},{6,2},{7,3},{8,4},{9,5},{1... | collective-permute-start | bytes 589832 | tf_op jit(solution)/shard_map/ppermute | solution.py:290
  69.8 0.9 copy-start.1
  73.7 1.2 collective-permute-start.12
  75.9 9.2 %collective-permute-start.13 = (bf16[8,2048]{1,0:T(8,128)(2,1)S(1)}, bf16[8,2048]{1,0:T(8,128)(2,1)S(1)}, u32[]{:S(2)}, u32[]{:S(2)}) collective-permute-start(bf16[8,2048]{1,0:T(8,128)(2,1)S(1)} %get-tuple-element.43), channel_id=1, source_target_pairs={{0,16},{16,0},{32,48},{48,32},{64,80},{80,64},{96,112},{112,96},{1... | collective-permute-start | bytes 98312 | tf_op jit(solution)/shard_map/ppermute | solution.py:279
  76.1 10.8 %collective-permute-start.19 = (bf16[64,2048]{1,0:T(8,128)(2,1)S(1)}, bf16[64,2048]{1,0:T(8,128)(2,1)S(1)}, u32[]{:S(2)}, u32[]{:S(2)}) collective-permute-start(bf16[64,2048]{1,0:T(8,128)(2,1)S(1)} %get-tuple-element.45.rest_4_), channel_id=1, source_target_pairs={{0,2},{1,3},{2,0},{3,1},{4,6},{5,7},{6,4},{7,5},{8,10},{9,11},{10,... | collective-permute-start | bytes 786440 | tf_op jit(solution)/shard_map/ppermute | solution.py:286
  79.3 13.6 %collective-permute-start.20 = (bf16[64,2048]{1,0:T(8,128)(2,1)S(1)}, bf16[64,2048]{1,0:T(8,128)(2,1)S(1)}, u32[]{:S(2)}, u32[]{:S(2)}) collective-permute-start(bf16[64,2048]{1,0:T(8,128)(2,1)S(1)} %get-tuple-element.45.rest_4_), channel_id=1, source_target_pairs={{0,3},{1,0},{2,1},{3,2},{4,7},{5,4},{6,5},{7,6},{8,11},{9,8},{10,9... | collective-permute-start | bytes 786440 | tf_op jit(solution)/shard_map/ppermute | solution.py:286
  81.1 11.7 %collective-permute-start.15 = (bf16[64,2048]{1,0:T(8,128)(2,1)S(1)}, bf16[64,2048]{1,0:T(8,128)(2,1)S(1)}, u32[]{:S(2)}, u32[]{:S(2)}) collective-permute-start(bf16[64,2048]{1,0:T(8,128)(2,1)S(1)} %get-tuple-element.44.rest_0_), channel_id=1, source_target_pairs={{0,4},{1,5},{2,6},{3,7},{4,8},{5,9},{6,10},{7,11},{8,12},{9,13},{1... | collective-permute-start | bytes 786440 | tf_op jit(solution)/shard_map/ppermute | solution.py:290
  83.9 12.7 %collective-permute-start.16 = (bf16[64,2048]{1,0:T(8,128)(2,1)S(1)}, bf16[64,2048]{1,0:T(8,128)(2,1)S(1)}, u32[]{:S(2)}, u32[]{:S(2)}) collective-permute-start(bf16[64,2048]{1,0:T(8,128)(2,1)S(1)} %get-tuple-element.44.rest_0_), channel_id=1, source_target_pairs={{0,8},{1,9},{2,10},{3,11},{4,12},{5,13},{6,14},{7,15},{8,0},{9,1},... | collective-permute-start | bytes 786440 | tf_op jit(solution)/shard_map/ppermute | solution.py:290
  85.1 11.6 %collective-permute-start.17 = (bf16[64,2048]{1,0:T(8,128)(2,1)S(1)}, bf16[64,2048]{1,0:T(8,128)(2,1)S(1)}, u32[]{:S(2)}, u32[]{:S(2)}) collective-permute-start(bf16[64,2048]{1,0:T(8,128)(2,1)S(1)} %get-tuple-element.44.rest_0_), channel_id=1, source_target_pairs={{0,12},{1,13},{2,14},{3,15},{4,0},{5,1},{6,2},{7,3},{8,4},{9,5},{1... | collective-permute-start | bytes 786440 | tf_op jit(solution)/shard_map/ppermute | solution.py:290
  86.9 9.9 %collective-permute-start.14 = (bf16[8,2048]{1,0:T(8,128)(2,1)S(1)}, bf16[8,2048]{1,0:T(8,128)(2,1)S(1)}, u32[]{:S(2)}, u32[]{:S(2)}) collective-permute-start(bf16[8,2048]{1,0:T(8,128)(2,1)S(1)} %add_convert_fusion.5.own_ref), channel_id=1, source_target_pairs={{0,32},{16,48},{32,0},{48,16},{64,96},{80,112},{96,64},{112,80},{1... | collective-permute-start | bytes 98312 | tf_op jit(solution)/shard_map/ppermute | solution.py:279
  99.1 1.3 collective-permute-start.21
  100.4 4.3 %collective-permute-start.22 = (bf16[8,4096]{1,0:T(8,128)(2,1)S(1)}, bf16[8,4096]{1,0:T(8,128)(2,1)S(1)}, u32[]{:S(2)}, u32[]{:S(2)}) collective-permute-start(bf16[8,4096]{1,0:T(8,128)(2,1)S(1)} %add_convert_fusion.3), channel_id=1, source_target_pairs={{0,32},{16,48},{32,0},{48,16},{64,96},{80,112},{96,64},{112,80},{1... | collective-permute-start | bytes 196616 | tf_op jit(solution)/shard_map/ppermute | solution.py:279
  101.0 15.2 %collective-permute-start.24 = (bf16[64,4096]{1,0:T(8,128)(2,1)S(1)}, bf16[64,4096]{1,0:T(8,128)(2,1)S(1)}, u32[]{:S(2)}, u32[]{:S(2)}) collective-permute-start(bf16[64,4096]{1,0:T(8,128)(2,1)S(1)} %get-tuple-element.48.rest_0_), channel_id=1, source_target_pairs={{0,4},{1,5},{2,6},{3,7},{4,8},{5,9},{6,10},{7,11},{8,12},{9,13},{1... | collective-permute-start | bytes 1572872 | tf_op jit(solution)/shard_map/ppermute | solution.py:290
  104.8 6.0 %collective-permute-start.23 = (bf16[8,4096]{1,0:T(8,128)(2,1)S(1)}, bf16[8,4096]{1,0:T(8,128)(2,1)S(1)}, u32[]{:S(2)}, u32[]{:S(2)}) collective-permute-start(bf16[8,4096]{1,0:T(8,128)(2,1)S(1)} %add_convert_fusion.2.own_ref), channel_id=1, source_target_pairs={{0,96},{16,112},{32,64},{48,80},{64,32},{80,48},{96,0},{112,16},{1... | collective-permute-start | bytes 196616 | tf_op jit(solution)/shard_map/ppermute | solution.py:279
  106.0 22.0 %collective-permute-start.25 = (bf16[64,4096]{1,0:T(8,128)(2,1)S(1)}, bf16[64,4096]{1,0:T(8,128)(2,1)S(1)}, u32[]{:S(2)}, u32[]{:S(2)}) collective-permute-start(bf16[64,4096]{1,0:T(8,128)(2,1)S(1)} %get-tuple-element.48.rest_0_), channel_id=1, source_target_pairs={{0,8},{1,9},{2,10},{3,11},{4,12},{5,13},{6,14},{7,15},{8,0},{9,1},... | collective-permute-start | bytes 1572872 | tf_op jit(solution)/shard_map/ppermute | solution.py:290
  109.1 22.2 %collective-permute-start.26 = (bf16[64,4096]{1,0:T(8,128)(2,1)S(1)}, bf16[64,4096]{1,0:T(8,128)(2,1)S(1)}, u32[]{:S(2)}, u32[]{:S(2)}) collective-permute-start(bf16[64,4096]{1,0:T(8,128)(2,1)S(1)} %get-tuple-element.48.rest_0_), channel_id=1, source_target_pairs={{0,12},{1,13},{2,14},{3,15},{4,0},{5,1},{6,2},{7,3},{8,4},{9,5},{1... | collective-permute-start | bytes 1572872 | tf_op jit(solution)/shard_map/ppermute | solution.py:290
  110.8 24.4 %collective-permute-start.27 = (bf16[64,4096]{1,0:T(8,128)(2,1)S(1)}, bf16[64,4096]{1,0:T(8,128)(2,1)S(1)}, u32[]{:S(2)}, u32[]{:S(2)}) collective-permute-start(bf16[64,4096]{1,0:T(8,128)(2,1)S(1)} %get-tuple-element.49.rest_4_), channel_id=1, source_target_pairs={{0,1},{1,2},{2,3},{3,0},{4,5},{5,6},{6,7},{7,4},{8,9},{9,10},{10,1... | collective-permute-start | bytes 1572872 | tf_op jit(solution)/shard_map/ppermute | solution.py:286
  110.8 24.4 %collective-permute-start.28 = (bf16[64,4096]{1,0:T(8,128)(2,1)S(1)}, bf16[64,4096]{1,0:T(8,128)(2,1)S(1)}, u32[]{:S(2)}, u32[]{:S(2)}) collective-permute-start(bf16[64,4096]{1,0:T(8,128)(2,1)S(1)} %get-tuple-element.49.rest_4_), channel_id=1, source_target_pairs={{0,2},{1,3},{2,0},{3,1},{4,6},{5,7},{6,4},{7,5},{8,10},{9,11},{10,... | collective-permute-start | bytes 1572872 | tf_op jit(solution)/shard_map/ppermute | solution.py:286
  116.2 19.6 %collective-permute-start.29 = (bf16[64,4096]{1,0:T(8,128)(2,1)S(1)}, bf16[64,4096]{1,0:T(8,128)(2,1)S(1)}, u32[]{:S(2)}, u32[]{:S(2)}) collective-permute-start(bf16[64,4096]{1,0:T(8,128)(2,1)S(1)} %get-tuple-element.49.rest_4_), channel_id=1, source_target_pairs={{0,3},{1,0},{2,1},{3,2},{4,7},{5,4},{6,5},{7,6},{8,11},{9,8},{10,9... | collective-permute-start | bytes 1572872 | tf_op jit(solution)/shard_map/ppermute | solution.py:286
  137.7 1.3 collective-permute-start.30
  138.9 4.3 %collective-permute-start.31 = (bf16[8,4096]{1,0:T(8,128)(2,1)S(1)}, bf16[8,4096]{1,0:T(8,128)(2,1)S(1)}, u32[]{:S(2)}, u32[]{:S(2)}) collective-permute-start(bf16[8,4096]{1,0:T(8,128)(2,1)S(1)} %add_convert_fusion.1), channel_id=1, source_target_pairs={{0,32},{16,48},{32,0},{48,16},{64,96},{80,112},{96,64},{112,80},{1... | collective-permute-start | bytes 196616 | tf_op jit(solution)/shard_map/ppermute | solution.py:279
  143.3 5.6 %collective-permute-start.32 = (bf16[8,4096]{1,0:T(8,128)(2,1)S(1)}, bf16[8,4096]{1,0:T(8,128)(2,1)S(1)}, u32[]{:S(2)}, u32[]{:S(2)}) collective-permute-start(bf16[8,4096]{1,0:T(8,128)(2,1)S(1)} %add_convert_fusion.own_ref), channel_id=1, source_target_pairs={{0,96},{16,112},{32,64},{48,80},{64,32},{80,48},{96,0},{112,16},{1... | collective-permute-start | bytes 196616 | tf_op jit(solution)/shard_map/ppermute | solution.py:279
  150.1 1.2 collective-permute-start.33
  151.4 4.0 %collective-permute-start.34 = (bf16[8,2048]{1,0:T(8,128)(2,1)S(1)}, bf16[8,2048]{1,0:T(8,128)(2,1)S(1)}, u32[]{:S(2)}, u32[]{:S(2)}) collective-permute-start(bf16[8,2048]{1,0:T(8,128)(2,1)S(1)} %add_convert_fusion.4.own_ref), channel_id=1, source_target_pairs={{0,32},{16,48},{32,0},{48,16},{64,96},{80,112},{96,64},{112,80},{1... | collective-permute-start | bytes 98312 | tf_op jit(solution)/shard_map/ppermute | solution.py:279
  155.9 1.2 collective-permute-start.35

commit v5 on v4

--- a/solution.py
+++ b/solution.py
@@ -136,10 +136,6 @@
                     first = last
 
 
-def order_kernel(place_ref, *rest):
-    put_in_order(place_ref, rest[:-1], rest[-1:])
-
-
 def stack_kernel(*refs):
     parts, outs = refs[:4], refs[4:]
     first = 0
@@ -152,7 +148,7 @@
 
 def first_kernel(leaf_ref, place_ref, msg_ref, *rest):
     pieces, outs = rest[:8], rest[8:]
-    b_ref, bd_ref, d0_ref, d1_ref, y0_ref, p1_ref = outs
+    b_ref, bd_ref, d0_ref, d1_ref, d2_ref, y0_ref, p1_ref = outs
     leaf = leaf_ref[0]
     chunk8 = lane_chunk(8)
     rhs = Rolled(
@@ -175,7 +171,7 @@
             block = msg_ref[4 * j : 4 * j + 4, at : at + 32, :].reshape(128, 128)
             spread = dot_nn(block, pick[m % 4])
             bd_ref[m, j] = jnp.where(same, spread, 0.0).astype(BF)
-    put_in_order(place_ref, pieces, (d0_ref, d1_ref))
+    put_in_order(place_ref, pieces, (d0_ref, d1_ref, d2_ref))
     y0 = dot_nt(b_ref[0].astype(BF), d0_ref[...]).astype(BF)
     y0_ref[...] = y0
     for i in range(2):
@@ -299,21 +295,20 @@
 
     stack = pl.pallas_call(
         stack_kernel,
-        out_shape=(shape((64, 1536)), shape((64, 2048)), shape((64, 4096))),
+        out_shape=(shape((64, 3584)), shape((64, 4096))),
         in_specs=[VMEM] * 4,
-        out_specs=(VMEM,) * 3,
+        out_specs=(VMEM,) * 2,
         compiler_params=params(),
         name="stack",
     )
-    upper1, upper2, upper = stack(*upper)
-    lower1, lower2, lower = stack(*lower)
+    upper1, upper = stack(*upper)
+    lower1, lower = stack(*lower)
 
     def far(upper, lower):
         pieces = [upper] + [shift_z(upper, k) for k in (1, 2, 3)]
         return pieces + [lower] + [shift_x(lower, k) for k in (1, 2, 3)]
 
     pieces1 = far(upper1, lower1)
-    pieces2 = far(upper2, lower2)
     split = pl.pallas_call(
         split_kernel,
         out_shape=shape((8, 32, 256)),
@@ -342,25 +337,16 @@
             shape((BLOCKS, 4, 128, 128)),
             shape((512, 512)),
             shape((512, 1024)),
+            shape((512, 2048)),
             shape((8, 512)),
             shape((8, 1024)),
         ),
         in_specs=[SMEM, SMEM] + [VMEM] * 9,
-        out_specs=(VMEM,) * 6,
+        out_specs=(VMEM,) * 7,
         compiler_params=params(),
         name="level0",
     )
-    b, bd, d0, d1, y0, p1 = first_call(leaf, place, message, *pieces1)
-
-    order_call = pl.pallas_call(
-        order_kernel,
-        out_shape=shape((512, 2048)),
-        in_specs=[SMEM] + [VMEM] * 8,
-        out_specs=VMEM,
-        compiler_params=params(),
-        name="order2",
-    )
-    d2 = order_call(place, *pieces2)
+    b, bd, d0, d1, d2, y0, p1 = first_call(leaf, place, message, *pieces1)
 
     def forward(level, part, d, ys):
         own, other = reduce_over(part, level)

time: 170 us -> 185 us (1.088)
  waiting for transfers between devices: 81.8 us -> 107 us
  starting transfers between devices: 57.6 us -> 47.3 us
    ppermute x12 -> x9, waiting for transfers between devices: 38 us -> 49.1 us  [shift_z(): lax.ppermute(values, 'tile', [(t, (t + 4 * by) % 16) for t in range(16)])]
    ppermute x12 -> x9, starting transfers between devices: 21.2 us -> 13.2 us  [shift_z(): lax.ppermute(values, 'tile', [(t, (t + 4 * by) % 16) for t in range(16)])]
    ppermute x12, waiting for transfers between devices: 19.3 us -> 26.2 us  [reduce_over(): other = lax.ppermute(part, 'leaf', hops[n])]
    ppermute x12 -> x9, waiting for transfers between devices: 18.4 us -> 25.3 us  [shift_x(): lax.ppermute(values, 'tile', [(t, t // 4 * 4 + (t + by) % 4) for t in ran...]
    unnamed x12 -> x8, local copies, waits for them, and re-layouts: 3.99 us -> 2.38 us
    ppermute x12 -> x9, starting transfers between devices: 18.9 us -> 17.3 us  [shift_x(): lax.ppermute(values, 'tile', [(t, t // 4 * 4 + (t + by) % 4) for t in ran...]
    pallas_call x4 -> x3, Pallas kernels: 3.95 us -> 4.48 us  [the longest x1 3.56 us: local(): b, bd, d0, d1, d2, y0, p1 = first_call(leaf, place, message, *pieces1)]
  transfers between devices with their start and end apart: 38 -> 32, of which waited for: 23 -> 25; matrix products, arithmetic and copies ran while one was open for 0% -> 0% of each run, Pallas kernels for 3% -> 0%
where the time goes in v5:
time: 185 us
  waiting for transfers between devices  107 us (58%)
  starting transfers between devices  47.3 us (26%)
  Pallas kernels  14.4 us (8%)
  blocking collectives  13 us (7%)
  local copies, waits for them, and re-layouts  3.14 us (2%)
    ppermute x9, waiting for transfers between devices, shift_z(): lax.ppermute(values, 'tile', [(t, (t + 4 * by) % 16) for t in range(16)])  49.1 us
    ppermute x12, waiting for transfers between devices, reduce_over(): other = lax.ppermute(part, 'leaf', hops[n])  26.2 us
    ppermute x9, waiting for transfers between devices, shift_x(): lax.ppermute(values, 'tile', [(t, t // 4 * 4 + (t + by) % 4) for t in ran...  25.3 us
    ppermute x9, starting transfers between devices, shift_x(): lax.ppermute(values, 'tile', [(t, t // 4 * 4 + (t + by) % 4) for t in ran...  17.3 us
    ppermute x9, starting transfers between devices, shift_z(): lax.ppermute(values, 'tile', [(t, (t + 4 * by) % 16) for t in range(16)])  13.2 us
    all_to_all x1, blocking collectives, local(): packed = lax.all_to_all(packed, 'tile', 0, 0, tiled=True)  13 us
    all_to_all x1, starting transfers between devices, local(): message = lax.all_to_all(message, 'tile', 0, 0, tiled=True)  7.88 us
    all_to_all x1, waiting for transfers between devices, local(): columns = lax.all_to_all(split, 'leaf', 0, 0, tiled=True)  6.1 us
  transfers between devices with their start and end apart: 32, of which 25 were waited for; matrix products, arithmetic and copies ran while one was open for 0% of the time, Pallas kernels for 0%

profile of v5, /device:TPU:0, one launch (start us, length us, event | category | flops | bytes accessed | tf_op | source)
XLA Modules:
  0.0 184.8 jit_solution(1424915705134702303)
XLA Ops:
  1.5 1.3 split_couplings.1
  2.9 4.6 %all-to-all-start = ((bf16[8,32,256]{2,1,0:T(8,128)(2,1)}), bf16[8,32,256]{2,1,0:T(8,128)(2,1)S(1)}, u32[]{:S(2)}, u32[]{:S(2)}) async-start(bf16[8,32,256]{2,1,0:T(8,128)(2,1)} %split_couplings.1), calls=%async_computation | async-start | bytes 262144 | tf_op jit(solution)/shard_map/all_to_all | solution.py:320
  7.4 6.1 %all-to-all-done.columns_ref = bf16[8,32,256]{2,1,0:T(8,128)(2,1)S(1)} async-done(((bf16[8,32,256]{2,1,0:T(8,128)(2,1)}), bf16[8,32,256]{2,1,0:T(8,128)(2,1)S(1)}, u32[]{:S(2)}, u32[]{:S(2)}) %all-to-all-start) | async-done | bytes 131104 | tf_op jit(solution)/shard_map/all_to_all | solution.py:320
  14.4 1.3 message.1
  15.6 7.9 %all-to-all-start.1 = ((bf16[16,304,128]{2,1,0:T(8,128)(2,1)}), bf16[16,304,128]{2,1,0:T(8,128)(2,1)S(1)}, u32[]{:S(2)}, u32[]{:S(2)}) async-start(bf16[16,304,128]{2,1,0:T(8,128)(2,1)} %message.1), calls=%async_computation.1 | async-start | bytes 2490368 | tf_op jit(solution)/shard_map/all_to_all | solution.py:330
  23.6 2.0 %collective-permute-start.3 = (bf16[16,7680]{1,0:T(8,128)(2,1)S(1)}, bf16[16,7680]{1,0:T(8,128)(2,1)S(1)}, u32[]{:S(2)}, u32[]{:S(2)}) collective-permute-start(bf16[16,7680]{1,0:T(8,128)(2,1)S(1)} %get-tuple-element.59.refs_0_), channel_id=1, source_target_pairs={{0,4},{1,5},{2,6},{3,7},{4,8},{5,9},{6,10},{7,11},{8,12},{9,13},{1... | collective-permute-start | bytes 737288 | tf_op jit(solution)/shard_map/ppermute | solution.py:286
  25.6 2.7 %collective-permute-start.4 = (bf16[16,7680]{1,0:T(8,128)(2,1)S(1)}, bf16[16,7680]{1,0:T(8,128)(2,1)S(1)}, u32[]{:S(2)}, u32[]{:S(2)}) collective-permute-start(bf16[16,7680]{1,0:T(8,128)(2,1)S(1)} %get-tuple-element.59.refs_0_), channel_id=1, source_target_pairs={{0,8},{1,9},{2,10},{3,11},{4,12},{5,13},{6,14},{7,15},{8,0},{9,1},... | collective-permute-start | bytes 737288 | tf_op jit(solution)/shard_map/ppermute | solution.py:286
  28.2 1.5 collective-permute-start.5
  29.7 17.0 %collective-permute-done.3.refs_1_ = bf16[16,7680]{1,0:T(8,128)(2,1)S(1)} collective-permute-done((bf16[16,7680]{1,0:T(8,128)(2,1)S(1)}, bf16[16,7680]{1,0:T(8,128)(2,1)S(1)}, u32[]{:S(2)}, u32[]{:S(2)}) %collective-permute-start.3) | collective-permute-done | bytes 245792 | tf_op jit(solution)/shard_map/ppermute | solution.py:286
  46.7 4.3 %collective-permute-done.4.refs_2_ = bf16[16,7680]{1,0:T(8,128)(2,1)S(1)} collective-permute-done((bf16[16,7680]{1,0:T(8,128)(2,1)S(1)}, bf16[16,7680]{1,0:T(8,128)(2,1)S(1)}, u32[]{:S(2)}, u32[]{:S(2)}) %collective-permute-start.4) | collective-permute-done | bytes 245792 | tf_op jit(solution)/shard_map/ppermute | solution.py:286
  51.0 3.0 %collective-permute-start.10 = (bf16[64,3584]{1,0:T(8,128)(2,1)S(1)}, bf16[64,3584]{1,0:T(8,128)(2,1)S(1)}, u32[]{:S(2)}, u32[]{:S(2)}) collective-permute-start(bf16[64,3584]{1,0:T(8,128)(2,1)S(1)} %get-tuple-element.36.rest_4_), channel_id=1, source_target_pairs={{0,2},{1,3},{2,0},{3,1},{4,6},{5,7},{6,4},{7,5},{8,10},{9,11},{10,... | collective-permute-start | bytes 1376264 | tf_op jit(solution)/shard_map/ppermute | solution.py:282
  54.7 2.1 %collective-permute-start.1 = (bf16[16,7680]{1,0:T(8,128)(2,1)S(1)}, bf16[16,7680]{1,0:T(8,128)(2,1)S(1)}, u32[]{:S(2)}, u32[]{:S(2)}) collective-permute-start(bf16[16,7680]{1,0:T(8,128)(2,1)S(1)} %get-tuple-element.60.refs_0_), channel_id=1, source_target_pairs={{0,2},{1,3},{2,0},{3,1},{4,6},{5,7},{6,4},{7,5},{8,10},{9,11},{10,... | collective-permute-start | bytes 737288 | tf_op jit(solution)/shard_map/ppermute | solution.py:282
  57.3 1.4 collective-permute-start.11
  58.7 12.5 %collective-permute-done.refs_1_ = bf16[16,7680]{1,0:T(8,128)(2,1)S(1)} collective-permute-done((bf16[16,7680]{1,0:T(8,128)(2,1)S(1)}, bf16[16,7680]{1,0:T(8,128)(2,1)S(1)}, u32[]{:S(2)}, u32[]{:S(2)}) %collective-permute-start) | collective-permute-done | bytes 245792 | tf_op jit(solution)/shard_map/ppermute | solution.py:282
  71.2 1.6 collective-permute-start.9
  72.8 3.8 %collective-permute-done.1.refs_2_ = bf16[16,7680]{1,0:T(8,128)(2,1)S(1)} collective-permute-done((bf16[16,7680]{1,0:T(8,128)(2,1)S(1)}, bf16[16,7680]{1,0:T(8,128)(2,1)S(1)}, u32[]{:S(2)}, u32[]{:S(2)}) %collective-permute-start.1) | collective-permute-done | bytes 245792 | tf_op jit(solution)/shard_map/ppermute | solution.py:282
  77.5 1.8 collective-permute-start.7
  79.3 2.1 %collective-permute-start.8 = (bf16[64,3584]{1,0:T(8,128)(2,1)}, bf16[64,3584]{1,0:T(8,128)(2,1)}, u32[]{:S(2)}, u32[]{:S(2)}) collective-permute-start(bf16[64,3584]{1,0:T(8,128)(2,1)} %get-tuple-element.35.rest_0_), channel_id=1, source_target_pairs={{0,12},{1,13},{2,14},{3,15},{4,0},{5,1},{6,2},{7,3},{8,4},{9,5},{1... | collective-permute-start | bytes 1376264 | tf_op jit(solution)/shard_map/ppermute | solution.py:286
  81.3 3.4 %collective-permute-done.11.rest_7_ = bf16[64,3584]{1,0:T(8,128)(2,1)} collective-permute-done((bf16[64,3584]{1,0:T(8,128)(2,1)S(1)}, bf16[64,3584]{1,0:T(8,128)(2,1)}, u32[]{:S(2)}, u32[]{:S(2)}) %collective-permute-start.11) | collective-permute-done | bytes 458784 | tf_op jit(solution)/shard_map/ppermute | solution.py:282
  84.7 1.0 collective-permute-done.9.rest_5_
  85.7 13.2 %collective-permute-done.6.rest_1_ = bf16[64,3584]{1,0:T(8,128)(2,1)} collective-permute-done((bf16[64,3584]{1,0:T(8,128)(2,1)}, bf16[64,3584]{1,0:T(8,128)(2,1)}, u32[]{:S(2)}, u32[]{:S(2)}) %collective-permute-start.6) | collective-permute-done | bytes 458784 | tf_op jit(solution)/shard_map/ppermute | solution.py:286
  99.5 3.6 %level0.1 = (f32[4,8,512]{2,1,0:T(8,128)S(1)}, bf16[34,4,128,128]{3,2,1,0:T(8,128)(2,1)S(1)}, bf16[512,512]{1,0:T(8,128)(2,1)S(1)}, bf16[512,1024]{1,0:T(8,128)(...) custom-call(s32[1]{0:T(128)} %bitcast.leaf_ref, ...), custom_call_target="tpu_custom_call" | custom-call | tf_op jit(solution)/shard_map/level0/pallas_call | solution.py:349
  103.1 1.2 collective-permute-done.12.other_ref
  104.3 1.0 shard_map.46
  105.5 1.0 collective-permute-done.13
  107.2 3.3 %collective-permute-done.14.other_ref = bf16[8,2048]{1,0:T(8,128)(2,1)S(1)} collective-permute-done((bf16[8,2048]{1,0:T(8,128)(2,1)S(1)}, bf16[8,2048]{1,0:T(8,128)(2,1)S(1)}, u32[]{:S(2)}, u32[]{:S(2)}) %collective-permute-start.14) | collective-permute-done | bytes 32800 | tf_op jit(solution)/shard_map/ppermute | solution.py:275
  110.5 2.3 %shard_map.47 = (bf16[8,512]{1,0:T(8,128)(2,1)S(1)}, bf16[8,4096]{1,0:T(8,128)(2,1)S(1)}) custom-call(s32[1]{0:T(128)} %bitcast.leaf_ref, bf16[8,2048]{1,0:T(8,128)(2,1)S(1)} %add_convert_fusion.5.own_ref, bf16[8,2048]{1,0:T(8,128)(2,1)S(1)} %collective-permute-done.14.other_ref, bf16[512,2048]{1,0:T(8,128)(2,1)S(1)} %get-tuple-element.43.d_ref, ...), custom_call_target="tpu_custom_call" | custom-call | tf_op jit(solution)/shard_map/pallas_call | solution.py:353
  112.8 1.3 collective-permute-done.15
  115.0 3.4 %collective-permute-done.16 = bf16[8,4096]{1,0:T(8,128)(2,1)S(1)} collective-permute-done((bf16[8,4096]{1,0:T(8,128)(2,1)S(1)}, bf16[8,4096]{1,0:T(8,128)(2,1)S(1)}, u32[]{:S(2)}, u32[]{:S(2)}) %collective-permute-start.16) | collective-permute-done | bytes 65568 | tf_op jit(solution)/shard_map/ppermute | solution.py:275
  118.5 1.3 collective-permute-start.17
  120.7 2.0 %collective-permute-start.20 = (bf16[64,4096]{1,0:T(8,128)(2,1)S(1)}, bf16[64,4096]{1,0:T(8,128)(2,1)S(1)}, u32[]{:S(2)}, u32[]{:S(2)}) collective-permute-start(bf16[64,4096]{1,0:T(8,128)(2,1)S(1)} %get-tuple-element.46.rest_0_), channel_id=1, source_target_pairs={{0,12},{1,13},{2,14},{3,15},{4,0},{5,1},{6,2},{7,3},{8,4},{9,5},{1... | collective-permute-start | bytes 1572872 | tf_op jit(solution)/shard_map/ppermute | solution.py:286
  122.7 2.0 %collective-permute-start.21 = (bf16[64,4096]{1,0:T(8,128)(2,1)S(1)}, bf16[64,4096]{1,0:T(8,128)(2,1)S(1)}, u32[]{:S(2)}, u32[]{:S(2)}) collective-permute-start(bf16[64,4096]{1,0:T(8,128)(2,1)S(1)} %get-tuple-element.47.rest_4_), channel_id=1, source_target_pairs={{0,1},{1,2},{2,3},{3,0},{4,5},{5,6},{6,7},{7,4},{8,9},{9,10},{10,1... | collective-permute-start | bytes 1572872 | tf_op jit(solution)/shard_map/ppermute | solution.py:282
  124.7 2.9 %collective-permute-start.22 = (bf16[64,4096]{1,0:T(8,128)(2,1)S(1)}, bf16[64,4096]{1,0:T(8,128)(2,1)S(1)}, u32[]{:S(2)}, u32[]{:S(2)}) collective-permute-start(bf16[64,4096]{1,0:T(8,128)(2,1)S(1)} %get-tuple-element.47.rest_4_), channel_id=1, source_target_pairs={{0,2},{1,3},{2,0},{3,1},{4,6},{5,7},{6,4},{7,5},{8,10},{9,11},{10,... | collective-permute-start | bytes 1572872 | tf_op jit(solution)/shard_map/ppermute | solution.py:282
  127.6 2.6 %collective-permute-done.18.rest_1_ = bf16[64,4096]{1,0:T(8,128)(2,1)S(1)} collective-permute-done((bf16[64,4096]{1,0:T(8,128)(2,1)S(1)}, bf16[64,4096]{1,0:T(8,128)(2,1)S(1)}, u32[]{:S(2)}, u32[]{:S(2)}) %collective-permute-start.18) | collective-permute-done | bytes 524320 | tf_op jit(solution)/shard_map/ppermute | solution.py:286
  130.2 3.1 %collective-permute-start.23 = (bf16[64,4096]{1,0:T(8,128)(2,1)S(1)}, bf16[64,4096]{1,0:T(8,128)(2,1)S(1)}, u32[]{:S(2)}, u32[]{:S(2)}) collective-permute-start(bf16[64,4096]{1,0:T(8,128)(2,1)S(1)} %get-tuple-element.47.rest_4_), channel_id=1, source_target_pairs={{0,3},{1,0},{2,1},{3,2},{4,7},{5,4},{6,5},{7,6},{8,11},{9,8},{10,9... | collective-permute-start | bytes 1572872 | tf_op jit(solution)/shard_map/ppermute | solution.py:282
  133.3 8.1 %collective-permute-done.19.rest_2_ = bf16[64,4096]{1,0:T(8,128)(2,1)S(1)} collective-permute-done((bf16[64,4096]{1,0:T(8,128)(2,1)S(1)}, bf16[64,4096]{1,0:T(8,128)(2,1)S(1)}, u32[]{:S(2)}, u32[]{:S(2)}) %collective-permute-start.19) | collective-permute-done | bytes 524320 | tf_op jit(solution)/shard_map/ppermute | solution.py:286
  141.5 3.3 %collective-permute-done.20.rest_3_ = bf16[64,4096]{1,0:T(8,128)(2,1)S(1)} collective-permute-done((bf16[64,4096]{1,0:T(8,128)(2,1)S(1)}, bf16[64,4096]{1,0:T(8,128)(2,1)S(1)}, u32[]{:S(2)}, u32[]{:S(2)}) %collective-permute-start.20) | collective-permute-done | bytes 524320 | tf_op jit(solution)/shard_map/ppermute | solution.py:286
  144.8 3.8 %collective-permute-done.22.rest_6_ = bf16[64,4096]{1,0:T(8,128)(2,1)S(1)} collective-permute-done((bf16[64,4096]{1,0:T(8,128)(2,1)S(1)}, bf16[64,4096]{1,0:T(8,128)(2,1)S(1)}, u32[]{:S(2)}, u32[]{:S(2)}) %collective-permute-start.22) | collective-permute-done | bytes 524320 | tf_op jit(solution)/shard_map/ppermute | solution.py:282
  149.3 1.8 level3.1
  151.2 1.3 collective-permute-done.24
  152.5 4.3 %collective-permute-done.25 = bf16[8,4096]{1,0:T(8,128)(2,1)S(1)} collective-permute-done((bf16[8,4096]{1,0:T(8,128)(2,1)S(1)}, bf16[8,4096]{1,0:T(8,128)(2,1)S(1)}, u32[]{:S(2)}, u32[]{:S(2)}) %collective-permute-start.25) | collective-permute-done | bytes 65568 | tf_op jit(solution)/shard_map/ppermute | solution.py:275
  156.8 1.4 collective-permute-start.26
  158.2 4.1 %collective-permute-done.26.other_ref = bf16[8,4096]{1,0:T(8,128)(2,1)S(1)} collective-permute-done((bf16[8,4096]{1,0:T(8,128)(2,1)S(1)}, bf16[8,4096]{1,0:T(8,128)(2,1)S(1)}, u32[]{:S(2)}, u32[]{:S(2)}) %collective-permute-start.26) | collective-permute-done | bytes 65568 | tf_op jit(solution)/shard_map/ppermute | solution.py:275
  162.4 1.2 shard_map.48
  163.6 1.2 collective-permute-done.27
  164.9 3.9 %collective-permute-done.28.other_ref = bf16[8,2048]{1,0:T(8,128)(2,1)S(1)} collective-permute-done((bf16[8,2048]{1,0:T(8,128)(2,1)S(1)}, bf16[8,2048]{1,0:T(8,128)(2,1)S(1)}, u32[]{:S(2)}, u32[]{:S(2)}) %collective-permute-start.28) | collective-permute-done | bytes 32800 | tf_op jit(solution)/shard_map/ppermute | solution.py:275
  169.4 1.2 collective-permute-done.29.other_ref
  171.0 13.0 %all_to_all.15 = f32[16,8,128]{2,1,0:T(8,128)S(1)} all-to-all(f32[16,8,128]{2,1,0:T(8,128)S(1)} %pack.1), channel_id=1, replica_groups=mesh['leaf'=8,'tile'=16] {'tile'}, dimensions={0} | all-to-all | bytes 131072 | tf_op jit(solution)/shard_map/all_to_all | solution.py:397
  (45 shorter events, 10.6 us)
Async XLA Ops:
  0.0 0.9 copy-start
  0.9 0.7 copy-start.2
  2.9 10.7 %all-to-all-start = ((bf16[8,32,256]{2,1,0:T(8,128)(2,1)}), bf16[8,32,256]{2,1,0:T(8,128)(2,1)S(1)}, u32[]{:S(2)}, u32[]{:S(2)}) async-start(bf16[8,32,256]{2,1,0:T(8,128)(2,1)} %split_couplings.1), calls=%async_computation | async-start | bytes 262144 | tf_op jit(solution)/shard_map/all_to_all | solution.py:320
  13.5 0.8 copy-start.1
  14.4 9.1 %copy-start.3 = (bf16[32,7680]{1,0:T(8,128)(2,1)S(1)}, bf16[32,7680]{1,0:T(8,128)(2,1)}, u32[]{:S(2)}) copy-start(bf16[32,7680]{1,0:T(8,128)(2,1)} %param.5) | copy-start | bytes 1474564
  15.6 65.7 %all-to-all-start.1 = ((bf16[16,304,128]{2,1,0:T(8,128)(2,1)}), bf16[16,304,128]{2,1,0:T(8,128)(2,1)S(1)}, u32[]{:S(2)}, u32[]{:S(2)}) async-start(bf16[16,304,128]{2,1,0:T(8,128)(2,1)} %message.1), calls=%async_computation.1 | async-start | bytes 2490368 | tf_op jit(solution)/shard_map/all_to_all | solution.py:330
  23.6 23.1 %collective-permute-start.3 = (bf16[16,7680]{1,0:T(8,128)(2,1)S(1)}, bf16[16,7680]{1,0:T(8,128)(2,1)S(1)}, u32[]{:S(2)}, u32[]{:S(2)}) collective-permute-start(bf16[16,7680]{1,0:T(8,128)(2,1)S(1)} %get-tuple-element.59.refs_0_), channel_id=1, source_target_pairs={{0,4},{1,5},{2,6},{3,7},{4,8},{5,9},{6,10},{7,11},{8,12},{9,13},{1... | collective-permute-start | bytes 737288 | tf_op jit(solution)/shard_map/ppermute | solution.py:286
  25.6 25.4 %collective-permute-start.4 = (bf16[16,7680]{1,0:T(8,128)(2,1)S(1)}, bf16[16,7680]{1,0:T(8,128)(2,1)S(1)}, u32[]{:S(2)}, u32[]{:S(2)}) collective-permute-start(bf16[16,7680]{1,0:T(8,128)(2,1)S(1)} %get-tuple-element.59.refs_0_), channel_id=1, source_target_pairs={{0,8},{1,9},{2,10},{3,11},{4,12},{5,13},{6,14},{7,15},{8,0},{9,1},... | collective-permute-start | bytes 737288 | tf_op jit(solution)/shard_map/ppermute | solution.py:286
  28.2 22.7 %collective-permute-start.5 = (bf16[16,7680]{1,0:T(8,128)(2,1)S(1)}, bf16[16,7680]{1,0:T(8,128)(2,1)S(1)}, u32[]{:S(2)}, u32[]{:S(2)}) collective-permute-start(bf16[16,7680]{1,0:T(8,128)(2,1)S(1)} %get-tuple-element.59.refs_0_), channel_id=1, source_target_pairs={{0,12},{1,13},{2,14},{3,15},{4,0},{5,1},{6,2},{7,3},{8,4},{9,5},{1... | collective-permute-start | bytes 737288 | tf_op jit(solution)/shard_map/ppermute | solution.py:286
  51.0 28.2 %collective-permute-start.10 = (bf16[64,3584]{1,0:T(8,128)(2,1)S(1)}, bf16[64,3584]{1,0:T(8,128)(2,1)S(1)}, u32[]{:S(2)}, u32[]{:S(2)}) collective-permute-start(bf16[64,3584]{1,0:T(8,128)(2,1)S(1)} %get-tuple-element.36.rest_4_), channel_id=1, source_target_pairs={{0,2},{1,3},{2,0},{3,1},{4,6},{5,7},{6,4},{7,5},{8,10},{9,11},{10,... | collective-permute-start | bytes 1376264 | tf_op jit(solution)/shard_map/ppermute | solution.py:282
  54.1 17.2 %collective-permute-start = (bf16[16,7680]{1,0:T(8,128)(2,1)S(1)}, bf16[16,7680]{1,0:T(8,128)(2,1)S(1)}, u32[]{:S(2)}, u32[]{:S(2)}) collective-permute-start(bf16[16,7680]{1,0:T(8,128)(2,1)S(1)} %get-tuple-element.60.refs_0_), channel_id=1, source_target_pairs={{0,1},{1,2},{2,3},{3,0},{4,5},{5,6},{6,7},{7,4},{8,9},{9,10},{10,1... | collective-permute-start | bytes 737288 | tf_op jit(solution)/shard_map/ppermute | solution.py:282
  54.7 21.9 %collective-permute-start.1 = (bf16[16,7680]{1,0:T(8,128)(2,1)S(1)}, bf16[16,7680]{1,0:T(8,128)(2,1)S(1)}, u32[]{:S(2)}, u32[]{:S(2)}) collective-permute-start(bf16[16,7680]{1,0:T(8,128)(2,1)S(1)} %get-tuple-element.60.refs_0_), channel_id=1, source_target_pairs={{0,2},{1,3},{2,0},{3,1},{4,6},{5,7},{6,4},{7,5},{8,10},{9,11},{10,... | collective-permute-start | bytes 737288 | tf_op jit(solution)/shard_map/ppermute | solution.py:282
  56.7 19.9 %collective-permute-start.2 = (bf16[16,7680]{1,0:T(8,128)(2,1)S(1)}, bf16[16,7680]{1,0:T(8,128)(2,1)S(1)}, u32[]{:S(2)}, u32[]{:S(2)}) collective-permute-start(bf16[16,7680]{1,0:T(8,128)(2,1)S(1)} %get-tuple-element.60.refs_0_), channel_id=1, source_target_pairs={{0,3},{1,0},{2,1},{3,2},{4,7},{5,4},{6,5},{7,6},{8,11},{9,8},{10,9... | collective-permute-start | bytes 737288 | tf_op jit(solution)/shard_map/ppermute | solution.py:282
  57.3 27.4 %collective-permute-start.11 = (bf16[64,3584]{1,0:T(8,128)(2,1)S(1)}, bf16[64,3584]{1,0:T(8,128)(2,1)}, u32[]{:S(2)}, u32[]{:S(2)}) collective-permute-start(bf16[64,3584]{1,0:T(8,128)(2,1)S(1)} %get-tuple-element.36.rest_4_), channel_id=1, source_target_pairs={{0,3},{1,0},{2,1},{3,2},{4,7},{5,4},{6,5},{7,6},{8,11},{9,8},{10,9... | collective-permute-start | bytes 1376264 | tf_op jit(solution)/shard_map/ppermute | solution.py:282
  71.2 14.5 %collective-permute-start.9 = (bf16[64,3584]{1,0:T(8,128)(2,1)S(1)}, bf16[64,3584]{1,0:T(8,128)(2,1)}, u32[]{:S(2)}, u32[]{:S(2)}) collective-permute-start(bf16[64,3584]{1,0:T(8,128)(2,1)S(1)} %get-tuple-element.36.rest_4_), channel_id=1, source_target_pairs={{0,1},{1,2},{2,3},{3,0},{4,5},{5,6},{6,7},{7,4},{8,9},{9,10},{10,1... | collective-permute-start | bytes 1376264 | tf_op jit(solution)/shard_map/ppermute | solution.py:282
  77.5 21.4 %collective-permute-start.6 = (bf16[64,3584]{1,0:T(8,128)(2,1)}, bf16[64,3584]{1,0:T(8,128)(2,1)}, u32[]{:S(2)}, u32[]{:S(2)}) collective-permute-start(bf16[64,3584]{1,0:T(8,128)(2,1)} %get-tuple-element.35.rest_0_), channel_id=1, source_target_pairs={{0,4},{1,5},{2,6},{3,7},{4,8},{5,9},{6,10},{7,11},{8,12},{9,13},{1... | collective-permute-start | bytes 1376264 | tf_op jit(solution)/shard_map/ppermute | solution.py:286
  77.5 21.4 %collective-permute-start.7 = (bf16[64,3584]{1,0:T(8,128)(2,1)}, bf16[64,3584]{1,0:T(8,128)(2,1)}, u32[]{:S(2)}, u32[]{:S(2)}) collective-permute-start(bf16[64,3584]{1,0:T(8,128)(2,1)} %get-tuple-element.35.rest_0_), channel_id=1, source_target_pairs={{0,8},{1,9},{2,10},{3,11},{4,12},{5,13},{6,14},{7,15},{8,0},{9,1},... | collective-permute-start | bytes 1376264 | tf_op jit(solution)/shard_map/ppermute | solution.py:286
  79.3 20.3 %collective-permute-start.8 = (bf16[64,3584]{1,0:T(8,128)(2,1)}, bf16[64,3584]{1,0:T(8,128)(2,1)}, u32[]{:S(2)}, u32[]{:S(2)}) collective-permute-start(bf16[64,3584]{1,0:T(8,128)(2,1)} %get-tuple-element.35.rest_0_), channel_id=1, source_target_pairs={{0,12},{1,13},{2,14},{3,15},{4,0},{5,1},{6,2},{7,3},{8,4},{9,5},{1... | collective-permute-start | bytes 1376264 | tf_op jit(solution)/shard_map/ppermute | solution.py:286
  103.1 1.2 collective-permute-start.12
  105.3 1.2 collective-permute-start.13
  106.6 4.0 %collective-permute-start.14 = (bf16[8,2048]{1,0:T(8,128)(2,1)S(1)}, bf16[8,2048]{1,0:T(8,128)(2,1)S(1)}, u32[]{:S(2)}, u32[]{:S(2)}) collective-permute-start(bf16[8,2048]{1,0:T(8,128)(2,1)S(1)} %add_convert_fusion.5.own_ref), channel_id=1, source_target_pairs={{0,32},{16,48},{32,0},{48,16},{64,96},{80,112},{96,64},{112,80},{1... | collective-permute-start | bytes 98312 | tf_op jit(solution)/shard_map/ppermute | solution.py:275
  112.8 1.3 collective-permute-start.15
  114.1 4.3 %collective-permute-start.16 = (bf16[8,4096]{1,0:T(8,128)(2,1)S(1)}, bf16[8,4096]{1,0:T(8,128)(2,1)S(1)}, u32[]{:S(2)}, u32[]{:S(2)}) collective-permute-start(bf16[8,4096]{1,0:T(8,128)(2,1)S(1)} %add_convert_fusion.3), channel_id=1, source_target_pairs={{0,32},{16,48},{32,0},{48,16},{64,96},{80,112},{96,64},{112,80},{1... | collective-permute-start | bytes 196616 | tf_op jit(solution)/shard_map/ppermute | solution.py:275
  114.8 15.5 %collective-permute-start.18 = (bf16[64,4096]{1,0:T(8,128)(2,1)S(1)}, bf16[64,4096]{1,0:T(8,128)(2,1)S(1)}, u32[]{:S(2)}, u32[]{:S(2)}) collective-permute-start(bf16[64,4096]{1,0:T(8,128)(2,1)S(1)} %get-tuple-element.46.rest_0_), channel_id=1, source_target_pairs={{0,4},{1,5},{2,6},{3,7},{4,8},{5,9},{6,10},{7,11},{8,12},{9,13},{1... | collective-permute-start | bytes 1572872 | tf_op jit(solution)/shard_map/ppermute | solution.py:286
  118.5 6.2 %collective-permute-start.17 = (bf16[8,4096]{1,0:T(8,128)(2,1)S(1)}, bf16[8,4096]{1,0:T(8,128)(2,1)S(1)}, u32[]{:S(2)}, u32[]{:S(2)}) collective-permute-start(bf16[8,4096]{1,0:T(8,128)(2,1)S(1)} %add_convert_fusion.2.own_ref), channel_id=1, source_target_pairs={{0,96},{16,112},{32,64},{48,80},{64,32},{80,48},{96,0},{112,16},{1... | collective-permute-start | bytes 196616 | tf_op jit(solution)/shard_map/ppermute | solution.py:275
  119.7 21.7 %collective-permute-start.19 = (bf16[64,4096]{1,0:T(8,128)(2,1)S(1)}, bf16[64,4096]{1,0:T(8,128)(2,1)S(1)}, u32[]{:S(2)}, u32[]{:S(2)}) collective-permute-start(bf16[64,4096]{1,0:T(8,128)(2,1)S(1)} %get-tuple-element.46.rest_0_), channel_id=1, source_target_pairs={{0,8},{1,9},{2,10},{3,11},{4,12},{5,13},{6,14},{7,15},{8,0},{9,1},... | collective-permute-start | bytes 1572872 | tf_op jit(solution)/shard_map/ppermute | solution.py:286
  120.7 24.1 %collective-permute-start.20 = (bf16[64,4096]{1,0:T(8,128)(2,1)S(1)}, bf16[64,4096]{1,0:T(8,128)(2,1)S(1)}, u32[]{:S(2)}, u32[]{:S(2)}) collective-permute-start(bf16[64,4096]{1,0:T(8,128)(2,1)S(1)} %get-tuple-element.46.rest_0_), channel_id=1, source_target_pairs={{0,12},{1,13},{2,14},{3,15},{4,0},{5,1},{6,2},{7,3},{8,4},{9,5},{1... | collective-permute-start | bytes 1572872 | tf_op jit(solution)/shard_map/ppermute | solution.py:286
  122.7 22.1 %collective-permute-start.21 = (bf16[64,4096]{1,0:T(8,128)(2,1)S(1)}, bf16[64,4096]{1,0:T(8,128)(2,1)S(1)}, u32[]{:S(2)}, u32[]{:S(2)}) collective-permute-start(bf16[64,4096]{1,0:T(8,128)(2,1)S(1)} %get-tuple-element.47.rest_4_), channel_id=1, source_target_pairs={{0,1},{1,2},{2,3},{3,0},{4,5},{5,6},{6,7},{7,4},{8,9},{9,10},{10,1... | collective-permute-start | bytes 1572872 | tf_op jit(solution)/shard_map/ppermute | solution.py:282
  124.7 23.9 %collective-permute-start.22 = (bf16[64,4096]{1,0:T(8,128)(2,1)S(1)}, bf16[64,4096]{1,0:T(8,128)(2,1)S(1)}, u32[]{:S(2)}, u32[]{:S(2)}) collective-permute-start(bf16[64,4096]{1,0:T(8,128)(2,1)S(1)} %get-tuple-element.47.rest_4_), channel_id=1, source_target_pairs={{0,2},{1,3},{2,0},{3,1},{4,6},{5,7},{6,4},{7,5},{8,10},{9,11},{10,... | collective-permute-start | bytes 1572872 | tf_op jit(solution)/shard_map/ppermute | solution.py:282
  130.2 19.1 %collective-permute-start.23 = (bf16[64,4096]{1,0:T(8,128)(2,1)S(1)}, bf16[64,4096]{1,0:T(8,128)(2,1)S(1)}, u32[]{:S(2)}, u32[]{:S(2)}) collective-permute-start(bf16[64,4096]{1,0:T(8,128)(2,1)S(1)} %get-tuple-element.47.rest_4_), channel_id=1, source_target_pairs={{0,3},{1,0},{2,1},{3,2},{4,7},{5,4},{6,5},{7,6},{8,11},{9,8},{10,9... | collective-permute-start | bytes 1572872 | tf_op jit(solution)/shard_map/ppermute | solution.py:282
  151.2 1.3 collective-permute-start.24
  152.4 4.3 %collective-permute-start.25 = (bf16[8,4096]{1,0:T(8,128)(2,1)S(1)}, bf16[8,4096]{1,0:T(8,128)(2,1)S(1)}, u32[]{:S(2)}, u32[]{:S(2)}) collective-permute-start(bf16[8,4096]{1,0:T(8,128)(2,1)S(1)} %add_convert_fusion.1), channel_id=1, source_target_pairs={{0,32},{16,48},{32,0},{48,16},{64,96},{80,112},{96,64},{112,80},{1... | collective-permute-start | bytes 196616 | tf_op jit(solution)/shard_map/ppermute | solution.py:275
  156.8 5.6 %collective-permute-start.26 = (bf16[8,4096]{1,0:T(8,128)(2,1)S(1)}, bf16[8,4096]{1,0:T(8,128)(2,1)S(1)}, u32[]{:S(2)}, u32[]{:S(2)}) collective-permute-start(bf16[8,4096]{1,0:T(8,128)(2,1)S(1)} %add_convert_fusion.own_ref), channel_id=1, source_target_pairs={{0,96},{16,112},{32,64},{48,80},{64,32},{80,48},{96,0},{112,16},{1... | collective-permute-start | bytes 196616 | tf_op jit(solution)/shard_map/ppermute | solution.py:275
  163.6 1.2 collective-permute-start.27
  164.8 4.0 %collective-permute-start.28 = (bf16[8,2048]{1,0:T(8,128)(2,1)S(1)}, bf16[8,2048]{1,0:T(8,128)(2,1)S(1)}, u32[]{:S(2)}, u32[]{:S(2)}) collective-permute-start(bf16[8,2048]{1,0:T(8,128)(2,1)S(1)} %add_convert_fusion.4.own_ref), channel_id=1, source_target_pairs={{0,32},{16,48},{32,0},{48,16},{64,96},{80,112},{96,64},{112,80},{1... | collective-permute-start | bytes 98312 | tf_op jit(solution)/shard_map/ppermute | solution.py:275
  169.4 1.2 collective-permute-start.29

commit v6 on v4

--- a/solution.py
+++ b/solution.py
@@ -262,7 +262,7 @@
     rolled = Rolled(tiles)
     for t in range(16):
         parts = [rolled.take(4 * v + t // 4, t % 4, v) for v in range(4)]
-        out_ref[t] = merge(parts, chunk)
+        out_ref[t] = merge(parts, chunk).astype(BF)
 
 
 def shape(dims, kind=BF):
@@ -402,14 +402,14 @@
     x1, x0 = back(0, xp, d0, y0, pending)
     packed = pl.pallas_call(
         pack_kernel,
-        out_shape=shape((16, 8, 128), F32),
+        out_shape=shape((16, 8, 128)),
         in_specs=[VMEM] * 4,
         out_specs=VMEM,
         compiler_params=params(),
         name="pack",
     )(x0, x1, x2, x3)
     packed = lax.all_to_all(packed, "tile", 0, 0, tiled=True)
-    return jnp.transpose(packed.reshape(128, 128)).reshape(4, 32, 128)
+    return jnp.transpose(packed.reshape(128, 128).astype(F32)).reshape(4, 32, 128)
 
 
 def solution(mesh):

time: 170 us -> 170 us (level)
  no operation moved by 1% of the time
where the time goes in v6:
time: 170 us
  waiting for transfers between devices  81.8 us (48%)
  starting transfers between devices  57.6 us (34%)
  Pallas kernels  13.8 us (8%)
  blocking collectives  11.6 us (7%)
  local copies, waits for them, and re-layouts  4.75 us (3%)
    ppermute x12, waiting for transfers between devices, shift_z(): lax.ppermute(values, 'tile', [(t, (t + 4 * by) % 16) for t in range(16)])  38 us
    ppermute x12, starting transfers between devices, shift_z(): lax.ppermute(values, 'tile', [(t, (t + 4 * by) % 16) for t in range(16)])  21.2 us
    ppermute x12, waiting for transfers between devices, reduce_over(): other = lax.ppermute(part, 'leaf', hops[n])  19.3 us
    ppermute x12, starting transfers between devices, shift_x(): lax.ppermute(values, 'tile', [(t, t // 4 * 4 + (t + by) % 4) for t in ran...  18.9 us
    ppermute x12, waiting for transfers between devices, shift_x(): lax.ppermute(values, 'tile', [(t, t // 4 * 4 + (t + by) % 4) for t in ran...  18.4 us
    all_to_all x1, blocking collectives, local(): packed = lax.all_to_all(packed, 'tile', 0, 0, tiled=True)  11.6 us
    all_to_all x1, starting transfers between devices, local(): message = lax.all_to_all(message, 'tile', 0, 0, tiled=True)  7.88 us
    all_to_all x1, waiting for transfers between devices, local(): columns = lax.all_to_all(split, 'leaf', 0, 0, tiled=True)  6.1 us
  transfers between devices with their start and end apart: 38, of which 23 were waited for; matrix products, arithmetic and copies ran while one was open for 0% of the time, Pallas kernels for 3%

profile of v6, /device:TPU:0, one launch (start us, length us, event | category | flops | bytes accessed | tf_op | source)
XLA Modules:
  0.0 169.9 jit_solution(1835731941802874262)
XLA Ops:
  1.5 1.3 split_couplings.1
  2.9 4.6 %all-to-all-start = ((bf16[8,32,256]{2,1,0:T(8,128)(2,1)}), bf16[8,32,256]{2,1,0:T(8,128)(2,1)S(1)}, u32[]{:S(2)}, u32[]{:S(2)}) async-start(bf16[8,32,256]{2,1,0:T(8,128)(2,1)} %split_couplings.1), calls=%async_computation | async-start | bytes 262144 | tf_op jit(solution)/shard_map/all_to_all | solution.py:325
  7.4 6.1 %all-to-all-done.columns_ref = bf16[8,32,256]{2,1,0:T(8,128)(2,1)S(1)} async-done(((bf16[8,32,256]{2,1,0:T(8,128)(2,1)}), bf16[8,32,256]{2,1,0:T(8,128)(2,1)S(1)}, u32[]{:S(2)}, u32[]{:S(2)}) %all-to-all-start) | async-done | bytes 131104 | tf_op jit(solution)/shard_map/all_to_all | solution.py:325
  14.4 1.3 message.1
  15.6 7.9 %all-to-all-start.1 = ((bf16[16,304,128]{2,1,0:T(8,128)(2,1)}), bf16[16,304,128]{2,1,0:T(8,128)(2,1)S(1)}, u32[]{:S(2)}, u32[]{:S(2)}) async-start(bf16[16,304,128]{2,1,0:T(8,128)(2,1)} %message.1), calls=%async_computation.1 | async-start | bytes 2490368 | tf_op jit(solution)/shard_map/all_to_all | solution.py:335
  23.6 2.0 %collective-permute-start.3 = (bf16[16,7680]{1,0:T(8,128)(2,1)S(1)}, bf16[16,7680]{1,0:T(8,128)(2,1)S(1)}, u32[]{:S(2)}, u32[]{:S(2)}) collective-permute-start(bf16[16,7680]{1,0:T(8,128)(2,1)S(1)} %get-tuple-element.61.refs_0_), channel_id=1, source_target_pairs={{0,4},{1,5},{2,6},{3,7},{4,8},{5,9},{6,10},{7,11},{8,12},{9,13},{1... | collective-permute-start | bytes 737288 | tf_op jit(solution)/shard_map/ppermute | solution.py:290
  25.6 2.7 %collective-permute-start.4 = (bf16[16,7680]{1,0:T(8,128)(2,1)S(1)}, bf16[16,7680]{1,0:T(8,128)(2,1)S(1)}, u32[]{:S(2)}, u32[]{:S(2)}) collective-permute-start(bf16[16,7680]{1,0:T(8,128)(2,1)S(1)} %get-tuple-element.61.refs_0_), channel_id=1, source_target_pairs={{0,8},{1,9},{2,10},{3,11},{4,12},{5,13},{6,14},{7,15},{8,0},{9,1},... | collective-permute-start | bytes 737288 | tf_op jit(solution)/shard_map/ppermute | solution.py:290
  28.2 1.5 collective-permute-start.5
  29.7 1.5 collective-permute-start
  31.2 2.7 %collective-permute-start.1 = (bf16[16,7680]{1,0:T(8,128)(2,1)S(1)}, bf16[16,7680]{1,0:T(8,128)(2,1)S(1)}, u32[]{:S(2)}, u32[]{:S(2)}) collective-permute-start(bf16[16,7680]{1,0:T(8,128)(2,1)S(1)} %get-tuple-element.62.refs_0_), channel_id=1, source_target_pairs={{0,2},{1,3},{2,0},{3,1},{4,6},{5,7},{6,4},{7,5},{8,10},{9,11},{10,... | collective-permute-start | bytes 737288 | tf_op jit(solution)/shard_map/ppermute | solution.py:286
  33.8 12.9 %collective-permute-done.3.refs_1_ = bf16[16,7680]{1,0:T(8,128)(2,1)S(1)} collective-permute-done((bf16[16,7680]{1,0:T(8,128)(2,1)S(1)}, bf16[16,7680]{1,0:T(8,128)(2,1)S(1)}, u32[]{:S(2)}, u32[]{:S(2)}) %collective-permute-start.3) | collective-permute-done | bytes 245792 | tf_op jit(solution)/shard_map/ppermute | solution.py:290
  46.7 2.0 %collective-permute-start.2 = (bf16[16,7680]{1,0:T(8,128)(2,1)S(1)}, bf16[16,7680]{1,0:T(8,128)(2,1)S(1)}, u32[]{:S(2)}, u32[]{:S(2)}) collective-permute-start(bf16[16,7680]{1,0:T(8,128)(2,1)S(1)} %get-tuple-element.62.refs_0_), channel_id=1, source_target_pairs={{0,3},{1,0},{2,1},{3,2},{4,7},{5,4},{6,5},{7,6},{8,11},{9,8},{10,9... | collective-permute-start | bytes 737288 | tf_op jit(solution)/shard_map/ppermute | solution.py:286
  48.7 2.2 %collective-permute-done.4.refs_2_ = bf16[16,7680]{1,0:T(8,128)(2,1)S(1)} collective-permute-done((bf16[16,7680]{1,0:T(8,128)(2,1)S(1)}, bf16[16,7680]{1,0:T(8,128)(2,1)S(1)}, u32[]{:S(2)}, u32[]{:S(2)}) %collective-permute-start.4) | collective-permute-done | bytes 245792 | tf_op jit(solution)/shard_map/ppermute | solution.py:290
  51.0 3.0 %collective-permute-start.10 = (bf16[64,1536]{1,0:T(8,128)(2,1)S(1)}, bf16[64,1536]{1,0:T(8,128)(2,1)S(1)}, u32[]{:S(2)}, u32[]{:S(2)}) collective-permute-start(bf16[64,1536]{1,0:T(8,128)(2,1)S(1)} %get-tuple-element.37.rest_4_), channel_id=1, source_target_pairs={{0,2},{1,3},{2,0},{3,1},{4,6},{5,7},{6,4},{7,5},{8,10},{9,11},{10,... | collective-permute-start | bytes 589832 | tf_op jit(solution)/shard_map/ppermute | solution.py:286
  57.4 3.0 %collective-permute-done.10.rest_6_ = bf16[64,1536]{1,0:T(8,128)(2,1)S(1)} collective-permute-done((bf16[64,1536]{1,0:T(8,128)(2,1)S(1)}, bf16[64,1536]{1,0:T(8,128)(2,1)S(1)}, u32[]{:S(2)}, u32[]{:S(2)}) %collective-permute-start.10) | collective-permute-done | bytes 196640 | tf_op jit(solution)/shard_map/ppermute | solution.py:286
  60.4 1.2 collective-permute-start.7
  61.6 1.2 collective-permute-done.11.rest_7_
  63.5 1.3 collective-permute-start.8
  64.8 4.3 %collective-permute-done.9.rest_5_ = bf16[64,1536]{1,0:T(8,128)(2,1)} collective-permute-done((bf16[64,1536]{1,0:T(8,128)(2,1)S(1)}, bf16[64,1536]{1,0:T(8,128)(2,1)}, u32[]{:S(2)}, u32[]{:S(2)}) %collective-permute-start.9) | collective-permute-done | bytes 196640 | tf_op jit(solution)/shard_map/ppermute | solution.py:286
  70.7 3.0 %level0.1 = (f32[4,8,512]{2,1,0:T(8,128)S(1)}, bf16[34,4,128,128]{3,2,1,0:T(8,128)(2,1)S(1)}, bf16[512,512]{1,0:T(8,128)(2,1)S(1)}, bf16[512,1024]{1,0:T(8,128)(...) custom-call(s32[1]{0:T(128)} %bitcast.leaf_ref, s32[1]{0:T(128)} %bitcast.1.place_ref, ...), custom_call_target="tpu_custom_call" | custom-call | tf_op jit(solution)/shard_map/level0/pallas_call | solution.py:353
  76.1 3.2 %collective-permute-start.19 = (bf16[64,2048]{1,0:T(8,128)(2,1)S(1)}, bf16[64,2048]{1,0:T(8,128)(2,1)S(1)}, u32[]{:S(2)}, u32[]{:S(2)}) collective-permute-start(bf16[64,2048]{1,0:T(8,128)(2,1)S(1)} %get-tuple-element.45.rest_4_), channel_id=1, source_target_pairs={{0,2},{1,3},{2,0},{3,1},{4,6},{5,7},{6,4},{7,5},{8,10},{9,11},{10,... | collective-permute-start | bytes 786440 | tf_op jit(solution)/shard_map/ppermute | solution.py:286
  79.3 1.8 %collective-permute-start.20 = (bf16[64,2048]{1,0:T(8,128)(2,1)S(1)}, bf16[64,2048]{1,0:T(8,128)(2,1)S(1)}, u32[]{:S(2)}, u32[]{:S(2)}) collective-permute-start(bf16[64,2048]{1,0:T(8,128)(2,1)S(1)} %get-tuple-element.45.rest_4_), channel_id=1, source_target_pairs={{0,3},{1,0},{2,1},{3,2},{4,7},{5,4},{6,5},{7,6},{8,11},{9,8},{10,9... | collective-permute-start | bytes 786440 | tf_op jit(solution)/shard_map/ppermute | solution.py:286
  81.1 2.8 %collective-permute-start.15 = (bf16[64,2048]{1,0:T(8,128)(2,1)S(1)}, bf16[64,2048]{1,0:T(8,128)(2,1)S(1)}, u32[]{:S(2)}, u32[]{:S(2)}) collective-permute-start(bf16[64,2048]{1,0:T(8,128)(2,1)S(1)} %get-tuple-element.44.rest_0_), channel_id=1, source_target_pairs={{0,4},{1,5},{2,6},{3,7},{4,8},{5,9},{6,10},{7,11},{8,12},{9,13},{1... | collective-permute-start | bytes 786440 | tf_op jit(solution)/shard_map/ppermute | solution.py:290
  85.1 1.8 %collective-permute-start.17 = (bf16[64,2048]{1,0:T(8,128)(2,1)S(1)}, bf16[64,2048]{1,0:T(8,128)(2,1)S(1)}, u32[]{:S(2)}, u32[]{:S(2)}) collective-permute-start(bf16[64,2048]{1,0:T(8,128)(2,1)S(1)} %get-tuple-element.44.rest_0_), channel_id=1, source_target_pairs={{0,12},{1,13},{2,14},{3,15},{4,0},{5,1},{6,2},{7,3},{8,4},{9,5},{1... | collective-permute-start | bytes 786440 | tf_op jit(solution)/shard_map/ppermute | solution.py:290
  87.5 5.4 %collective-permute-done.20.rest_7_ = bf16[64,2048]{1,0:T(8,128)(2,1)S(1)} collective-permute-done((bf16[64,2048]{1,0:T(8,128)(2,1)S(1)}, bf16[64,2048]{1,0:T(8,128)(2,1)S(1)}, u32[]{:S(2)}, u32[]{:S(2)}) %collective-permute-start.20) | collective-permute-done | bytes 262176 | tf_op jit(solution)/shard_map/ppermute | solution.py:286
  92.9 3.8 %collective-permute-done.16.rest_2_ = bf16[64,2048]{1,0:T(8,128)(2,1)S(1)} collective-permute-done((bf16[64,2048]{1,0:T(8,128)(2,1)S(1)}, bf16[64,2048]{1,0:T(8,128)(2,1)S(1)}, u32[]{:S(2)}, u32[]{:S(2)}) %collective-permute-start.16) | collective-permute-done | bytes 262176 | tf_op jit(solution)/shard_map/ppermute | solution.py:290
  96.8 2.3 %shard_map.47 = (bf16[8,512]{1,0:T(8,128)(2,1)S(1)}, bf16[8,4096]{1,0:T(8,128)(2,1)S(1)}) custom-call(s32[1]{0:T(128)} %bitcast.leaf_ref, bf16[8,2048]{1,0:T(8,128)(2,1)S(1)} %add_convert_fusion.5.own_ref, bf16[8,2048]{1,0:T(8,128)(2,1)S(1)} %collective-permute-done.14.other_ref, bf16[512,2048]{1,0:T(8,128)(2,1)S(1)} %order2.1.d_ref, ...), custom_call_target="tpu_custom_call" | custom-call | tf_op jit(solution)/shard_map/pallas_call | solution.py:367
  99.1 1.3 collective-permute-done.21
  101.0 2.1 %collective-permute-start.24 = (bf16[64,4096]{1,0:T(8,128)(2,1)S(1)}, bf16[64,4096]{1,0:T(8,128)(2,1)S(1)}, u32[]{:S(2)}, u32[]{:S(2)}) collective-permute-start(bf16[64,4096]{1,0:T(8,128)(2,1)S(1)} %get-tuple-element.48.rest_0_), channel_id=1, source_target_pairs={{0,4},{1,5},{2,6},{3,7},{4,8},{5,9},{6,10},{7,11},{8,12},{9,13},{1... | collective-permute-start | bytes 1572872 | tf_op jit(solution)/shard_map/ppermute | solution.py:290
  103.1 1.6 collective-permute-done.22
  104.8 1.2 collective-permute-start.23
  106.0 3.1 %collective-permute-start.25 = (bf16[64,4096]{1,0:T(8,128)(2,1)S(1)}, bf16[64,4096]{1,0:T(8,128)(2,1)S(1)}, u32[]{:S(2)}, u32[]{:S(2)}) collective-permute-start(bf16[64,4096]{1,0:T(8,128)(2,1)S(1)} %get-tuple-element.48.rest_0_), channel_id=1, source_target_pairs={{0,8},{1,9},{2,10},{3,11},{4,12},{5,13},{6,14},{7,15},{8,0},{9,1},... | collective-permute-start | bytes 1572872 | tf_op jit(solution)/shard_map/ppermute | solution.py:290
  109.1 1.7 %collective-permute-start.26 = (bf16[64,4096]{1,0:T(8,128)(2,1)S(1)}, bf16[64,4096]{1,0:T(8,128)(2,1)S(1)}, u32[]{:S(2)}, u32[]{:S(2)}) collective-permute-start(bf16[64,4096]{1,0:T(8,128)(2,1)S(1)} %get-tuple-element.48.rest_0_), channel_id=1, source_target_pairs={{0,12},{1,13},{2,14},{3,15},{4,0},{5,1},{6,2},{7,3},{8,4},{9,5},{1... | collective-permute-start | bytes 1572872 | tf_op jit(solution)/shard_map/ppermute | solution.py:290
  110.8 1.7 %collective-permute-start.28 = (bf16[64,4096]{1,0:T(8,128)(2,1)S(1)}, bf16[64,4096]{1,0:T(8,128)(2,1)S(1)}, u32[]{:S(2)}, u32[]{:S(2)}) collective-permute-start(bf16[64,4096]{1,0:T(8,128)(2,1)S(1)} %get-tuple-element.49.rest_4_), channel_id=1, source_target_pairs={{0,2},{1,3},{2,0},{3,1},{4,6},{5,7},{6,4},{7,5},{8,10},{9,11},{10,... | collective-permute-start | bytes 1572872 | tf_op jit(solution)/shard_map/ppermute | solution.py:286
  112.5 3.7 %collective-permute-done.24.rest_1_ = bf16[64,4096]{1,0:T(8,128)(2,1)S(1)} collective-permute-done((bf16[64,4096]{1,0:T(8,128)(2,1)S(1)}, bf16[64,4096]{1,0:T(8,128)(2,1)S(1)}, u32[]{:S(2)}, u32[]{:S(2)}) %collective-permute-start.24) | collective-permute-done | bytes 524320 | tf_op jit(solution)/shard_map/ppermute | solution.py:290
  116.5 11.5 %collective-permute-done.25.rest_2_ = bf16[64,4096]{1,0:T(8,128)(2,1)S(1)} collective-permute-done((bf16[64,4096]{1,0:T(8,128)(2,1)S(1)}, bf16[64,4096]{1,0:T(8,128)(2,1)S(1)}, u32[]{:S(2)}, u32[]{:S(2)}) %collective-permute-start.25) | collective-permute-done | bytes 524320 | tf_op jit(solution)/shard_map/ppermute | solution.py:290
  128.0 3.3 %collective-permute-done.26.rest_3_ = bf16[64,4096]{1,0:T(8,128)(2,1)S(1)} collective-permute-done((bf16[64,4096]{1,0:T(8,128)(2,1)S(1)}, bf16[64,4096]{1,0:T(8,128)(2,1)S(1)}, u32[]{:S(2)}, u32[]{:S(2)}) %collective-permute-start.26) | collective-permute-done | bytes 524320 | tf_op jit(solution)/shard_map/ppermute | solution.py:290
  131.3 4.0 %collective-permute-done.27.rest_5_ = bf16[64,4096]{1,0:T(8,128)(2,1)S(1)} collective-permute-done((bf16[64,4096]{1,0:T(8,128)(2,1)S(1)}, bf16[64,4096]{1,0:T(8,128)(2,1)S(1)}, u32[]{:S(2)}, u32[]{:S(2)}) %collective-permute-start.27) | collective-permute-done | bytes 524320 | tf_op jit(solution)/shard_map/ppermute | solution.py:286
  135.9 1.8 %level3.1 = bf16[8,4096]{1,0:T(8,128)(2,1)S(1)} custom-call(bf16[8,4096]{1,0:T(8,128)(2,1)S(1)} %add_convert_fusion.2.own_ref, bf16[8,4096]{1,0:T(8,128)(2,1)S(1)} %collective-permute-done.23.other_ref, bf16[64,4096]{1,0:T(8,128)(2,1)S(1)} %get-tuple-element.48.rest_0_, bf16[64,4096]{1,0:T(8,128)(2,1)S(1)} %collective-permute-done.24.rest_1_, ...), custom_call_target="tpu_custom_call" | custom-call | tf_op jit(solution)/shard_map/level3/pallas_call | solution.py:378
  137.7 1.3 collective-permute-done.30
  139.0 4.3 %collective-permute-done.31 = bf16[8,4096]{1,0:T(8,128)(2,1)S(1)} collective-permute-done((bf16[8,4096]{1,0:T(8,128)(2,1)S(1)}, bf16[8,4096]{1,0:T(8,128)(2,1)S(1)}, u32[]{:S(2)}, u32[]{:S(2)}) %collective-permute-start.31) | collective-permute-done | bytes 65568 | tf_op jit(solution)/shard_map/ppermute | solution.py:279
  143.3 2.1 %collective-permute-start.32 = (bf16[8,4096]{1,0:T(8,128)(2,1)S(1)}, bf16[8,4096]{1,0:T(8,128)(2,1)S(1)}, u32[]{:S(2)}, u32[]{:S(2)}) collective-permute-start(bf16[8,4096]{1,0:T(8,128)(2,1)S(1)} %add_convert_fusion.own_ref), channel_id=1, source_target_pairs={{0,96},{16,112},{32,64},{48,80},{64,32},{80,48},{96,0},{112,16},{1... | collective-permute-start | bytes 196616 | tf_op jit(solution)/shard_map/ppermute | solution.py:279
  145.5 3.4 %collective-permute-done.32.other_ref = bf16[8,4096]{1,0:T(8,128)(2,1)S(1)} collective-permute-done((bf16[8,4096]{1,0:T(8,128)(2,1)S(1)}, bf16[8,4096]{1,0:T(8,128)(2,1)S(1)}, u32[]{:S(2)}, u32[]{:S(2)}) %collective-permute-start.32) | collective-permute-done | bytes 65568 | tf_op jit(solution)/shard_map/ppermute | solution.py:279
  148.9 1.2 shard_map.48
  150.1 1.2 collective-permute-done.33
  151.4 3.9 %collective-permute-done.34.other_ref = bf16[8,2048]{1,0:T(8,128)(2,1)S(1)} collective-permute-done((bf16[8,2048]{1,0:T(8,128)(2,1)S(1)}, bf16[8,2048]{1,0:T(8,128)(2,1)S(1)}, u32[]{:S(2)}, u32[]{:S(2)}) %collective-permute-start.34) | collective-permute-done | bytes 32800 | tf_op jit(solution)/shard_map/ppermute | solution.py:279
  155.9 1.2 collective-permute-done.35.other_ref
  157.5 11.6 %all_to_all.15 = bf16[16,8,128]{2,1,0:T(8,128)(2,1)S(1)} all-to-all(bf16[16,8,128]{2,1,0:T(8,128)(2,1)S(1)} %pack.1), channel_id=1, replica_groups=mesh['leaf'=8,'tile'=16] {'tile'}, dimensions={0} | all-to-all | bytes 65536 | tf_op jit(solution)/shard_map/all_to_all | solution.py:411
  (63 shorter events, 16.0 us)
Async XLA Ops:
  0.0 0.9 copy-start.2
  0.9 0.7 copy-start.4
  2.9 10.7 %all-to-all-start = ((bf16[8,32,256]{2,1,0:T(8,128)(2,1)}), bf16[8,32,256]{2,1,0:T(8,128)(2,1)S(1)}, u32[]{:S(2)}, u32[]{:S(2)}) async-start(bf16[8,32,256]{2,1,0:T(8,128)(2,1)} %split_couplings.1), calls=%async_computation | async-start | bytes 262144 | tf_op jit(solution)/shard_map/all_to_all | solution.py:325
  13.5 0.8 copy-start.3
  14.4 9.1 %copy-start.5 = (bf16[32,7680]{1,0:T(8,128)(2,1)S(1)}, bf16[32,7680]{1,0:T(8,128)(2,1)}, u32[]{:S(2)}) copy-start(bf16[32,7680]{1,0:T(8,128)(2,1)} %param.5) | copy-start | bytes 1474564
  15.6 49.2 %all-to-all-start.1 = ((bf16[16,304,128]{2,1,0:T(8,128)(2,1)}), bf16[16,304,128]{2,1,0:T(8,128)(2,1)S(1)}, u32[]{:S(2)}, u32[]{:S(2)}) async-start(bf16[16,304,128]{2,1,0:T(8,128)(2,1)} %message.1), calls=%async_computation.1 | async-start | bytes 2490368 | tf_op jit(solution)/shard_map/all_to_all | solution.py:335
  23.6 23.1 %collective-permute-start.3 = (bf16[16,7680]{1,0:T(8,128)(2,1)S(1)}, bf16[16,7680]{1,0:T(8,128)(2,1)S(1)}, u32[]{:S(2)}, u32[]{:S(2)}) collective-permute-start(bf16[16,7680]{1,0:T(8,128)(2,1)S(1)} %get-tuple-element.61.refs_0_), channel_id=1, source_target_pairs={{0,4},{1,5},{2,6},{3,7},{4,8},{5,9},{6,10},{7,11},{8,12},{9,13},{1... | collective-permute-start | bytes 737288 | tf_op jit(solution)/shard_map/ppermute | solution.py:290
  25.6 25.4 %collective-permute-start.4 = (bf16[16,7680]{1,0:T(8,128)(2,1)S(1)}, bf16[16,7680]{1,0:T(8,128)(2,1)S(1)}, u32[]{:S(2)}, u32[]{:S(2)}) collective-permute-start(bf16[16,7680]{1,0:T(8,128)(2,1)S(1)} %get-tuple-element.61.refs_0_), channel_id=1, source_target_pairs={{0,8},{1,9},{2,10},{3,11},{4,12},{5,13},{6,14},{7,15},{8,0},{9,1},... | collective-permute-start | bytes 737288 | tf_op jit(solution)/shard_map/ppermute | solution.py:290
  28.2 22.7 %collective-permute-start.5 = (bf16[16,7680]{1,0:T(8,128)(2,1)S(1)}, bf16[16,7680]{1,0:T(8,128)(2,1)S(1)}, u32[]{:S(2)}, u32[]{:S(2)}) collective-permute-start(bf16[16,7680]{1,0:T(8,128)(2,1)S(1)} %get-tuple-element.61.refs_0_), channel_id=1, source_target_pairs={{0,12},{1,13},{2,14},{3,15},{4,0},{5,1},{6,2},{7,3},{8,4},{9,5},{1... | collective-permute-start | bytes 737288 | tf_op jit(solution)/shard_map/ppermute | solution.py:290
  29.7 25.6 %collective-permute-start = (bf16[16,7680]{1,0:T(8,128)(2,1)S(1)}, bf16[16,7680]{1,0:T(8,128)(2,1)S(1)}, u32[]{:S(2)}, u32[]{:S(2)}) collective-permute-start(bf16[16,7680]{1,0:T(8,128)(2,1)S(1)} %get-tuple-element.62.refs_0_), channel_id=1, source_target_pairs={{0,1},{1,2},{2,3},{3,0},{4,5},{5,6},{6,7},{7,4},{8,9},{9,10},{10,1... | collective-permute-start | bytes 737288 | tf_op jit(solution)/shard_map/ppermute | solution.py:286
  31.2 24.9 %collective-permute-start.1 = (bf16[16,7680]{1,0:T(8,128)(2,1)S(1)}, bf16[16,7680]{1,0:T(8,128)(2,1)S(1)}, u32[]{:S(2)}, u32[]{:S(2)}) collective-permute-start(bf16[16,7680]{1,0:T(8,128)(2,1)S(1)} %get-tuple-element.62.refs_0_), channel_id=1, source_target_pairs={{0,2},{1,3},{2,0},{3,1},{4,6},{5,7},{6,4},{7,5},{8,10},{9,11},{10,... | collective-permute-start | bytes 737288 | tf_op jit(solution)/shard_map/ppermute | solution.py:286
  46.7 10.0 %collective-permute-start.2 = (bf16[16,7680]{1,0:T(8,128)(2,1)S(1)}, bf16[16,7680]{1,0:T(8,128)(2,1)S(1)}, u32[]{:S(2)}, u32[]{:S(2)}) collective-permute-start(bf16[16,7680]{1,0:T(8,128)(2,1)S(1)} %get-tuple-element.62.refs_0_), channel_id=1, source_target_pairs={{0,3},{1,0},{2,1},{3,2},{4,7},{5,4},{6,5},{7,6},{8,11},{9,8},{10,9... | collective-permute-start | bytes 737288 | tf_op jit(solution)/shard_map/ppermute | solution.py:286
  51.0 9.4 %collective-permute-start.10 = (bf16[64,1536]{1,0:T(8,128)(2,1)S(1)}, bf16[64,1536]{1,0:T(8,128)(2,1)S(1)}, u32[]{:S(2)}, u32[]{:S(2)}) collective-permute-start(bf16[64,1536]{1,0:T(8,128)(2,1)S(1)} %get-tuple-element.37.rest_4_), channel_id=1, source_target_pairs={{0,2},{1,3},{2,0},{3,1},{4,6},{5,7},{6,4},{7,5},{8,10},{9,11},{10,... | collective-permute-start | bytes 589832 | tf_op jit(solution)/shard_map/ppermute | solution.py:286
  54.1 8.7 %collective-permute-start.11 = (bf16[64,1536]{1,0:T(8,128)(2,1)S(1)}, bf16[64,1536]{1,0:T(8,128)(2,1)S(1)}, u32[]{:S(2)}, u32[]{:S(2)}) collective-permute-start(bf16[64,1536]{1,0:T(8,128)(2,1)S(1)} %get-tuple-element.37.rest_4_), channel_id=1, source_target_pairs={{0,3},{1,0},{2,1},{3,2},{4,7},{5,4},{6,5},{7,6},{8,11},{9,8},{10,9... | collective-permute-start | bytes 589832 | tf_op jit(solution)/shard_map/ppermute | solution.py:286
  55.3 28.7 %collective-permute-start.18 = (bf16[64,2048]{1,0:T(8,128)(2,1)S(1)}, bf16[64,2048]{1,0:T(8,128)(2,1)S(1)}, u32[]{:S(2)}, u32[]{:S(2)}) collective-permute-start(bf16[64,2048]{1,0:T(8,128)(2,1)S(1)} %get-tuple-element.45.rest_4_), channel_id=1, source_target_pairs={{0,1},{1,2},{2,3},{3,0},{4,5},{5,6},{6,7},{7,4},{8,9},{9,10},{10,1... | collective-permute-start | bytes 786440 | tf_op jit(solution)/shard_map/ppermute | solution.py:286
  56.1 13.0 %collective-permute-start.9 = (bf16[64,1536]{1,0:T(8,128)(2,1)S(1)}, bf16[64,1536]{1,0:T(8,128)(2,1)}, u32[]{:S(2)}, u32[]{:S(2)}) collective-permute-start(bf16[64,1536]{1,0:T(8,128)(2,1)S(1)} %get-tuple-element.37.rest_4_), channel_id=1, source_target_pairs={{0,1},{1,2},{2,3},{3,0},{4,5},{5,6},{6,7},{7,4},{8,9},{9,10},{10,1... | collective-permute-start | bytes 589832 | tf_op jit(solution)/shard_map/ppermute | solution.py:286
  57.4 11.7 %collective-permute-start.6 = (bf16[64,1536]{1,0:T(8,128)(2,1)}, bf16[64,1536]{1,0:T(8,128)(2,1)}, u32[]{:S(2)}, u32[]{:S(2)}) collective-permute-start(bf16[64,1536]{1,0:T(8,128)(2,1)} %get-tuple-element.36.rest_0_), channel_id=1, source_target_pairs={{0,4},{1,5},{2,6},{3,7},{4,8},{5,9},{6,10},{7,11},{8,12},{9,13},{1... | collective-permute-start | bytes 589832 | tf_op jit(solution)/shard_map/ppermute | solution.py:290
  60.4 8.7 %collective-permute-start.7 = (bf16[64,1536]{1,0:T(8,128)(2,1)}, bf16[64,1536]{1,0:T(8,128)(2,1)}, u32[]{:S(2)}, u32[]{:S(2)}) collective-permute-start(bf16[64,1536]{1,0:T(8,128)(2,1)} %get-tuple-element.36.rest_0_), channel_id=1, source_target_pairs={{0,8},{1,9},{2,10},{3,11},{4,12},{5,13},{6,14},{7,15},{8,0},{9,1},... | collective-permute-start | bytes 589832 | tf_op jit(solution)/shard_map/ppermute | solution.py:290
  62.8 0.7 copy-start
  63.5 6.2 %collective-permute-start.8 = (bf16[64,1536]{1,0:T(8,128)(2,1)}, bf16[64,1536]{1,0:T(8,128)(2,1)}, u32[]{:S(2)}, u32[]{:S(2)}) collective-permute-start(bf16[64,1536]{1,0:T(8,128)(2,1)} %get-tuple-element.36.rest_0_), channel_id=1, source_target_pairs={{0,12},{1,13},{2,14},{3,15},{4,0},{5,1},{6,2},{7,3},{8,4},{9,5},{1... | collective-permute-start | bytes 589832 | tf_op jit(solution)/shard_map/ppermute | solution.py:290
  69.8 0.9 copy-start.1
  73.7 1.2 collective-permute-start.12
  75.9 9.2 %collective-permute-start.13 = (bf16[8,2048]{1,0:T(8,128)(2,1)S(1)}, bf16[8,2048]{1,0:T(8,128)(2,1)S(1)}, u32[]{:S(2)}, u32[]{:S(2)}) collective-permute-start(bf16[8,2048]{1,0:T(8,128)(2,1)S(1)} %get-tuple-element.43), channel_id=1, source_target_pairs={{0,16},{16,0},{32,48},{48,32},{64,80},{80,64},{96,112},{112,96},{1... | collective-permute-start | bytes 98312 | tf_op jit(solution)/shard_map/ppermute | solution.py:279
  76.1 10.8 %collective-permute-start.19 = (bf16[64,2048]{1,0:T(8,128)(2,1)S(1)}, bf16[64,2048]{1,0:T(8,128)(2,1)S(1)}, u32[]{:S(2)}, u32[]{:S(2)}) collective-permute-start(bf16[64,2048]{1,0:T(8,128)(2,1)S(1)} %get-tuple-element.45.rest_4_), channel_id=1, source_target_pairs={{0,2},{1,3},{2,0},{3,1},{4,6},{5,7},{6,4},{7,5},{8,10},{9,11},{10,... | collective-permute-start | bytes 786440 | tf_op jit(solution)/shard_map/ppermute | solution.py:286
  79.3 13.6 %collective-permute-start.20 = (bf16[64,2048]{1,0:T(8,128)(2,1)S(1)}, bf16[64,2048]{1,0:T(8,128)(2,1)S(1)}, u32[]{:S(2)}, u32[]{:S(2)}) collective-permute-start(bf16[64,2048]{1,0:T(8,128)(2,1)S(1)} %get-tuple-element.45.rest_4_), channel_id=1, source_target_pairs={{0,3},{1,0},{2,1},{3,2},{4,7},{5,4},{6,5},{7,6},{8,11},{9,8},{10,9... | collective-permute-start | bytes 786440 | tf_op jit(solution)/shard_map/ppermute | solution.py:286
  81.1 11.7 %collective-permute-start.15 = (bf16[64,2048]{1,0:T(8,128)(2,1)S(1)}, bf16[64,2048]{1,0:T(8,128)(2,1)S(1)}, u32[]{:S(2)}, u32[]{:S(2)}) collective-permute-start(bf16[64,2048]{1,0:T(8,128)(2,1)S(1)} %get-tuple-element.44.rest_0_), channel_id=1, source_target_pairs={{0,4},{1,5},{2,6},{3,7},{4,8},{5,9},{6,10},{7,11},{8,12},{9,13},{1... | collective-permute-start | bytes 786440 | tf_op jit(solution)/shard_map/ppermute | solution.py:290
  83.9 12.7 %collective-permute-start.16 = (bf16[64,2048]{1,0:T(8,128)(2,1)S(1)}, bf16[64,2048]{1,0:T(8,128)(2,1)S(1)}, u32[]{:S(2)}, u32[]{:S(2)}) collective-permute-start(bf16[64,2048]{1,0:T(8,128)(2,1)S(1)} %get-tuple-element.44.rest_0_), channel_id=1, source_target_pairs={{0,8},{1,9},{2,10},{3,11},{4,12},{5,13},{6,14},{7,15},{8,0},{9,1},... | collective-permute-start | bytes 786440 | tf_op jit(solution)/shard_map/ppermute | solution.py:290
  85.1 11.6 %collective-permute-start.17 = (bf16[64,2048]{1,0:T(8,128)(2,1)S(1)}, bf16[64,2048]{1,0:T(8,128)(2,1)S(1)}, u32[]{:S(2)}, u32[]{:S(2)}) collective-permute-start(bf16[64,2048]{1,0:T(8,128)(2,1)S(1)} %get-tuple-element.44.rest_0_), channel_id=1, source_target_pairs={{0,12},{1,13},{2,14},{3,15},{4,0},{5,1},{6,2},{7,3},{8,4},{9,5},{1... | collective-permute-start | bytes 786440 | tf_op jit(solution)/shard_map/ppermute | solution.py:290
  86.9 9.9 %collective-permute-start.14 = (bf16[8,2048]{1,0:T(8,128)(2,1)S(1)}, bf16[8,2048]{1,0:T(8,128)(2,1)S(1)}, u32[]{:S(2)}, u32[]{:S(2)}) collective-permute-start(bf16[8,2048]{1,0:T(8,128)(2,1)S(1)} %add_convert_fusion.5.own_ref), channel_id=1, source_target_pairs={{0,32},{16,48},{32,0},{48,16},{64,96},{80,112},{96,64},{112,80},{1... | collective-permute-start | bytes 98312 | tf_op jit(solution)/shard_map/ppermute | solution.py:279
  99.1 1.3 collective-permute-start.21
  100.4 4.3 %collective-permute-start.22 = (bf16[8,4096]{1,0:T(8,128)(2,1)S(1)}, bf16[8,4096]{1,0:T(8,128)(2,1)S(1)}, u32[]{:S(2)}, u32[]{:S(2)}) collective-permute-start(bf16[8,4096]{1,0:T(8,128)(2,1)S(1)} %add_convert_fusion.3), channel_id=1, source_target_pairs={{0,32},{16,48},{32,0},{48,16},{64,96},{80,112},{96,64},{112,80},{1... | collective-permute-start | bytes 196616 | tf_op jit(solution)/shard_map/ppermute | solution.py:279
  101.0 15.2 %collective-permute-start.24 = (bf16[64,4096]{1,0:T(8,128)(2,1)S(1)}, bf16[64,4096]{1,0:T(8,128)(2,1)S(1)}, u32[]{:S(2)}, u32[]{:S(2)}) collective-permute-start(bf16[64,4096]{1,0:T(8,128)(2,1)S(1)} %get-tuple-element.48.rest_0_), channel_id=1, source_target_pairs={{0,4},{1,5},{2,6},{3,7},{4,8},{5,9},{6,10},{7,11},{8,12},{9,13},{1... | collective-permute-start | bytes 1572872 | tf_op jit(solution)/shard_map/ppermute | solution.py:290
  104.8 6.0 %collective-permute-start.23 = (bf16[8,4096]{1,0:T(8,128)(2,1)S(1)}, bf16[8,4096]{1,0:T(8,128)(2,1)S(1)}, u32[]{:S(2)}, u32[]{:S(2)}) collective-permute-start(bf16[8,4096]{1,0:T(8,128)(2,1)S(1)} %add_convert_fusion.2.own_ref), channel_id=1, source_target_pairs={{0,96},{16,112},{32,64},{48,80},{64,32},{80,48},{96,0},{112,16},{1... | collective-permute-start | bytes 196616 | tf_op jit(solution)/shard_map/ppermute | solution.py:279
  106.0 22.0 %collective-permute-start.25 = (bf16[64,4096]{1,0:T(8,128)(2,1)S(1)}, bf16[64,4096]{1,0:T(8,128)(2,1)S(1)}, u32[]{:S(2)}, u32[]{:S(2)}) collective-permute-start(bf16[64,4096]{1,0:T(8,128)(2,1)S(1)} %get-tuple-element.48.rest_0_), channel_id=1, source_target_pairs={{0,8},{1,9},{2,10},{3,11},{4,12},{5,13},{6,14},{7,15},{8,0},{9,1},... | collective-permute-start | bytes 1572872 | tf_op jit(solution)/shard_map/ppermute | solution.py:290
  109.1 22.2 %collective-permute-start.26 = (bf16[64,4096]{1,0:T(8,128)(2,1)S(1)}, bf16[64,4096]{1,0:T(8,128)(2,1)S(1)}, u32[]{:S(2)}, u32[]{:S(2)}) collective-permute-start(bf16[64,4096]{1,0:T(8,128)(2,1)S(1)} %get-tuple-element.48.rest_0_), channel_id=1, source_target_pairs={{0,12},{1,13},{2,14},{3,15},{4,0},{5,1},{6,2},{7,3},{8,4},{9,5},{1... | collective-permute-start | bytes 1572872 | tf_op jit(solution)/shard_map/ppermute | solution.py:290
  110.8 24.4 %collective-permute-start.27 = (bf16[64,4096]{1,0:T(8,128)(2,1)S(1)}, bf16[64,4096]{1,0:T(8,128)(2,1)S(1)}, u32[]{:S(2)}, u32[]{:S(2)}) collective-permute-start(bf16[64,4096]{1,0:T(8,128)(2,1)S(1)} %get-tuple-element.49.rest_4_), channel_id=1, source_target_pairs={{0,1},{1,2},{2,3},{3,0},{4,5},{5,6},{6,7},{7,4},{8,9},{9,10},{10,1... | collective-permute-start | bytes 1572872 | tf_op jit(solution)/shard_map/ppermute | solution.py:286
  110.8 24.4 %collective-permute-start.28 = (bf16[64,4096]{1,0:T(8,128)(2,1)S(1)}, bf16[64,4096]{1,0:T(8,128)(2,1)S(1)}, u32[]{:S(2)}, u32[]{:S(2)}) collective-permute-start(bf16[64,4096]{1,0:T(8,128)(2,1)S(1)} %get-tuple-element.49.rest_4_), channel_id=1, source_target_pairs={{0,2},{1,3},{2,0},{3,1},{4,6},{5,7},{6,4},{7,5},{8,10},{9,11},{10,... | collective-permute-start | bytes 1572872 | tf_op jit(solution)/shard_map/ppermute | solution.py:286
  116.2 19.6 %collective-permute-start.29 = (bf16[64,4096]{1,0:T(8,128)(2,1)S(1)}, bf16[64,4096]{1,0:T(8,128)(2,1)S(1)}, u32[]{:S(2)}, u32[]{:S(2)}) collective-permute-start(bf16[64,4096]{1,0:T(8,128)(2,1)S(1)} %get-tuple-element.49.rest_4_), channel_id=1, source_target_pairs={{0,3},{1,0},{2,1},{3,2},{4,7},{5,4},{6,5},{7,6},{8,11},{9,8},{10,9... | collective-permute-start | bytes 1572872 | tf_op jit(solution)/shard_map/ppermute | solution.py:286
  137.7 1.3 collective-permute-start.30
  138.9 4.3 %collective-permute-start.31 = (bf16[8,4096]{1,0:T(8,128)(2,1)S(1)}, bf16[8,4096]{1,0:T(8,128)(2,1)S(1)}, u32[]{:S(2)}, u32[]{:S(2)}) collective-permute-start(bf16[8,4096]{1,0:T(8,128)(2,1)S(1)} %add_convert_fusion.1), channel_id=1, source_target_pairs={{0,32},{16,48},{32,0},{48,16},{64,96},{80,112},{96,64},{112,80},{1... | collective-permute-start | bytes 196616 | tf_op jit(solution)/shard_map/ppermute | solution.py:279
  143.3 5.6 %collective-permute-start.32 = (bf16[8,4096]{1,0:T(8,128)(2,1)S(1)}, bf16[8,4096]{1,0:T(8,128)(2,1)S(1)}, u32[]{:S(2)}, u32[]{:S(2)}) collective-permute-start(bf16[8,4096]{1,0:T(8,128)(2,1)S(1)} %add_convert_fusion.own_ref), channel_id=1, source_target_pairs={{0,96},{16,112},{32,64},{48,80},{64,32},{80,48},{96,0},{112,16},{1... | collective-permute-start | bytes 196616 | tf_op jit(solution)/shard_map/ppermute | solution.py:279
  150.1 1.2 collective-permute-start.33
  151.4 4.0 %collective-permute-start.34 = (bf16[8,2048]{1,0:T(8,128)(2,1)S(1)}, bf16[8,2048]{1,0:T(8,128)(2,1)S(1)}, u32[]{:S(2)}, u32[]{:S(2)}) collective-permute-start(bf16[8,2048]{1,0:T(8,128)(2,1)S(1)} %add_convert_fusion.4.own_ref), channel_id=1, source_target_pairs={{0,32},{16,48},{32,0},{48,16},{64,96},{80,112},{96,64},{112,80},{1... | collective-permute-start | bytes 98312 | tf_op jit(solution)/shard_map/ppermute | solution.py:279
  155.9 1.2 collective-permute-start.35
